TPU v7x, 32 devices: a whole 2x2x4 slice. The times are simulated.
32 devices in a mesh: fsdp: 8 (over z, y), rep: 4 (over x, core).
Axes of the slice: x: 2, y: 2, z: 4, core: 2. Of those that a mesh axis runs over, the one named last changes fastest.
Arguments:
- block_input: bfloat16 [2, 4096, 768], P(None, ('fsdp', 'rep')), may hold values from -6 to 6
- segment_ids: int32 [2, 4096], P(None, ('fsdp', 'rep')), may hold values from -1 to 1, as said below
- out_cotangent: bfloat16 [2, 4096, 768], P(None, ('fsdp', 'rep')), may hold values from -6 to 6
- first_gain: bfloat16 [768], P('fsdp'), may hold values from 0.099609375 to 1.8984375
- first_shift: bfloat16 [768], P('fsdp'), may hold values from -3 to 3
- second_gain: bfloat16 [768], P('fsdp'), may hold values from 0.099609375 to 1.8984375
- second_shift: bfloat16 [768], P('fsdp'), may hold values from -3 to 3
- qkv_weight: bfloat16 [768, 2304], P('fsdp'), may hold values from -2 to 2
- qkv_bias: bfloat16 [2304], P('fsdp'), may hold values from -3 to 3
- proj_weight: bfloat16 [768, 768], P('fsdp'), may hold values from -0.625 to 0.625
- proj_bias: bfloat16 [768], P('fsdp'), may hold values from -3 to 3
- up_weight: bfloat16 [768, 3072], P('fsdp'), may hold values from -0.21875 to 0.21875
- up_bias: bfloat16 [3072], P('fsdp'), may hold values from -3 to 3
- down_weight: bfloat16 [3072, 768], P('fsdp'), may hold values from -0.109375 to 0.109375
- down_bias: bfloat16 [768], P('fsdp'), may hold values from -3 to 3
Outputs:
- block_output: bfloat16 [2, 4096, 768], P(None, ('fsdp', 'rep'))
- input_grad: bfloat16 [2, 4096, 768], P(None, ('fsdp', 'rep'))
- first_gain_grad: float32 [768], P('fsdp')
- first_shift_grad: float32 [768], P('fsdp')
- second_gain_grad: float32 [768], P('fsdp')
- second_shift_grad: float32 [768], P('fsdp')
- qkv_weight_grad: float32 [768, 2304], P('fsdp')
- qkv_bias_grad: float32 [2304], P('fsdp')
- proj_weight_grad: float32 [768, 768], P('fsdp')
- proj_bias_grad: float32 [768], P('fsdp')
- up_weight_grad: float32 [768, 3072], P('fsdp')
- up_bias_grad: float32 [3072], P('fsdp')
- down_weight_grad: float32 [3072, 768], P('fsdp')
- down_bias_grad: float32 [768], P('fsdp')
Inputs may be any that keep to these rules, and one draw needn't show every extreme that they name: `segment_ids`: in each aligned block of 128 slots (one device's slots of a micro-batch) the live slots come first, numbered 0 and then possibly 1, followed by empty slots marked -1; a block holds 32 or more live slots, and in every micro-batch some block is full.
All inputs are finite; a program needn't handle non-finite values.
Results may differ from a plain program's by a relative error of at most 0.0092.
Values may be sent and summed in bfloat16 or wider, within the bound.
No kernel may reach another device: no remote copies, remote signals or barrier semaphores. Data moves between devices by JAX's collectives and lax.ppermute only.
A program may use at most 192 MiB of HBM per device.

v0:
```python
import functools

import jax
import jax.numpy as jnp
import numpy as np
from jax import lax
from jax.experimental import pallas as pl
from jax.experimental.pallas import tpu as pltpu
from jax.sharding import PartitionSpec as P


D = 768
HEADS = 12
HDIM = 64
ROT = 16
FF = 3072
GROUP = 4
QUART = D // GROUP
LOCAL_HEADS = HEADS // GROUP
VEC_LANES = 128

EPSILON = 1e-05
NEG_FILL = -1e30
BF16 = jnp.bfloat16
F32 = jnp.float32


def dot(left, right):
    return jnp.dot(left, right, preferred_element_type=F32)


def dot_t(left, right):
    return lax.dot_general(left, right, (((1,), (1,)), ((), ())), preferred_element_type=F32)


def t_dot(left, right):
    return lax.dot_general(left, right, (((0,), (0,)), ((), ())), preferred_element_type=F32)


LANES = 128
EXT = LOCAL_HEADS * LANES


def layer_norm(values, gain_a, shift_a):
    centered = values - jnp.mean(values, axis=-1, keepdims=True)
    variance = jnp.mean(centered * centered, axis=-1, keepdims=True)
    inverse = lax.rsqrt(variance + EPSILON)
    unit = centered * inverse
    return (unit * gain_a + shift_a).astype(BF16), unit


def take(step, refs, rows):
    value = refs[-1][rows]
    for place in range(len(refs) - 2, -1, -1):
        value = jnp.where(step == place, refs[place][rows], value)
    return value


def mlp_kernel(
    near, across, beside, far, up_lo, up_hi, down_lo, down_hi, to_rel, rep,
    keep, send, out_part, grad_norm, vectors_out, sums,
    up_rel, down_rel, down_acc, up_acc,
):
    step = pl.program_id(0)
    packs = (near, across, beside, far)
    own = (near.shape[0] - 16) // 2
    half = D // 2

    @pl.when(step == 0)
    def _():
        up_rel[:half] = dot(up_lo[:, :D], to_rel[...]).astype(BF16)
        up_rel[half:] = dot(up_hi[:, :D], to_rel[...]).astype(BF16)
        down_rel[:half] = down_lo[...]
        down_rel[half:] = down_hi[...]
        vectors_out[:, :half] = up_lo[:, D:].astype(F32).T[:16]
        vectors_out[:, half:] = up_hi[:, D:].astype(F32).T[:16]
        down_acc[...] = jnp.zeros_like(down_acc)
        up_acc[...] = jnp.zeros_like(up_acc)
        sums[...] = jnp.zeros_like(sums)

    inputs = take(step, packs, slice(0, own))
    grad_out = take(step, packs, slice(own, 2 * own))
    normed, unit = layer_norm(dot(inputs, to_rel[...]), vectors_out[2:3], vectors_out[3:4])
    bias = vectors_out[11:12]
    for quarter in range(GROUP - 1):
        bias = jnp.where(rep[0] == quarter, vectors_out[8 + quarter : 9 + quarter], bias)
    pre_act = dot(normed, up_rel[...]) + bias
    phi = 0.5 * (1.0 + lax.erf(pre_act * 0.7071067811865476))
    activ = (pre_act * phi).astype(BF16)
    slope = phi + pre_act * jnp.exp(-0.5 * pre_act * pre_act) * 0.3989422804014327
    down_acc[...] += t_dot(activ, grad_out)
    grad_pre = dot_t(grad_out, down_rel[...]) * slope
    grad_pre_b = grad_pre.astype(BF16)
    grad_nat = dot_t(grad_pre_b, to_rel[...]).astype(BF16)
    up_acc[...] += t_dot(normed, grad_nat)
    gn = dot_t(grad_pre_b, up_rel[...])
    out_part[0] = dot(activ, down_rel[...])
    grad_norm[0] = gn
    sums[0:1] += jnp.sum(gn * unit, axis=0, keepdims=True)
    sums[1:2] += jnp.sum(gn, axis=0, keepdims=True)
    sums[2:3] += jnp.sum(grad_pre, axis=0, keepdims=True)

    @pl.when(step == pl.num_programs(0) - 1)
    def _():
        keep[:, :D] = down_acc[:half].astype(BF16)
        send[:, :D] = down_acc[half:].astype(BF16)
        keep[:, D:] = up_acc[:half].astype(BF16)
        send[:, D:] = up_acc[half:].astype(BF16)


def attention_kernel(
    block_rows,
    near, across, beside, far, qkv_lo, qkv_hi, proj, to_rel, vectors, mlp_sums, place, spread, head_spread,
    cosines, sines, mlp_part, mlp_norm, rep,
    keep, send, partial_near, partial_far,
    wide, proj_wide, bias_wide, qkv_acc, proj_acc, gp_ref, ctx_ref, sums, bias_sums,
):
    step = pl.program_id(0)
    packs = (near, across, beside, far)
    half = D // 2
    own = (near.shape[0] - 16) // 2
    count = 2 * own

    @pl.when(step == 0)
    def _():
        wide[:half] = dot(qkv_lo[...], spread[...]).astype(BF16)
        wide[half:] = dot(qkv_hi[...], spread[...]).astype(BF16)
        proj_wide[...] = dot(head_spread[...], proj[...]).astype(BF16)
        vectors_b = vectors[...].astype(BF16)
        bias = sum(dot_t(vectors_b[4 + k : 5 + k], place[:, k * D : (k + 1) * D]) for k in range(3))
        bias = jnp.broadcast_to(bias, (8, bias.shape[1])).astype(BF16)
        bias_wide[...] = dot(bias, spread[...])
        qkv_acc[...] = jnp.zeros_like(qkv_acc)
        proj_acc[...] = jnp.zeros_like(proj_acc)
        sums[...] = jnp.zeros_like(sums)
        bias_sums[...] = jnp.zeros_like(bias_sums)

    inputs = take(step, packs, slice(0, own))
    grad_out = take(step, packs, slice(own, count))
    segment_row = take(step, packs, slice(count, count + 16)).astype(F32)
    normed, unit = layer_norm(dot(inputs, to_rel[...]), vectors[0:1], vectors[1:2])
    projected = dot(normed, wide[...]) + bias_wide[0:1]
    grad_context = dot_t(grad_out, proj_wide[...]).astype(BF16)
    lane = lax.broadcasted_iota(jnp.int32, (LANES, LANES), 1)
    sublane = lax.broadcasted_iota(jnp.int32, (LANES, LANES), 0)
    lower = lane < HDIM
    zero = jnp.zeros((LANES, LANES), F32)
    for slab in range(own // LANES):
        row = slice(slab * LANES, (slab + 1) * LANES)
        seg_keys = jnp.broadcast_to(segment_row[0:1, row], (LANES, LANES))
        seg_queries = seg_keys.T
        same = seg_keys == seg_queries
        allowed = same & (lane <= sublane)
        position = jnp.sum(jnp.where(same & (lane < sublane), 1.0, 0.0), axis=1, keepdims=True)
        pick = (lane.astype(F32) == position).astype(BF16)
        cos = dot(pick, cosines[0]) + dot(pick, cosines[1]) + dot(pick, cosines[2])
        sin = dot(pick, sines[0]) + dot(pick, sines[1]) + dot(pick, sines[2])

        def turn(value, direction):
            return value * cos + direction * (pltpu.roll(value, HDIM, 1) * sin)

        for head in range(LOCAL_HEADS):
            def part(which):
                start = which * EXT + head * LANES
                return slice(start, start + LANES)

            query = (turn(projected[row, part(0)], 1.0) * 0.125).astype(BF16)
            key = turn(projected[row, part(1)], 1.0).astype(BF16)
            value = projected[row, part(2)].astype(BF16)
            gctx = grad_context[row, part(0)]
            query_half = jnp.where(lower, query, jnp.zeros_like(query))
            scores = jnp.where(allowed, dot_t(query_half, key), NEG_FILL)
            highest = jnp.max(scores, axis=-1, keepdims=True)
            weight = jnp.exp(scores - highest)
            probs = weight / jnp.sum(weight, axis=-1, keepdims=True)
            probs_b = probs.astype(BF16)
            ctx_ref[row, part(0)] = dot(probs_b, value).astype(BF16)
            grad_probs = dot_t(gctx, value)
            grad_value = t_dot(probs_b, gctx)
            delta = jnp.sum(probs * grad_probs, axis=-1, keepdims=True)
            grad_sc = (probs * (grad_probs - delta)).astype(BF16)
            grad_query = jnp.where(lower, turn(dot(grad_sc, key) * 0.125, -1.0), zero)
            grad_key = jnp.where(lower, turn(t_dot(grad_sc, query), -1.0), zero)
            for which, grad in enumerate((grad_query, grad_key, grad_value)):
                gp_ref[row, part(which)] = grad.astype(BF16)
                bias_sums[0:1, part(which)] += jnp.sum(grad, axis=0, keepdims=True)

    grad_wide = gp_ref[...]
    qkv_acc[...] += t_dot(normed, dot_t(grad_wide, spread[...]).astype(BF16))
    gn = dot_t(grad_wide, wide[...])
    context = ctx_ref[...]
    proj_acc[...] += t_dot(dot(context, head_spread[...]).astype(BF16), grad_out)
    out_part = (dot(context, proj_wide[...]) + mlp_part[0]).astype(BF16)
    mixed = (gn * vectors[0:1] + mlp_norm[0] * vectors[2:3]).astype(BF16)
    sums[0:1] += jnp.sum(gn * unit, axis=0, keepdims=True)
    sums[1:2] += jnp.sum(gn, axis=0, keepdims=True)

    @pl.when(step < 2)
    def _():
        partial_near[0, :, :D] = out_part
        partial_near[0, :, D:] = mixed

    @pl.when(step >= 2)
    def _():
        partial_far[0, :, :D] = out_part
        partial_far[0, :, D:] = mixed

    @pl.when(step == 0)
    def _():
        sums[2:3] = jnp.sum(grad_out.astype(F32), axis=0, keepdims=True)

    @pl.when(step == pl.num_programs(0) - 1)
    def _():
        width = 3 * QUART
        side = width + VEC_LANES
        vec = lax.broadcasted_iota(jnp.int32, (VEC_LANES, D), 0)
        out_bias = dot(sums[...].astype(BF16), to_rel[...])[2:3]
        small = dot_t(bias_sums[...].astype(BF16), spread[...]).astype(BF16)
        small = dot(small, place[...])
        rows = [sums[0:1], sums[1:2], mlp_sums[0:1], mlp_sums[1:2]]
        rows += [small[0:1, k * D : (k + 1) * D] for k in range(3)] + [out_bias]
        table = jnp.where(vec == 8 + rep[0], mlp_sums[2:3], 0.0)
        for index, line in enumerate(rows):
            table = jnp.where(vec == index, line, table)
        table = table.T.astype(BF16)
        keep[:, :width] = qkv_acc[:half].astype(BF16)
        send[:, :width] = qkv_acc[half:].astype(BF16)
        keep[:, width:side] = table[:half]
        send[:, width:side] = table[half:]
        for target, first in ((keep, 0), (send, QUART // 2)):
            piece = proj_acc[first : first + QUART // 2]
            block = min(block_rows, QUART // 2)
            for start in range(0, QUART // 2, block):
                for quarter in range(GROUP):
                    target[
                        start * GROUP + quarter * block : start * GROUP + (quarter + 1) * block, side:
                    ] = piece[start : start + block, quarter * QUART : (quarter + 1) * QUART].astype(BF16)


def whole(*shape):
    return pl.BlockSpec(shape, lambda i: (0,) * len(shape))


def token_block(count, width):
    return pl.BlockSpec((1, count, width), lambda i: (i, 0, 0))


PARAMS = pltpu.CompilerParams(vmem_limit_bytes=60 * 1024 * 1024)


def smem():
    return pl.BlockSpec(memory_space=pltpu.SMEM)


def run_mlp(packs, up_lo, up_hi, down_lo, down_hi, to_rel, rep):
    packed = packs[0].shape[0]
    own = (packed - 16) // 2
    half = D // 2
    wide = D + VEC_LANES
    grad = jax.ShapeDtypeStruct((half, 2 * D), BF16)
    acts = jax.ShapeDtypeStruct((GROUP, own, D), F32)
    return pl.pallas_call(
        mlp_kernel,
        grid=(GROUP,),
        in_specs=[whole(packed, D)] * 4
        + [whole(half, wide), whole(half, wide), whole(half, D), whole(half, D), whole(D, D), smem()],
        out_specs=[whole(half, 2 * D)] * 2 + [token_block(own, D)] * 2 + [whole(16, D), whole(8, D)],
        out_shape=[grad] * 2 + [acts] * 2 + [jax.ShapeDtypeStruct((16, D), F32), jax.ShapeDtypeStruct((8, D), F32)],
        scratch_shapes=[
            pltpu.VMEM((D, D), BF16),
            pltpu.VMEM((D, D), BF16),
            pltpu.VMEM((D, D), F32),
            pltpu.VMEM((D, D), F32),
        ],
        compiler_params=PARAMS,
        name="mlp",
    )(*packs, up_lo, up_hi, down_lo, down_hi, to_rel, rep)


def run_attention(packs, qkv_lo, qkv_hi, proj, to_rel, vectors, mlp_sums, place, head_spread, mlp_part, mlp_norm, rep, rows):
    packed = packs[0].shape[0]
    own = (packed - 16) // 2
    half = D // 2
    width = 3 * QUART
    column = np.arange(3 * EXT)
    which, head, unit = column // EXT, column % EXT // LANES, column % LANES
    inner = unit % HDIM
    halfway = ROT // 2
    partner = np.where(inner < halfway, inner + halfway, np.where(inner < ROT, inner - halfway, inner))
    source = which * QUART + head * HDIM + np.where(unit < HDIM, inner, partner)
    source = np.where((which == 2) & (unit >= HDIM), -1, source)
    spread = (jnp.arange(width)[:, None] == jnp.asarray(source, jnp.int32)[None, :]).astype(BF16)
    lane = np.arange(LANES) % HDIM
    angle = np.arange(LANES)[:, None] * (10000.0 ** (-(lane % halfway) / halfway))[None, :]
    sign = np.where(lane < halfway, -1.0, 1.0) * np.where(np.arange(LANES) < HDIM, 1.0, -1.0)
    turning = (lane < ROT)[None, :]
    tables = []
    for table in (np.where(turning, np.cos(angle), 1.0), np.where(turning, np.sin(angle) * sign, 0.0)):
        left = table.astype(np.float32)
        pieces = []
        for _ in range(3):
            piece = left.astype(BF16)
            pieces.append(piece)
            left = left - piece.astype(np.float32)
        tables.append(jnp.asarray(np.stack(pieces)))
    total = width + VEC_LANES + QUART
    grad = jax.ShapeDtypeStruct((half, total), BF16)
    part = jax.ShapeDtypeStruct((2, own, 2 * D), BF16)
    return pl.pallas_call(
        functools.partial(attention_kernel, rows),
        grid=(GROUP,),
        in_specs=[whole(packed, D)] * 4
        + [
            whole(half, width),
            whole(half, width),
            whole(QUART, D),
            whole(D, D),
            whole(16, D),
            whole(8, D),
            whole(width, 3 * D),
            whole(width, 3 * EXT),
            whole(EXT, QUART),
            whole(3, LANES, LANES),
            whole(3, LANES, LANES),
            token_block(own, D),
            token_block(own, D),
            smem(),
        ],
        out_specs=[
            whole(half, total),
            whole(half, total),
            pl.BlockSpec((1, own, 2 * D), lambda i: (jnp.minimum(i, 1), 0, 0)),
            pl.BlockSpec((1, own, 2 * D), lambda i: (jnp.maximum(i - 2, 0), 0, 0)),
        ],
        out_shape=[grad, grad, part, part],
        scratch_shapes=[
            pltpu.VMEM((D, 3 * EXT), BF16),
            pltpu.VMEM((EXT, D), BF16),
            pltpu.VMEM((8, 3 * EXT), F32),
            pltpu.VMEM((D, width), F32),
            pltpu.VMEM((QUART, D), F32),
            pltpu.VMEM((own, 3 * EXT), BF16),
            pltpu.VMEM((own, EXT), BF16),
            pltpu.VMEM((8, D), F32),
            pltpu.VMEM((8, 3 * EXT), F32),
        ],
        compiler_params=PARAMS,
        name="attention",
    )(
        *packs, qkv_lo, qkv_hi, proj, to_rel, vectors, mlp_sums, place, spread, head_spread, *tables, mlp_part, mlp_norm, rep
    )


def finish_kernel(pack, near, received, to_rel, out_bias, live, block_out, input_grad):
    own = near.shape[0]
    partial = near[...].astype(F32) + received[...].astype(F32)
    block_out[...] = (live[...] * (pack[:own].astype(F32) + partial[:, :D] + out_bias[...])).astype(BF16)
    values = dot(pack[:own], to_rel[...])
    centered = values - jnp.mean(values, axis=-1, keepdims=True)
    inverse = lax.rsqrt(jnp.mean(centered * centered, axis=-1, keepdims=True) + EPSILON)
    unit = centered * inverse
    error = partial[:, D:]
    through = inverse * (
        error
        - jnp.mean(error, axis=-1, keepdims=True)
        - unit * jnp.mean(error * unit, axis=-1, keepdims=True)
    )
    grad = (dot(pack[own : 2 * own], to_rel[...]) + through).astype(BF16)
    input_grad[...] = dot_t(grad, to_rel[...]).astype(BF16)


def run_finish(pack, near, received, to_rel, out_bias, live):
    own = near.shape[0]
    out = jax.ShapeDtypeStruct((own, D), BF16)
    return pl.pallas_call(finish_kernel, out_shape=[out, out], compiler_params=PARAMS, name="finish")(
        pack, near, received, to_rel, out_bias, live
    )


def assemble_kernel(*refs):
    pairs, columns = refs[:4], refs[4:8]
    place = refs[8]
    qkv_out, proj_out, up_out, down_out, vec_out = refs[9:]
    rows = proj_out.shape[0]
    width = 3 * QUART
    side = width + VEC_LANES
    rep, top = place[0], place[1]

    def owner(values, natural):
        first, second, third, fourth = values
        chosen = jnp.where(rep == natural ^ 1, third, fourth)
        chosen = jnp.where(rep == natural ^ 2, second, chosen)
        return jnp.where(rep == natural, first, chosen)

    for natural in range(GROUP):
        down_out[natural * rows : (natural + 1) * rows] = owner([ref[:, :D].astype(F32) for ref in pairs], natural)
        up = owner([ref[:, D:].astype(F32) for ref in pairs], natural)
        for shard in range(D // rows):
            start = (shard * GROUP + natural) * rows
            up_out[:, start : start + rows] = up[:, shard * rows : (shard + 1) * rows]
        qkv = owner([ref[:, :width].astype(F32) for ref in columns], natural)
        for which in range(3):
            start = (which * GROUP + natural) * QUART
            qkv_out[:, start : start + QUART] = qkv[:, which * QUART : (which + 1) * QUART]
    parts = [ref[:, side:].astype(F32) for ref in columns]
    chosen = jnp.where((rep ^ top) == 1, parts[2], parts[3])
    chosen = jnp.where((rep ^ top) == 2, parts[1], chosen)
    proj_out[...] = jnp.where((rep ^ top) == 0, parts[0], chosen)
    vec = [ref[:, width:side].astype(F32) for ref in columns]
    vec_out[...] = ((vec[0] + vec[1]) + (vec[2] + vec[3])).T[:16]


def run_assemble(pairs, columns, place, rows):
    shapes = [(rows, 3 * D), (rows, D), (rows, FF), (GROUP * rows, D), (16, rows)]
    return pl.pallas_call(
        assemble_kernel,
        in_specs=[pl.BlockSpec(memory_space=pltpu.VMEM)] * 8 + [smem()],
        out_shape=[jax.ShapeDtypeStruct(shape, F32) for shape in shapes],
        compiler_params=PARAMS,
        name="assemble",
    )(*pairs, *columns, place)


def assemble_plain(pairs, columns, place, rows):
    width = 3 * QUART
    side = width + VEC_LANES
    rep, top = place[0], place[1]
    pairs = jnp.stack(pairs).astype(F32)
    columns = jnp.stack(columns).astype(F32)
    natural = jnp.arange(GROUP)
    swapped = natural ^ rep
    order = (swapped % 2) * 2 + swapped // 2
    pairs_nat, columns_nat = pairs[order], columns[order]
    qkv = columns_nat[:, :, :width].reshape(GROUP, rows, 3, QUART).transpose(1, 2, 0, 3)
    up = pairs_nat[:, :, D:].reshape(GROUP, rows, D // rows, rows).transpose(1, 2, 0, 3)
    vec = columns[:, :, width:side]
    vec = ((vec[0] + vec[1]) + (vec[2] + vec[3])).T[:16]
    return (
        qkv.reshape(rows, 3 * D),
        columns_nat[top][:, side:],
        up.reshape(rows, FF),
        pairs_nat[:, :, :D].reshape(GROUP * rows, D),
        vec,
    )


def quarter_kernel(up, qkv, vectors, rep, up_own, qkv_own):
    rows = up.shape[0]
    for natural in range(GROUP):

        @pl.when(rep[0] == natural)
        def _():
            for shard in range(D // rows):
                start = (shard * GROUP + natural) * rows
                up_own[:, shard * rows : (shard + 1) * rows] = up[:, start : start + rows]
            for which in range(3):
                start = (which * GROUP + natural) * QUART
                qkv_own[:, which * QUART : (which + 1) * QUART] = qkv[:, start : start + QUART]

    up_own[:, D:] = jnp.pad(vectors[...], ((0, VEC_LANES - 16), (0, 0))).T.astype(BF16)


def run_quarter(up, qkv, vectors, rep):
    rows = up.shape[0]
    return pl.pallas_call(
        quarter_kernel,
        in_specs=[pl.BlockSpec(memory_space=pltpu.VMEM)] * 3 + [smem()],
        out_shape=[
            jax.ShapeDtypeStruct((rows, D + VEC_LANES), BF16),
            jax.ShapeDtypeStruct((rows, 3 * QUART), BF16),
        ],
        compiler_params=PARAMS,
        name="quarter",
    )(up, qkv, vectors, rep)


def make_body(shards):
    bits = shards.bit_length() - 1
    rows = D // shards
    lowest_first = [1 << k for k in range(bits)]
    highest_first = lowest_first[::-1]

    def reverse(value, width):
        return sum(((value >> k) & 1) << (width - 1 - k) for k in range(width))

    def shard_swap(value, mask):
        return lax.ppermute(value, "fsdp", [(i, i ^ mask) for i in range(shards)])

    def core_swap(value):
        return lax.ppermute(value, "rep", [(i, i ^ 1) for i in range(GROUP)])

    def x_swap(value):
        return lax.ppermute(value, "rep", [(i, i ^ 2) for i in range(GROUP)])

    def gather_all(own):
        for mask in highest_first[:-1]:
            own = jnp.concatenate([own, shard_swap(own, mask)], axis=0)
        return own, shard_swap(own, highest_first[-1])

    def add(keep, received):
        return keep.astype(F32) + received.astype(F32)

    def reduce_all(keep, send):
        for mask in lowest_first:
            total = add(keep, shard_swap(send, mask)).astype(BF16)
            half = total.shape[0] // 2
            keep, send = total[:half], total[half:]
        return total

    def one_hot(count, width, mine):
        place = jnp.array([reverse(p, width) for p in range(count)], jnp.int32)
        natural = ((place ^ mine)[:, None] * rows + jnp.arange(rows)[None, :]).reshape(1, count * rows)
        return (jnp.arange(count * rows)[:, None] == natural).astype(BF16)

    def body(
        block_input,
        segment_ids,
        out_cotangent,
        first_gain,
        first_shift,
        second_gain,
        second_shift,
        qkv_weight,
        qkv_bias,
        proj_weight,
        proj_bias,
        up_weight,
        up_bias,
        down_weight,
        down_bias,
    ):
        micro, slot = block_input.shape[0], block_input.shape[1]
        own_tokens = micro * slot
        mine = lax.axis_index("fsdp")
        rep = lax.axis_index("rep")
        core = rep % 2
        across = rep // 2
        top = mine // (shards // 4)
        top_across, top_core = top // 2, top % 2

        rep_ref = rep.reshape(1)
        vector_own = jnp.concatenate(
            [first_gain, first_shift, second_gain, second_shift, qkv_bias, proj_bias, up_bias, down_bias]
        )
        vector_own = jnp.pad(vector_own.reshape(13, rows), ((0, 3), (0, 0)))
        if rows % 32:
            up_own = lax.dynamic_index_in_dim(
                up_weight.reshape(rows, shards, GROUP, rows), rep, axis=2, keepdims=False
            ).reshape(rows, D)
            up_own = jnp.concatenate([up_own, jnp.pad(vector_own, ((0, VEC_LANES - 16), (0, 0))).T], axis=1)
            qkv_own = lax.dynamic_index_in_dim(
                qkv_weight.reshape(rows, 3, GROUP, QUART), rep, axis=2, keepdims=False
            ).reshape(rows, 3 * QUART)
        else:
            up_own, qkv_own = run_quarter(up_weight, qkv_weight, vector_own.astype(F32), rep_ref)
        down_own = lax.dynamic_index_in_dim(
            down_weight.reshape(GROUP, rows, D), rep, axis=0, keepdims=False
        )

        live = (segment_ids.reshape(own_tokens, 1) >= 0).astype(F32)
        own_input = block_input.reshape(own_tokens, D)
        own_grad = (out_cotangent.reshape(own_tokens, D).astype(F32) * live).astype(BF16)
        segment_row = jnp.pad(
            segment_ids.reshape(1, own_tokens).astype(BF16), ((0, 15), (0, D - own_tokens))
        )
        token_pack = jnp.concatenate([own_input, own_grad, segment_row], axis=0)
        token_across = x_swap(token_pack)
        token_beside = core_swap(token_pack)
        token_far = core_swap(token_across)
        packs = (token_pack, token_across, token_beside, token_far)

        up_lo, up_hi = gather_all(up_own)
        down_lo, down_hi = gather_all(down_own)
        qkv_lo, qkv_hi = gather_all(qkv_own)

        proj_part = jnp.where(top_across == across, proj_weight, shard_swap(proj_weight, highest_first[0]))
        proj_part = jnp.where(top_core == core, proj_part, shard_swap(proj_part, highest_first[1]))
        for mask in highest_first[2:]:
            proj_part = jnp.concatenate([proj_part, shard_swap(proj_part, mask)], axis=0)

        to_rel = one_hot(shards, bits, mine)
        head_to_rel = one_hot(shards // 4, bits - 2, mine % (shards // 4))
        head_spread = jnp.pad(
            head_to_rel.reshape(LOCAL_HEADS, HDIM, QUART), ((0, 0), (0, LANES - HDIM), (0, 0))
        ).reshape(EXT, QUART)

        width = 3 * QUART
        place = jnp.array([reverse(p, bits) for p in range(shards)], jnp.int32)
        shard_start = (place ^ mine)[None, :, None] * (3 * rows)
        found = shard_start + jnp.arange(3)[:, None, None] * rows + jnp.arange(rows)[None, None, :]
        found = found.reshape(1, 3 * D)
        found = jnp.where(found % D // QUART == rep, found // D * QUART + found % QUART, -1)
        bias_place = (jnp.arange(width)[:, None] == found).astype(BF16)

        keep, send, mlp_part, mlp_norm, vectors, mlp_sums = run_mlp(
            packs, up_lo, up_hi, down_lo, down_hi, to_rel, rep_ref
        )
        pair = reduce_all(keep, send)
        keep, send, partial, partial_far = run_attention(
            packs, qkv_lo, qkv_hi, proj_part, to_rel, vectors, mlp_sums, bias_place, head_spread,
            mlp_part, mlp_norm, rep_ref, rows,
        )

        side = width + VEC_LANES
        for mask in lowest_first[:-2]:
            total = add(keep, shard_swap(send, mask)).astype(BF16)
            half = total.shape[0] // 2
            keep, send = total[:half], total[half:]
        columns, proj_block = total[:, :side], total[:, side:]
        proj_block = jnp.concatenate([proj_block[: 2 * rows], proj_block[2 * rows :]], axis=1)
        packed = jnp.concatenate([columns[2 * rows :], proj_block], axis=1)
        sent = shard_swap(packed, lowest_first[-2])
        columns = add(columns[: 2 * rows], sent[:, :side])
        proj_block = add(proj_block, sent[:, side:])
        proj_block = jnp.concatenate(
            [
                proj_block[:rows, :QUART],
                proj_block[rows:, :QUART],
                proj_block[:rows, QUART:],
                proj_block[rows:, QUART:],
            ],
            axis=1,
        ).astype(BF16)
        packed = jnp.concatenate([columns[rows:].astype(BF16), proj_block], axis=1)
        own = jnp.concatenate([columns[:rows].astype(BF16), proj_block], axis=1)
        column = add(own, shard_swap(packed, lowest_first[-1])).astype(BF16)

        summed = add(partial, core_swap(partial_far))
        received = x_swap(summed[1].astype(BF16))
        vectors_nat = dot_t(vectors.astype(BF16), to_rel)
        out_bias = (vectors_nat[7] + vectors_nat[12])[None]
        block_out, input_grad = run_finish(token_pack, summed[0], received, to_rel, out_bias, live)

        pair_across = x_swap(pair)
        pair_all = (pair, pair_across, core_swap(pair), core_swap(pair_across))
        column_across = x_swap(column)
        column_all = (column, column_across, core_swap(column), core_swap(column_across))
        assemble = assemble_plain if rows % 32 else run_assemble
        qkv_out, proj_out, up_out, down_out, vec_out = assemble(
            pair_all, column_all, jnp.stack([rep, top]), rows
        )
        return (
            block_out.reshape(micro, slot, D),
            input_grad.reshape(micro, slot, D),
            vec_out[0],
            vec_out[1],
            vec_out[2],
            vec_out[3],
            qkv_out,
            vec_out[4:7].reshape(3 * rows),
            proj_out,
            vec_out[7],
            up_out,
            vec_out[8:12].reshape(GROUP * rows),
            down_out,
            vec_out[7],
        )

    return body


def solution(mesh):
    in_specs = (
        P(None, ("fsdp", "rep"), None),
        P(None, ("fsdp", "rep")),
        P(None, ("fsdp", "rep"), None),
        P("fsdp"),
        P("fsdp"),
        P("fsdp"),
        P("fsdp"),
        P("fsdp", None),
        P("fsdp"),
        P("fsdp", None),
        P("fsdp"),
        P("fsdp", None),
        P("fsdp"),
        P("fsdp", None),
        P("fsdp"),
    )
    out_specs = (
        P(None, ("fsdp", "rep"), None),
        P(None, ("fsdp", "rep"), None),
        P("fsdp"),
        P("fsdp"),
        P("fsdp"),
        P("fsdp"),
        P("fsdp", None),
        P("fsdp"),
        P("fsdp", None),
        P("fsdp"),
        P("fsdp", None),
        P("fsdp"),
        P("fsdp", None),
        P("fsdp"),
    )
    plain = make_body(mesh.shape["fsdp"])

    return jax.shard_map(plain, mesh=mesh, in_specs=in_specs, out_specs=out_specs, check_vma=False)
```

profile of v0, /device:TPU:0, one launch (start us, length us, event | category | flops | bytes accessed | tf_op | source)
XLA Modules:
  0.0 246.6 jit_solution(4171701034568583617)
XLA Ops:
  4.4 3.0 %collective-permute-start = (bf16[528,768]{1,0:T(8,128)(2,1)S(1)}, bf16[528,768]{1,0:T(8,128)(2,1)S(1)}, u32[]{:S(2)}, u32[]{:S(2)}) collective-permute-start(bf16[528,768]{1,0:T(8,128)(2,1)S(1)} %fusion.6.near.pack), channel_id=1, source_target_pairs={{0,2},{1,3},{2,0},{3,1},{4,6},{5,7},{6,4},{7,5},{8,10},{9,11},{10,... | collective-permute-start | bytes 2433032 | tf_op jit(solution)/shard_map/ppermute | solution.py:493
  7.4 2.7 %collective-permute-start.12 = (bf16[96,768]{1,0:T(8,128)(2,1)S(1)}, bf16[96,768]{1,0:T(8,128)(2,1)}, u32[]{:S(2)}, u32[]{:S(2)}) collective-permute-start(bf16[96,768]{1,0:T(8,128)(2,1)S(1)} %dynamic-slice_bitcast_fusion), channel_id=1, source_target_pairs={{0,16},{4,20},{8,24},{12,28},{16,0},{20,4},{24,8},{28,12},{1,17},{... | collective-permute-start | bytes 442376 | tf_op jit(solution)/shard_map/ppermute | solution.py:487
  10.9 2.1 quarter.1
  13.4 2.6 %collective-permute-start.3 = (bf16[96,576]{1,0:T(8,128)(2,1)}, bf16[96,576]{1,0:T(8,128)(2,1)}, u32[]{:S(2)}, u32[]{:S(2)}) collective-permute-start(bf16[96,576]{1,0:T(8,128)(2,1)} %get-tuple-element.33), channel_id=1, source_target_pairs={{0,16},{4,20},{8,24},{12,28},{16,0},{20,4},{24,8},{28,12},{1,17},{... | collective-permute-start | bytes 331784 | tf_op jit(solution)/shard_map/ppermute | solution.py:487
  16.0 1.6 constant_dynamic-update-slice_fusion.5
  18.5 2.3 fusion.place
  23.3 7.2 %collective-permute-done.3 = bf16[96,576]{1,0:T(8,128)(2,1)} collective-permute-done((bf16[96,576]{1,0:T(8,128)(2,1)}, bf16[96,576]{1,0:T(8,128)(2,1)}, u32[]{:S(2)}, u32[]{:S(2)}) %collective-permute-start.3) | collective-permute-done | bytes 110624 | tf_op jit(solution)/shard_map/ppermute | solution.py:487
  32.5 7.8 %collective-permute-done.6 = bf16[96,768]{1,0:T(8,128)(2,1)S(1)} collective-permute-done((bf16[96,768]{1,0:T(8,128)(2,1)}, bf16[96,768]{1,0:T(8,128)(2,1)S(1)}, u32[]{:S(2)}, u32[]{:S(2)}) %collective-permute-start.6) | collective-permute-done | bytes 147488 | tf_op jit(solution)/shard_map/ppermute | solution.py:487
  41.2 2.1 collective-permute-start.7
  44.4 7.8 %collective-permute-done.7 = bf16[96,768]{1,0:T(8,128)(2,1)S(1)} collective-permute-done((bf16[96,768]{1,0:T(8,128)(2,1)S(1)}, bf16[96,768]{1,0:T(8,128)(2,1)S(1)}, u32[]{:S(2)}, u32[]{:S(2)}) %collective-permute-start.7) | collective-permute-done | bytes 147488 | tf_op jit(solution)/shard_map/ppermute | solution.py:487
  52.2 7.3 %collective-permute-done.10 = bf16[192,896]{1,0:T(8,128)(2,1)S(1)} collective-permute-done((bf16[192,896]{1,0:T(8,128)(2,1)S(1)}, bf16[192,896]{1,0:T(8,128)(2,1)S(1)}, u32[]{:S(2)}, u32[]{:S(2)}) %collective-permute-start.10) | collective-permute-done | bytes 344096 | tf_op jit(solution)/shard_map/ppermute | solution.py:487
  59.6 1.5 collective-permute-start.8
  61.2 2.6 %collective-permute-done.13 = bf16[192,768]{1,0:T(8,128)(2,1)S(1)} collective-permute-done((bf16[192,768]{1,0:T(8,128)(2,1)S(1)}, bf16[192,768]{1,0:T(8,128)(2,1)S(1)}, u32[]{:S(2)}, u32[]{:S(2)}) %collective-permute-start.13) | collective-permute-done | bytes 294944 | tf_op jit(solution)/shard_map/ppermute | solution.py:487
  63.7 1.5 collective-permute-start.11
  66.9 1.6 collective-permute-start.5
  71.3 23.4 %collective-permute-done.14.down_hi = bf16[384,768]{1,0:T(8,128)(2,1)S(1)} collective-permute-done((bf16[384,768]{1,0:T(8,128)(2,1)S(1)}, bf16[384,768]{1,0:T(8,128)(2,1)S(1)}, u32[]{:S(2)}, u32[]{:S(2)}) %collective-permute-start.14) | collective-permute-done | bytes 589856 | tf_op jit(solution)/shard_map/ppermute | solution.py:487
  95.7 20.1 %mlp.1 = (bf16[384,1536]{1,0:T(8,128)(2,1)}, bf16[384,1536]{1,0:T(8,128)(2,1)}, f32[4,256,768]{2,1,0:T(8,128)}, f32[4,256,768]{2,1,0:T(8,128)}, f32[16,768]{1,0:T(8,128)}, /*index=5*/f32[8,768]{1,0:T(8,128)}) custom-call(bf16[528,768]{1,0:T(8,128)(2,1)} %copy-done.1, bf16[528,768]{1,0:T(8,128)(2,1)} %copy-done.2, bf16[528,768]{1,0:T(8,128)(2,1)} %copy-done.3, ...), custom_call_target="tpu_custom_call" | custom-call | tf_op jit(solution)/shard_map/mlp/pallas_call | solution.py:262
  115.8 42.1 %attention.1 = (bf16[384,896]{1,0:T(8,128)(2,1)}, bf16[384,896]{1,0:T(8,128)(2,1)}, bf16[2,256,1536]{2,1,0:T(8,128)(2,1)}, bf16[2,256,1536]{2,1,0:T(8,128)(2,1)}) custom-call(bf16[528,768]{1,0:T(8,128)(2,1)} %copy-done.1, bf16[528,768]{1,0:T(8,128)(2,1)} %copy-done.2, bf16[528,768]{1,0:T(8,128)(2,1)} %copy-done.3, ...), custom_call_target="tpu_custom_call" | custom-call | tf_op jit(solution)/shard_map/attention/pallas_call | solution.py:309
  157.9 1.6 collective-permute-start.23
  159.5 11.7 %collective-permute-done.23 = bf16[384,896]{1,0:T(8,128)(2,1)S(1)} collective-permute-done((bf16[384,896]{1,0:T(8,128)(2,1)}, bf16[384,896]{1,0:T(8,128)(2,1)S(1)}, u32[]{:S(2)}, u32[]{:S(2)}) %collective-permute-start.23) | collective-permute-done | bytes 688160 | tf_op jit(solution)/shard_map/ppermute | solution.py:487
  173.6 1.5 collective-permute-start.17
  176.5 5.7 %collective-permute-done.24 = bf16[192,1088]{1,0:T(8,128)(2,1)} collective-permute-done((bf16[192,1088]{1,0:T(8,128)(2,1)}, bf16[192,1088]{1,0:T(8,128)(2,1)}, u32[]{:S(2)}, u32[]{:S(2)}) %collective-permute-start.24) | collective-permute-done | bytes 417824 | tf_op jit(solution)/shard_map/ppermute | solution.py:487
  184.7 1.5 collective-permute-start.25
  186.1 9.7 %collective-permute-done.17 = bf16[384,1536]{1,0:T(8,128)(2,1)} collective-permute-done((bf16[384,1536]{1,0:T(8,128)(2,1)}, bf16[384,1536]{1,0:T(8,128)(2,1)}, u32[]{:S(2)}, u32[]{:S(2)}) %collective-permute-start.17) | collective-permute-done | bytes 1179680 | tf_op jit(solution)/shard_map/ppermute | solution.py:487
  195.9 1.9 add_convert_fusion
  200.0 10.2 %collective-permute-done.18 = bf16[192,1536]{1,0:T(8,128)(2,1)S(1)} collective-permute-done((bf16[192,1536]{1,0:T(8,128)(2,1)S(1)}, bf16[192,1536]{1,0:T(8,128)(2,1)S(1)}, u32[]{:S(2)}, u32[]{:S(2)}) %collective-permute-start.18) | collective-permute-done | bytes 589856 | tf_op jit(solution)/shard_map/ppermute | solution.py:487
  210.4 3.9 %collective-permute-start.19 = (bf16[96,1536]{1,0:T(8,128)(2,1)S(1)}, bf16[96,1536]{1,0:T(8,128)(2,1)S(1)}, u32[]{:S(2)}, u32[]{:S(2)}) collective-permute-start(bf16[96,1536]{1,0:T(8,128)(2,1)S(1)} %slice.129), channel_id=1, source_target_pairs={{0,16},{4,20},{8,24},{12,28},{16,0},{20,4},{24,8},{28,12},{1,17},{... | collective-permute-start | bytes 884744 | tf_op jit(solution)/shard_map/ppermute | solution.py:487
  214.4 2.0 collective-permute-start.16
  216.4 5.7 %collective-permute-done.19 = bf16[96,1536]{1,0:T(8,128)(2,1)S(1)} collective-permute-done((bf16[96,1536]{1,0:T(8,128)(2,1)S(1)}, bf16[96,1536]{1,0:T(8,128)(2,1)S(1)}, u32[]{:S(2)}, u32[]{:S(2)}) %collective-permute-start.19) | collective-permute-done | bytes 294944 | tf_op jit(solution)/shard_map/ppermute | solution.py:487
  224.9 5.4 %collective-permute-done.20.refs_1_ = bf16[96,1536]{1,0:T(8,128)(2,1)S(1)} collective-permute-done((bf16[96,1536]{1,0:T(8,128)(2,1)S(1)}, bf16[96,1536]{1,0:T(8,128)(2,1)S(1)}, u32[]{:S(2)}, u32[]{:S(2)}) %collective-permute-start.20) | collective-permute-done | bytes 294944 | tf_op jit(solution)/shard_map/ppermute | solution.py:493
  232.6 4.5 %finish.1 = (bf16[256,768]{1,0:T(8,128)(2,1)}, bf16[256,768]{1,0:T(8,128)(2,1)}) custom-call(bf16[528,768]{1,0:T(8,128)(2,1)} %copy-done.1, f32[256,1536]{1,0:T(8,128)} %slice_bitcast_fusion.near, bf16[256,1536]{1,0:T(8,128)(2,1)} %copy-done.10, bf16[768,768]{1,0:T(8,128)(2,1)} %fusion.3.to_rel, f32[1,768]{1,0:T(1,128)} %slice_add_fusion.out_bias, ...), custom_call_target="tpu_custom_call" | custom-call | tf_op jit(solution)/shard_map/finish/pallas_call | solution.py:375
  237.8 4.2 %assemble.1 = (f32[96,2304]{1,0:T(8,128)}, f32[96,768]{1,0:T(8,128)}, f32[96,3072]{1,0:T(8,128)}, f32[384,768]{1,0:T(8,128)}, f32[16,96]{1,0:T(8,128)}) custom-call(bf16[96,1536]{1,0:T(8,128)(2,1)} %copy-done.7, bf16[96,1536]{1,0:T(8,128)(2,1)} %copy-done.16, bf16[96,1536]{1,0:T(8,128)(2,1)} %collective-permute-done.21.refs_2_, ...), custom_call_target="tpu_custom_call" | custom-call | tf_op jit(solution)/shard_map/assemble/pallas_call | solution.py:415
  (163 shorter events, 36.5 us)
Async XLA Ops:
  4.4 56.7 %collective-permute-start = (bf16[528,768]{1,0:T(8,128)(2,1)S(1)}, bf16[528,768]{1,0:T(8,128)(2,1)S(1)}, u32[]{:S(2)}, u32[]{:S(2)}) collective-permute-start(bf16[528,768]{1,0:T(8,128)(2,1)S(1)} %fusion.6.near.pack), channel_id=1, source_target_pairs={{0,2},{1,3},{2,0},{3,1},{4,6},{5,7},{6,4},{7,5},{8,10},{9,11},{10,... | collective-permute-start | bytes 2433032 | tf_op jit(solution)/shard_map/ppermute | solution.py:493
  7.4 63.9 %collective-permute-start.1 = (bf16[528,768]{1,0:T(8,128)(2,1)S(1)}, bf16[528,768]{1,0:T(8,128)(2,1)S(1)}, u32[]{:S(2)}, u32[]{:S(2)}) collective-permute-start(bf16[528,768]{1,0:T(8,128)(2,1)S(1)} %fusion.6.near.pack), channel_id=1, source_target_pairs={{0,1},{1,0},{2,3},{3,2},{4,5},{5,4},{6,7},{7,6},{8,9},{9,8},{10,11... | collective-permute-start | bytes 2433032 | tf_op jit(solution)/shard_map/ppermute | solution.py:490
  7.4 33.8 %collective-permute-start.12 = (bf16[96,768]{1,0:T(8,128)(2,1)S(1)}, bf16[96,768]{1,0:T(8,128)(2,1)}, u32[]{:S(2)}, u32[]{:S(2)}) collective-permute-start(bf16[96,768]{1,0:T(8,128)(2,1)S(1)} %dynamic-slice_bitcast_fusion), channel_id=1, source_target_pairs={{0,16},{4,20},{8,24},{12,28},{16,0},{20,4},{24,8},{28,12},{1,17},{... | collective-permute-start | bytes 442376 | tf_op jit(solution)/shard_map/ppermute | solution.py:487
  13.1 31.1 %collective-permute-start.9 = (bf16[96,896]{1,0:T(8,128)(2,1)}, bf16[96,896]{1,0:T(8,128)(2,1)S(1)}, u32[]{:S(2)}, u32[]{:S(2)}) collective-permute-start(bf16[96,896]{1,0:T(8,128)(2,1)} %get-tuple-element.34), channel_id=1, source_target_pairs={{0,16},{4,20},{8,24},{12,28},{16,0},{20,4},{24,8},{28,12},{1,17},{... | collective-permute-start | bytes 516104 | tf_op jit(solution)/shard_map/ppermute | solution.py:487
  13.4 17.2 %collective-permute-start.3 = (bf16[96,576]{1,0:T(8,128)(2,1)}, bf16[96,576]{1,0:T(8,128)(2,1)}, u32[]{:S(2)}, u32[]{:S(2)}) collective-permute-start(bf16[96,576]{1,0:T(8,128)(2,1)} %get-tuple-element.33), channel_id=1, source_target_pairs={{0,16},{4,20},{8,24},{12,28},{16,0},{20,4},{24,8},{28,12},{1,17},{... | collective-permute-start | bytes 331784 | tf_op jit(solution)/shard_map/ppermute | solution.py:487
  30.6 9.7 %collective-permute-start.6 = (bf16[96,768]{1,0:T(8,128)(2,1)}, bf16[96,768]{1,0:T(8,128)(2,1)S(1)}, u32[]{:S(2)}, u32[]{:S(2)}) collective-permute-start(bf16[96,768]{1,0:T(8,128)(2,1)} %param.30), channel_id=1, source_target_pairs={{0,16},{4,20},{8,24},{12,28},{16,0},{20,4},{24,8},{28,12},{1,17},{... | collective-permute-start | bytes 442376 | tf_op jit(solution)/shard_map/ppermute | solution.py:487
  40.2 26.0 %collective-permute-start.4 = (bf16[192,576]{1,0:T(8,128)(2,1)S(1)}, bf16[192,576]{1,0:T(8,128)(2,1)S(1)}, u32[]{:S(2)}, u32[]{:S(2)}) collective-permute-start(bf16[192,576]{1,0:T(8,128)(2,1)S(1)} %pad_maximum_fusion.4), channel_id=1, source_target_pairs={{0,8},{4,12},{8,0},{12,4},{16,24},{20,28},{24,16},{28,20},{1,9},{5... | collective-permute-start | bytes 663560 | tf_op jit(solution)/shard_map/ppermute | solution.py:487
  41.2 11.0 %collective-permute-start.7 = (bf16[96,768]{1,0:T(8,128)(2,1)S(1)}, bf16[96,768]{1,0:T(8,128)(2,1)S(1)}, u32[]{:S(2)}, u32[]{:S(2)}) collective-permute-start(bf16[96,768]{1,0:T(8,128)(2,1)S(1)} %broadcast_select_fusion), channel_id=1, source_target_pairs={{0,8},{4,12},{8,0},{12,4},{16,24},{20,28},{24,16},{28,20},{1,9},{5... | collective-permute-start | bytes 442376 | tf_op jit(solution)/shard_map/ppermute | solution.py:487
  44.3 15.3 %collective-permute-start.10 = (bf16[192,896]{1,0:T(8,128)(2,1)S(1)}, bf16[192,896]{1,0:T(8,128)(2,1)S(1)}, u32[]{:S(2)}, u32[]{:S(2)}) collective-permute-start(bf16[192,896]{1,0:T(8,128)(2,1)S(1)} %pad_maximum_fusion.1), channel_id=1, source_target_pairs={{0,8},{4,12},{8,0},{12,4},{16,24},{20,28},{24,16},{28,20},{1,9},{5... | collective-permute-start | bytes 1032200 | tf_op jit(solution)/shard_map/ppermute | solution.py:487
  52.2 11.5 %collective-permute-start.13 = (bf16[192,768]{1,0:T(8,128)(2,1)S(1)}, bf16[192,768]{1,0:T(8,128)(2,1)S(1)}, u32[]{:S(2)}, u32[]{:S(2)}) collective-permute-start(bf16[192,768]{1,0:T(8,128)(2,1)S(1)} %pad_maximum_fusion.3), channel_id=1, source_target_pairs={{0,8},{4,12},{8,0},{12,4},{16,24},{20,28},{24,16},{28,20},{1,9},{5... | collective-permute-start | bytes 884744 | tf_op jit(solution)/shard_map/ppermute | solution.py:487
  59.6 7.3 %collective-permute-start.8 = (bf16[96,768]{1,0:T(8,128)(2,1)S(1)}, bf16[96,768]{1,0:T(8,128)(2,1)S(1)}, u32[]{:S(2)}, u32[]{:S(2)}) collective-permute-start(bf16[96,768]{1,0:T(8,128)(2,1)S(1)} %broadcast_select_fusion.1), channel_id=1, source_target_pairs={{0,4},{4,0},{8,12},{12,8},{16,20},{20,16},{24,28},{28,24},{1,5},{5... | collective-permute-start | bytes 442376 | tf_op jit(solution)/shard_map/ppermute | solution.py:487
  61.1 34.5 %collective-permute-start.2 = (bf16[528,768]{1,0:T(8,128)(2,1)S(1)}, bf16[528,768]{1,0:T(8,128)(2,1)}, u32[]{:S(2)}, u32[]{:S(2)}) collective-permute-start(bf16[528,768]{1,0:T(8,128)(2,1)S(1)} %collective-permute-done.across), channel_id=1, source_target_pairs={{0,1},{1,0},{2,3},{3,2},{4,5},{5,4},{6,7},{7,6},{8,9},{9,8},{10,11... | collective-permute-start | bytes 2433032 | tf_op jit(solution)/shard_map/ppermute | solution.py:490
  63.7 31.0 %collective-permute-start.11 = (bf16[384,896]{1,0:T(8,128)(2,1)S(1)}, bf16[384,896]{1,0:T(8,128)(2,1)S(1)}, u32[]{:S(2)}, u32[]{:S(2)}) collective-permute-start(bf16[384,896]{1,0:T(8,128)(2,1)S(1)} %constant_dynamic-update-slice_fusion.3.up_lo), channel_id=1, source_target_pairs={{0,4},{4,0},{8,12},{12,8},{16,20},{20,16},{24,28},{28,24},{1,5},{5... | collective-permute-start | bytes 2064392 | tf_op jit(solution)/shard_map/ppermute | solution.py:487
  66.2 28.5 %collective-permute-start.14 = (bf16[384,768]{1,0:T(8,128)(2,1)S(1)}, bf16[384,768]{1,0:T(8,128)(2,1)S(1)}, u32[]{:S(2)}, u32[]{:S(2)}) collective-permute-start(bf16[384,768]{1,0:T(8,128)(2,1)S(1)} %pad_maximum_fusion.down_lo), channel_id=1, source_target_pairs={{0,4},{4,0},{8,12},{12,8},{16,20},{20,16},{24,28},{28,24},{1,5},{5... | collective-permute-start | bytes 1769480 | tf_op jit(solution)/shard_map/ppermute | solution.py:487
  66.8 49.0 %copy-start.11 = (bf16[384,576]{1,0:T(8,128)(2,1)}, bf16[384,576]{1,0:T(8,128)(2,1)S(1)}, u32[]{:S(2)}) copy-start(bf16[384,576]{1,0:T(8,128)(2,1)S(1)} %constant_dynamic-update-slice_fusion.qkv_lo) | copy-start | bytes 1327108
  66.9 48.9 %collective-permute-start.5 = (bf16[384,576]{1,0:T(8,128)(2,1)S(1)}, bf16[384,576]{1,0:T(8,128)(2,1)}, u32[]{:S(2)}, u32[]{:S(2)}) collective-permute-start(bf16[384,576]{1,0:T(8,128)(2,1)S(1)} %constant_dynamic-update-slice_fusion.qkv_lo), channel_id=1, source_target_pairs={{0,4},{4,0},{8,12},{12,8},{16,20},{20,16},{24,28},{28,24},{1,5},{5... | collective-permute-start | bytes 1327112 | tf_op jit(solution)/shard_map/ppermute | solution.py:487
  71.3 24.3 %copy-start.3 = (bf16[528,768]{1,0:T(8,128)(2,1)}, bf16[528,768]{1,0:T(8,128)(2,1)S(1)}, u32[]{:S(2)}) copy-start(bf16[528,768]{1,0:T(8,128)(2,1)S(1)} %collective-permute-done.1.beside) | copy-start | bytes 2433028
  157.9 13.3 %collective-permute-start.23 = (bf16[384,896]{1,0:T(8,128)(2,1)}, bf16[384,896]{1,0:T(8,128)(2,1)S(1)}, u32[]{:S(2)}, u32[]{:S(2)}) collective-permute-start(bf16[384,896]{1,0:T(8,128)(2,1)} %get-tuple-element.46), channel_id=1, source_target_pairs={{0,4},{4,0},{8,12},{12,8},{16,20},{20,16},{24,28},{28,24},{1,5},{5... | collective-permute-start | bytes 2064392 | tf_op jit(solution)/shard_map/ppermute | solution.py:487
  173.6 8.6 %collective-permute-start.24 = (bf16[192,1088]{1,0:T(8,128)(2,1)}, bf16[192,1088]{1,0:T(8,128)(2,1)}, u32[]{:S(2)}, u32[]{:S(2)}) collective-permute-start(bf16[192,1088]{1,0:T(8,128)(2,1)} %concatenate.56), channel_id=1, source_target_pairs={{0,8},{4,12},{8,0},{12,4},{16,24},{20,28},{24,16},{28,20},{1,9},{5... | collective-permute-start | bytes 1253384 | tf_op jit(solution)/shard_map/ppermute | solution.py:487
  173.6 22.3 %collective-permute-start.17 = (bf16[384,1536]{1,0:T(8,128)(2,1)}, bf16[384,1536]{1,0:T(8,128)(2,1)}, u32[]{:S(2)}, u32[]{:S(2)}) collective-permute-start(bf16[384,1536]{1,0:T(8,128)(2,1)} %get-tuple-element.44), channel_id=1, source_target_pairs={{0,4},{4,0},{8,12},{12,8},{16,20},{20,16},{24,28},{28,24},{1,5},{5... | collective-permute-start | bytes 3538952 | tf_op jit(solution)/shard_map/ppermute | solution.py:487
  176.5 23.1 %collective-permute-start.15 = (bf16[2,256,1536]{2,1,0:T(8,128)(2,1)}, bf16[2,256,1536]{2,1,0:T(8,128)(2,1)S(1)}, u32[]{:S(2)}, u32[]{:S(2)}) collective-permute-start(bf16[2,256,1536]{2,1,0:T(8,128)(2,1)} %get-tuple-element.40), channel_id=1, source_target_pairs={{0,1},{1,0},{2,3},{3,2},{4,5},{5,4},{6,7},{7,6},{8,9},{9,8},{10,11... | collective-permute-start | bytes 4718600 | tf_op jit(solution)/shard_map/ppermute | solution.py:490
  184.7 14.3 %collective-permute-start.25 = (bf16[96,1472]{1,0:T(8,128)(2,1)S(1)}, bf16[96,1472]{1,0:T(8,128)(2,1)S(1)}, u32[]{:S(2)}, u32[]{:S(2)}) collective-permute-start(bf16[96,1472]{1,0:T(8,128)(2,1)S(1)} %concatenate.59), channel_id=1, source_target_pairs={{0,16},{4,20},{8,24},{12,28},{16,0},{20,4},{24,8},{28,12},{1,17},{... | collective-permute-start | bytes 847880 | tf_op jit(solution)/shard_map/ppermute | solution.py:487
  197.8 12.4 %collective-permute-start.18 = (bf16[192,1536]{1,0:T(8,128)(2,1)S(1)}, bf16[192,1536]{1,0:T(8,128)(2,1)S(1)}, u32[]{:S(2)}, u32[]{:S(2)}) collective-permute-start(bf16[192,1536]{1,0:T(8,128)(2,1)S(1)} %slice.127), channel_id=1, source_target_pairs={{0,8},{4,12},{8,0},{12,4},{16,24},{20,28},{24,16},{28,20},{1,9},{5... | collective-permute-start | bytes 1769480 | tf_op jit(solution)/shard_map/ppermute | solution.py:487
  199.0 25.4 %copy-start.6 = (bf16[96,1472]{1,0:T(8,128)(2,1)}, bf16[96,1472]{1,0:T(8,128)(2,1)S(1)}, u32[]{:S(2)}) copy-start(bf16[96,1472]{1,0:T(8,128)(2,1)S(1)} %add_convert_fusion.3.refs_4_) | copy-start | bytes 847876
  199.0 25.4 %collective-permute-start.26 = (bf16[96,1472]{1,0:T(8,128)(2,1)S(1)}, bf16[96,1472]{1,0:T(8,128)(2,1)S(1)}, u32[]{:S(2)}, u32[]{:S(2)}) collective-permute-start(bf16[96,1472]{1,0:T(8,128)(2,1)S(1)} %add_convert_fusion.3.refs_4_), channel_id=1, source_target_pairs={{0,2},{1,3},{2,0},{3,1},{4,6},{5,7},{6,4},{7,5},{8,10},{9,11},{10,... | collective-permute-start | bytes 847880 | tf_op jit(solution)/shard_map/ppermute | solution.py:493
  210.4 11.6 %collective-permute-start.19 = (bf16[96,1536]{1,0:T(8,128)(2,1)S(1)}, bf16[96,1536]{1,0:T(8,128)(2,1)S(1)}, u32[]{:S(2)}, u32[]{:S(2)}) collective-permute-start(bf16[96,1536]{1,0:T(8,128)(2,1)S(1)} %slice.129), channel_id=1, source_target_pairs={{0,16},{4,20},{8,24},{12,28},{16,0},{20,4},{24,8},{28,12},{1,17},{... | collective-permute-start | bytes 884744 | tf_op jit(solution)/shard_map/ppermute | solution.py:487
  214.4 17.3 %collective-permute-start.16 = (bf16[256,1536]{1,0:T(8,128)(2,1)S(1)}, bf16[256,1536]{1,0:T(8,128)(2,1)S(1)}, u32[]{:S(2)}, u32[]{:S(2)}) collective-permute-start(bf16[256,1536]{1,0:T(8,128)(2,1)S(1)} %fusion.7), channel_id=1, source_target_pairs={{0,2},{1,3},{2,0},{3,1},{4,6},{5,7},{6,4},{7,5},{8,10},{9,11},{10,... | collective-permute-start | bytes 2359304 | tf_op jit(solution)/shard_map/ppermute | solution.py:493
  222.1 8.2 %collective-permute-start.20 = (bf16[96,1536]{1,0:T(8,128)(2,1)S(1)}, bf16[96,1536]{1,0:T(8,128)(2,1)S(1)}, u32[]{:S(2)}, u32[]{:S(2)}) collective-permute-start(bf16[96,1536]{1,0:T(8,128)(2,1)S(1)} %add_convert_fusion.5.refs_0_), channel_id=1, source_target_pairs={{0,2},{1,3},{2,0},{3,1},{4,6},{5,7},{6,4},{7,5},{8,10},{9,11},{10,... | collective-permute-start | bytes 884744 | tf_op jit(solution)/shard_map/ppermute | solution.py:493
  224.3 12.7 %collective-permute-start.27 = (bf16[96,1472]{1,0:T(8,128)(2,1)S(1)}, bf16[96,1472]{1,0:T(8,128)(2,1)S(1)}, u32[]{:S(2)}, u32[]{:S(2)}) collective-permute-start(bf16[96,1472]{1,0:T(8,128)(2,1)S(1)} %add_convert_fusion.3.refs_4_), channel_id=1, source_target_pairs={{0,1},{1,0},{2,3},{3,2},{4,5},{5,4},{6,7},{7,6},{8,9},{9,8},{10,11... | collective-permute-start | bytes 847880 | tf_op jit(solution)/shard_map/ppermute | solution.py:490
  224.4 12.7 %collective-permute-start.28 = (bf16[96,1472]{1,0:T(8,128)(2,1)S(1)}, bf16[96,1472]{1,0:T(8,128)(2,1)}, u32[]{:S(2)}, u32[]{:S(2)}) collective-permute-start(bf16[96,1472]{1,0:T(8,128)(2,1)S(1)} %collective-permute-done.26.refs_5_), channel_id=1, source_target_pairs={{0,1},{1,0},{2,3},{3,2},{4,5},{5,4},{6,7},{7,6},{8,9},{9,8},{10,11... | collective-permute-start | bytes 847880 | tf_op jit(solution)/shard_map/ppermute | solution.py:490
  224.9 12.2 %collective-permute-start.21 = (bf16[96,1536]{1,0:T(8,128)(2,1)S(1)}, bf16[96,1536]{1,0:T(8,128)(2,1)}, u32[]{:S(2)}, u32[]{:S(2)}) collective-permute-start(bf16[96,1536]{1,0:T(8,128)(2,1)S(1)} %add_convert_fusion.5.refs_0_), channel_id=1, source_target_pairs={{0,1},{1,0},{2,3},{3,2},{4,5},{5,4},{6,7},{7,6},{8,9},{9,8},{10,11... | collective-permute-start | bytes 884744 | tf_op jit(solution)/shard_map/ppermute | solution.py:490
  230.4 6.7 %collective-permute-start.22 = (bf16[96,1536]{1,0:T(8,128)(2,1)S(1)}, bf16[96,1536]{1,0:T(8,128)(2,1)}, u32[]{:S(2)}, u32[]{:S(2)}) collective-permute-start(bf16[96,1536]{1,0:T(8,128)(2,1)S(1)} %collective-permute-done.20.refs_1_), channel_id=1, source_target_pairs={{0,1},{1,0},{2,3},{3,2},{4,5},{5,4},{6,7},{7,6},{8,9},{9,8},{10,11... | collective-permute-start | bytes 884744 | tf_op jit(solution)/shard_map/ppermute | solution.py:490
  (27 other events, 224.4 us)
where the time goes:
time: 247 us
  waiting for transfers between devices  105 us (43%)
  Pallas kernels  73 us (30%)
  starting transfers between devices  29.8 us (12%)
  other arithmetic  22.3 us (9%)
  local copies, waits for them, and re-layouts  15.2 us (6%)
    ppermute x18, waiting for transfers between devices, shard_swap(): return lax.ppermute(value, 'fsdp', [(i, i ^ mask) for i in range(shards)])  99.2 us
    pallas_call x1, Pallas kernels, run_attention(): pl.pallas_call(functools.partial(attention_kernel, rows), grid=(GROUP,),...  42.1 us
    ppermute x18, starting transfers between devices, shard_swap(): return lax.ppermute(value, 'fsdp', [(i, i ^ mask) for i in range(shards)])  22.5 us
    pallas_call x1, Pallas kernels, run_mlp(): pl.pallas_call(mlp_kernel, grid=(GROUP,), in_specs=[whole(packed, D)] * 4...  20.1 us
    unnamed x66, local copies, waits for them, and re-layouts  6.73 us
    ppermute x4, starting transfers between devices, x_swap(): return lax.ppermute(value, 'rep', [(i, i ^ 2) for i in range(GROUP)])  6.64 us
    ppermute x4, waiting for transfers between devices, x_swap(): return lax.ppermute(value, 'rep', [(i, i ^ 2) for i in range(GROUP)])  5.45 us
  transfers between devices with their start and end apart: 29, of which 12 were waited for; matrix products, arithmetic and copies ran while one was open for 10% of the time, Pallas kernels for 11%

commit v1 on v0

--- a/solution.py
+++ b/solution.py
@@ -57,8 +57,9 @@
 
 
 def mlp_kernel(
+    down_place,
     near, across, beside, far, up_lo, up_hi, down_lo, down_hi, to_rel, rep,
-    keep, send, out_part, grad_norm, vectors_out, sums,
+    keep, send, out_part, grad_norm, values_out, vectors_out, sums,
     up_rel, down_rel, down_acc, up_acc,
 ):
     step = pl.program_id(0)
@@ -70,8 +71,15 @@
     def _():
         up_rel[:half] = dot(up_lo[:, :D], to_rel[...]).astype(BF16)
         up_rel[half:] = dot(up_hi[:, :D], to_rel[...]).astype(BF16)
-        down_rel[:half] = down_lo[...]
-        down_rel[half:] = down_hi[...]
+        block = D // len(down_place)
+        if down_place == sorted(down_place):
+            down_rel[:half] = down_lo[...]
+            down_rel[half:] = down_hi[...]
+        else:
+            for source, target in enumerate(down_place):
+                piece = down_hi if source * block >= half else down_lo
+                start = source * block % half
+                down_rel[target * block : (target + 1) * block] = piece[start : start + block]
         vectors_out[:, :half] = up_lo[:, D:].astype(F32).T[:16]
         vectors_out[:, half:] = up_hi[:, D:].astype(F32).T[:16]
         down_acc[...] = jnp.zeros_like(down_acc)
@@ -80,7 +88,9 @@
 
     inputs = take(step, packs, slice(0, own))
     grad_out = take(step, packs, slice(own, 2 * own))
-    normed, unit = layer_norm(dot(inputs, to_rel[...]), vectors_out[2:3], vectors_out[3:4])
+    values = dot(inputs, to_rel[...])
+    values_out[0] = values.astype(BF16)
+    normed, unit = layer_norm(values, vectors_out[2:3], vectors_out[3:4])
     bias = vectors_out[11:12]
     for quarter in range(GROUP - 1):
         bias = jnp.where(rep[0] == quarter, vectors_out[8 + quarter : 9 + quarter], bias)
@@ -91,8 +101,7 @@
     down_acc[...] += t_dot(activ, grad_out)
     grad_pre = dot_t(grad_out, down_rel[...]) * slope
     grad_pre_b = grad_pre.astype(BF16)
-    grad_nat = dot_t(grad_pre_b, to_rel[...]).astype(BF16)
-    up_acc[...] += t_dot(normed, grad_nat)
+    up_acc[...] += t_dot(normed, grad_pre_b)
     gn = dot_t(grad_pre_b, up_rel[...])
     out_part[0] = dot(activ, down_rel[...])
     grad_norm[0] = gn
@@ -104,16 +113,16 @@
     def _():
         keep[:, :D] = down_acc[:half].astype(BF16)
         send[:, :D] = down_acc[half:].astype(BF16)
-        keep[:, D:] = up_acc[:half].astype(BF16)
-        send[:, D:] = up_acc[half:].astype(BF16)
+        keep[:, D:] = dot_t(up_acc[:half].astype(BF16), to_rel[...]).astype(BF16)
+        send[:, D:] = dot_t(up_acc[half:].astype(BF16), to_rel[...]).astype(BF16)
 
 
 def attention_kernel(
     block_rows,
     near, across, beside, far, qkv_lo, qkv_hi, proj, to_rel, vectors, mlp_sums, place, spread, head_spread,
-    cosines, sines, mlp_part, mlp_norm, rep,
+    cosines, sines, mlp_part, mlp_norm, values, rep,
     keep, send, partial_near, partial_far,
-    wide, proj_wide, bias_wide, qkv_acc, proj_acc, gp_ref, ctx_ref, sums, bias_sums,
+    wide, proj_wide, bias_wide, qkv_rel, qkv_acc, proj_acc, gp_ref, ctx_ref, sums, bias_sums,
 ):
     step = pl.program_id(0)
     packs = (near, across, beside, far)
@@ -123,6 +132,8 @@
 
     @pl.when(step == 0)
     def _():
+        qkv_rel[:half] = qkv_lo[...]
+        qkv_rel[half:] = qkv_hi[...]
         wide[:half] = dot(qkv_lo[...], spread[...]).astype(BF16)
         wide[half:] = dot(qkv_hi[...], spread[...]).astype(BF16)
         proj_wide[...] = dot(head_spread[...], proj[...]).astype(BF16)
@@ -135,59 +146,67 @@
         sums[...] = jnp.zeros_like(sums)
         bias_sums[...] = jnp.zeros_like(bias_sums)
 
-    inputs = take(step, packs, slice(0, own))
     grad_out = take(step, packs, slice(own, count))
     segment_row = take(step, packs, slice(count, count + 16)).astype(F32)
-    normed, unit = layer_norm(dot(inputs, to_rel[...]), vectors[0:1], vectors[1:2])
+    normed, unit = layer_norm(values[0].astype(F32), vectors[0:1], vectors[1:2])
     projected = dot(normed, wide[...]) + bias_wide[0:1]
     grad_context = dot_t(grad_out, proj_wide[...]).astype(BF16)
     lane = lax.broadcasted_iota(jnp.int32, (LANES, LANES), 1)
     sublane = lax.broadcasted_iota(jnp.int32, (LANES, LANES), 0)
     lower = lane < HDIM
-    zero = jnp.zeros((LANES, LANES), F32)
+    units = [(slab, head) for slab in range(own // LANES) for head in range(LOCAL_HEADS)]
+    allowed, cos, sin = [], [], []
     for slab in range(own // LANES):
-        row = slice(slab * LANES, (slab + 1) * LANES)
-        seg_keys = jnp.broadcast_to(segment_row[0:1, row], (LANES, LANES))
-        seg_queries = seg_keys.T
-        same = seg_keys == seg_queries
-        allowed = same & (lane <= sublane)
+        seg_keys = jnp.broadcast_to(segment_row[0:1, slab * LANES : (slab + 1) * LANES], (LANES, LANES))
+        same = seg_keys == seg_keys.T
+        allowed.append(same & (lane <= sublane))
         position = jnp.sum(jnp.where(same & (lane < sublane), 1.0, 0.0), axis=1, keepdims=True)
         pick = (lane.astype(F32) == position).astype(BF16)
-        cos = dot(pick, cosines[0]) + dot(pick, cosines[1]) + dot(pick, cosines[2])
-        sin = dot(pick, sines[0]) + dot(pick, sines[1]) + dot(pick, sines[2])
-
-        def turn(value, direction):
-            return value * cos + direction * (pltpu.roll(value, HDIM, 1) * sin)
-
-        for head in range(LOCAL_HEADS):
-            def part(which):
-                start = which * EXT + head * LANES
-                return slice(start, start + LANES)
-
-            query = (turn(projected[row, part(0)], 1.0) * 0.125).astype(BF16)
-            key = turn(projected[row, part(1)], 1.0).astype(BF16)
-            value = projected[row, part(2)].astype(BF16)
-            gctx = grad_context[row, part(0)]
-            query_half = jnp.where(lower, query, jnp.zeros_like(query))
-            scores = jnp.where(allowed, dot_t(query_half, key), NEG_FILL)
-            highest = jnp.max(scores, axis=-1, keepdims=True)
-            weight = jnp.exp(scores - highest)
-            probs = weight / jnp.sum(weight, axis=-1, keepdims=True)
-            probs_b = probs.astype(BF16)
-            ctx_ref[row, part(0)] = dot(probs_b, value).astype(BF16)
-            grad_probs = dot_t(gctx, value)
-            grad_value = t_dot(probs_b, gctx)
-            delta = jnp.sum(probs * grad_probs, axis=-1, keepdims=True)
-            grad_sc = (probs * (grad_probs - delta)).astype(BF16)
-            grad_query = jnp.where(lower, turn(dot(grad_sc, key) * 0.125, -1.0), zero)
-            grad_key = jnp.where(lower, turn(t_dot(grad_sc, query), -1.0), zero)
-            for which, grad in enumerate((grad_query, grad_key, grad_value)):
-                gp_ref[row, part(which)] = grad.astype(BF16)
-                bias_sums[0:1, part(which)] += jnp.sum(grad, axis=0, keepdims=True)
-
-    grad_wide = gp_ref[...]
-    qkv_acc[...] += t_dot(normed, dot_t(grad_wide, spread[...]).astype(BF16))
-    gn = dot_t(grad_wide, wide[...])
+        cos.append(dot(pick, cosines[0]) + dot(pick, cosines[1]) + dot(pick, cosines[2]))
+        sin.append(dot(pick, sines[0]) + dot(pick, sines[1]) + dot(pick, sines[2]))
+
+    def part(value, unit, which):
+        slab, head = unit
+        start = which * EXT + head * LANES
+        return value[slab * LANES : (slab + 1) * LANES, start : start + LANES]
+
+    def turn(value, slab, direction):
+        return value * cos[slab] + direction * (pltpu.roll(value, HDIM, 1) * sin[slab])
+
+    query = [(turn(part(projected, u, 0), u[0], 1.0) * 0.125).astype(BF16) for u in units]
+    key = [turn(part(projected, u, 1), u[0], 1.0).astype(BF16) for u in units]
+    value = [part(projected, u, 2).astype(BF16) for u in units]
+    gctx = [part(grad_context, u, 0) for u in units]
+    count = range(len(units))
+    scores = [dot_t(jnp.where(lower, query[n], jnp.zeros_like(query[n])), key[n]) for n in count]
+    grad_probs = [dot_t(gctx[n], value[n]) for n in count]
+    scores = [jnp.where(allowed[units[n][0]], scores[n], NEG_FILL) for n in count]
+    weight = [jnp.exp(score - jnp.max(score, axis=-1, keepdims=True)) for score in scores]
+    probs = [each * (1.0 / jnp.sum(each, axis=-1, keepdims=True)) for each in weight]
+    probs_b = [each.astype(BF16) for each in probs]
+    context = [dot(probs_b[n], value[n]) for n in count]
+    grad_value = [t_dot(probs_b[n], gctx[n]) for n in count]
+    delta = [jnp.sum(probs[n] * grad_probs[n], axis=-1, keepdims=True) for n in count]
+    grad_sc = [(probs[n] * (grad_probs[n] - delta[n])).astype(BF16) for n in count]
+    grad_query = [dot(grad_sc[n], key[n]) for n in count]
+    grad_key = [t_dot(grad_sc[n], query[n]) for n in count]
+    for n, (slab, head) in enumerate(units):
+        row = slice(slab * LANES, (slab + 1) * LANES)
+        ctx_ref[row, head * LANES : (head + 1) * LANES] = context[n].astype(BF16)
+        turned = (
+            turn(grad_query[n] * 0.125, slab, -1.0),
+            turn(grad_key[n], slab, -1.0),
+            grad_value[n],
+        )
+        for which, grad in enumerate(turned):
+            start = which * QUART + head * HDIM
+            gp_ref[row, start : start + HDIM] = grad[:, :HDIM]
+
+    grad_proj = gp_ref[...]
+    bias_sums[0:1] += jnp.sum(grad_proj, axis=0, keepdims=True)
+    grad_proj = grad_proj.astype(BF16)
+    qkv_acc[...] += t_dot(normed, grad_proj)
+    gn = dot_t(grad_proj, qkv_rel[...])
     context = ctx_ref[...]
     proj_acc[...] += t_dot(dot(context, head_spread[...]).astype(BF16), grad_out)
     out_part = (dot(context, proj_wide[...]) + mlp_part[0]).astype(BF16)
@@ -215,8 +234,7 @@
         side = width + VEC_LANES
         vec = lax.broadcasted_iota(jnp.int32, (VEC_LANES, D), 0)
         out_bias = dot(sums[...].astype(BF16), to_rel[...])[2:3]
-        small = dot_t(bias_sums[...].astype(BF16), spread[...]).astype(BF16)
-        small = dot(small, place[...])
+        small = dot(bias_sums[...].astype(BF16), place[...])
         rows = [sums[0:1], sums[1:2], mlp_sums[0:1], mlp_sums[1:2]]
         rows += [small[0:1, k * D : (k + 1) * D] for k in range(3)] + [out_bias]
         table = jnp.where(vec == 8 + rep[0], mlp_sums[2:3], 0.0)
@@ -252,7 +270,7 @@
     return pl.BlockSpec(memory_space=pltpu.SMEM)
 
 
-def run_mlp(packs, up_lo, up_hi, down_lo, down_hi, to_rel, rep):
+def run_mlp(packs, up_lo, up_hi, down_lo, down_hi, to_rel, rep, down_place):
     packed = packs[0].shape[0]
     own = (packed - 16) // 2
     half = D // 2
@@ -260,12 +278,16 @@
     grad = jax.ShapeDtypeStruct((half, 2 * D), BF16)
     acts = jax.ShapeDtypeStruct((GROUP, own, D), F32)
     return pl.pallas_call(
-        mlp_kernel,
+        functools.partial(mlp_kernel, down_place),
         grid=(GROUP,),
         in_specs=[whole(packed, D)] * 4
         + [whole(half, wide), whole(half, wide), whole(half, D), whole(half, D), whole(D, D), smem()],
-        out_specs=[whole(half, 2 * D)] * 2 + [token_block(own, D)] * 2 + [whole(16, D), whole(8, D)],
-        out_shape=[grad] * 2 + [acts] * 2 + [jax.ShapeDtypeStruct((16, D), F32), jax.ShapeDtypeStruct((8, D), F32)],
+        out_specs=[whole(half, 2 * D)] * 2 + [token_block(own, D)] * 3 + [whole(16, D), whole(8, D)],
+        out_shape=[grad] * 2
+        + [acts] * 2
+        + [
+            jax.ShapeDtypeStruct((GROUP, own, D), BF16),
+            jax.ShapeDtypeStruct((16, D), F32), jax.ShapeDtypeStruct((8, D), F32)],
         scratch_shapes=[
             pltpu.VMEM((D, D), BF16),
             pltpu.VMEM((D, D), BF16),
@@ -277,7 +299,7 @@
     )(*packs, up_lo, up_hi, down_lo, down_hi, to_rel, rep)
 
 
-def run_attention(packs, qkv_lo, qkv_hi, proj, to_rel, vectors, mlp_sums, place, head_spread, mlp_part, mlp_norm, rep, rows):
+def run_attention(packs, qkv_lo, qkv_hi, proj, to_rel, vectors, mlp_sums, place, head_spread, mlp_part, mlp_norm, values, rep, rows):
     packed = packs[0].shape[0]
     own = (packed - 16) // 2
     half = D // 2
@@ -324,6 +346,7 @@
             whole(3, LANES, LANES),
             token_block(own, D),
             token_block(own, D),
+            token_block(own, D),
             smem(),
         ],
         out_specs=[
@@ -337,17 +360,19 @@
             pltpu.VMEM((D, 3 * EXT), BF16),
             pltpu.VMEM((EXT, D), BF16),
             pltpu.VMEM((8, 3 * EXT), F32),
+            pltpu.VMEM((D, width), BF16),
             pltpu.VMEM((D, width), F32),
             pltpu.VMEM((QUART, D), F32),
-            pltpu.VMEM((own, 3 * EXT), BF16),
+            pltpu.VMEM((own, width), F32),
             pltpu.VMEM((own, EXT), BF16),
             pltpu.VMEM((8, D), F32),
-            pltpu.VMEM((8, 3 * EXT), F32),
+            pltpu.VMEM((8, width), F32),
         ],
         compiler_params=PARAMS,
         name="attention",
     )(
-        *packs, qkv_lo, qkv_hi, proj, to_rel, vectors, mlp_sums, place, spread, head_spread, *tables, mlp_part, mlp_norm, rep
+        *packs, qkv_lo, qkv_hi, proj, to_rel, vectors, mlp_sums, place, spread, head_spread, *tables, mlp_part, mlp_norm,
+        values, rep
     )
 
 
@@ -444,7 +469,8 @@
     )
 
 
-def quarter_kernel(up, qkv, vectors, rep, up_own, qkv_own):
+def quarter_kernel(*refs):
+    vectors, (up, qkv, rep, up_own, qkv_own) = refs[:-5], refs[-5:]
     rows = up.shape[0]
     for natural in range(GROUP):
 
@@ -457,21 +483,26 @@
                 start = (which * GROUP + natural) * QUART
                 qkv_own[:, which * QUART : (which + 1) * QUART] = qkv[:, start : start + QUART]
 
-    up_own[:, D:] = jnp.pad(vectors[...], ((0, VEC_LANES - 16), (0, 0))).T.astype(BF16)
+    lines = [ref[k : k + 1].astype(F32) for ref in vectors for k in range(ref.shape[0])]
+    index = lax.broadcasted_iota(jnp.int32, (VEC_LANES, rows), 0)
+    table = jnp.zeros((VEC_LANES, rows), F32)
+    for place, line in enumerate(lines):
+        table = jnp.where(index == place, line, table)
+    up_own[:, D:] = table.T.astype(BF16)
 
 
 def run_quarter(up, qkv, vectors, rep):
     rows = up.shape[0]
     return pl.pallas_call(
         quarter_kernel,
-        in_specs=[pl.BlockSpec(memory_space=pltpu.VMEM)] * 3 + [smem()],
+        in_specs=[pl.BlockSpec(memory_space=pltpu.VMEM)] * (2 + len(vectors)) + [smem()],
         out_shape=[
             jax.ShapeDtypeStruct((rows, D + VEC_LANES), BF16),
             jax.ShapeDtypeStruct((rows, 3 * QUART), BF16),
         ],
         compiler_params=PARAMS,
         name="quarter",
-    )(up, qkv, vectors, rep)
+    )(*vectors, up, qkv, rep)
 
 
 def make_body(shards):
@@ -492,10 +523,15 @@
     def x_swap(value):
         return lax.ppermute(value, "rep", [(i, i ^ 2) for i in range(GROUP)])
 
-    def gather_all(own):
-        for mask in highest_first[:-1]:
+    down_order = highest_first if rows % 16 else lowest_first[:1] + highest_first[:-1]
+    down_place = [
+        reverse(sum(mask for k, mask in enumerate(down_order) if (p >> k) & 1), bits) for p in range(shards)
+    ]
+
+    def gather_all(own, order=highest_first):
+        for mask in order[:-1]:
             own = jnp.concatenate([own, shard_swap(own, mask)], axis=0)
-        return own, shard_swap(own, highest_first[-1])
+        return own, shard_swap(own, order[-1])
 
     def add(keep, received):
         return keep.astype(F32) + received.astype(F32)
@@ -539,20 +575,23 @@
         top_across, top_core = top // 2, top % 2
 
         rep_ref = rep.reshape(1)
-        vector_own = jnp.concatenate(
-            [first_gain, first_shift, second_gain, second_shift, qkv_bias, proj_bias, up_bias, down_bias]
-        )
-        vector_own = jnp.pad(vector_own.reshape(13, rows), ((0, 3), (0, 0)))
+        vectors_own = [
+            value.reshape(-1, rows)
+            for value in (
+                first_gain, first_shift, second_gain, second_shift, qkv_bias, proj_bias, up_bias, down_bias
+            )
+        ]
         if rows % 32:
+            vector_own = jnp.pad(jnp.concatenate(vectors_own, axis=0), ((0, VEC_LANES - 13), (0, 0))).T
             up_own = lax.dynamic_index_in_dim(
                 up_weight.reshape(rows, shards, GROUP, rows), rep, axis=2, keepdims=False
             ).reshape(rows, D)
-            up_own = jnp.concatenate([up_own, jnp.pad(vector_own, ((0, VEC_LANES - 16), (0, 0))).T], axis=1)
+            up_own = jnp.concatenate([up_own, vector_own], axis=1)
             qkv_own = lax.dynamic_index_in_dim(
                 qkv_weight.reshape(rows, 3, GROUP, QUART), rep, axis=2, keepdims=False
             ).reshape(rows, 3 * QUART)
         else:
-            up_own, qkv_own = run_quarter(up_weight, qkv_weight, vector_own.astype(F32), rep_ref)
+            up_own, qkv_own = run_quarter(up_weight, qkv_weight, vectors_own, rep_ref)
         down_own = lax.dynamic_index_in_dim(
             down_weight.reshape(GROUP, rows, D), rep, axis=0, keepdims=False
         )
@@ -570,7 +609,7 @@
         packs = (token_pack, token_across, token_beside, token_far)
 
         up_lo, up_hi = gather_all(up_own)
-        down_lo, down_hi = gather_all(down_own)
+        down_lo, down_hi = gather_all(down_own, down_order)
         qkv_lo, qkv_hi = gather_all(qkv_own)
 
         proj_part = jnp.where(top_across == across, proj_weight, shard_swap(proj_weight, highest_first[0]))
@@ -592,13 +631,13 @@
         found = jnp.where(found % D // QUART == rep, found // D * QUART + found % QUART, -1)
         bias_place = (jnp.arange(width)[:, None] == found).astype(BF16)
 
-        keep, send, mlp_part, mlp_norm, vectors, mlp_sums = run_mlp(
-            packs, up_lo, up_hi, down_lo, down_hi, to_rel, rep_ref
+        keep, send, mlp_part, mlp_norm, values, vectors, mlp_sums = run_mlp(
+            packs, up_lo, up_hi, down_lo, down_hi, to_rel, rep_ref, down_place
         )
         pair = reduce_all(keep, send)
         keep, send, partial, partial_far = run_attention(
             packs, qkv_lo, qkv_hi, proj_part, to_rel, vectors, mlp_sums, bias_place, head_spread,
-            mlp_part, mlp_norm, rep_ref, rows,
+            mlp_part, mlp_norm, values, rep_ref, rows,
         )
 
         side = width + VEC_LANES

time: 247 us -> 220 us (0.89)
  Pallas kernels: 73 us -> 57.3 us
  waiting for transfers between devices: 105 us -> 97.4 us
  starting transfers between devices: 29.8 us -> 24.6 us
    pallas_call x1, Pallas kernels: 42.1 us -> 25.7 us  [run_attention(): pl.pallas_call(functools.partial(attention_kernel, rows), grid=(GROUP,),...]
    ppermute x18, waiting for transfers between devices: 99.2 us -> 90.7 us  [shard_swap(): return lax.ppermute(value, 'fsdp', [(i, i ^ mask) for i in range(shards)])]
    ppermute x18, starting transfers between devices: 22.5 us -> 19 us  [shard_swap(): return lax.ppermute(value, 'fsdp', [(i, i ^ mask) for i in range(shards)])]
    unnamed x66 -> x54, local copies, waits for them, and re-layouts: 6.73 us -> 6.95 us
  transfers between devices with their start and end apart: 29 -> 29, of which waited for: 12 -> 13; matrix products, arithmetic and copies ran while one was open for 10% -> 12% of each run, Pallas kernels for 11% -> 12%
where the time goes in v1:
time: 220 us; the launch traced here: 219 us
  waiting for transfers between devices  97.4 us (44%)
  Pallas kernels  57.3 us (26%)
  starting transfers between devices  24.6 us (11%)
  other arithmetic  21.8 us (10%)
  local copies, waits for them, and re-layouts  16.5 us (8%)
    ppermute x18, waiting for transfers between devices, shard_swap(): return lax.ppermute(value, 'fsdp', [(i, i ^ mask) for i in range(shards)])  90.7 us
    pallas_call x1, Pallas kernels, run_attention(): pl.pallas_call(functools.partial(attention_kernel, rows), grid=(GROUP,),...  25.7 us
    pallas_call x1, Pallas kernels, run_mlp(): pl.pallas_call(functools.partial(mlp_kernel, down_place), grid=(GROUP,),...  20.6 us
    ppermute x18, starting transfers between devices, shard_swap(): return lax.ppermute(value, 'fsdp', [(i, i ^ mask) for i in range(shards)])  19 us
    unnamed x54, local copies, waits for them, and re-layouts  6.95 us
    ppermute x4, waiting for transfers between devices, x_swap(): return lax.ppermute(value, 'rep', [(i, i ^ 2) for i in range(GROUP)])  6.69 us
    ppermute x4, starting transfers between devices, x_swap(): return lax.ppermute(value, 'rep', [(i, i ^ 2) for i in range(GROUP)])  5.02 us
    pallas_call x1, Pallas kernels, run_finish(): pl.pallas_call(finish_kernel, out_shape=[out, out], compiler_params=PARAM...  4.46 us
  transfers between devices with their start and end apart: 29, of which 13 were waited for; matrix products, arithmetic and copies ran while one was open for 12% of the time, Pallas kernels for 12%

profile of v1, /device:TPU:0, one launch (start us, length us, event | category | flops | bytes accessed | tf_op | source)
XLA Modules:
  0.0 219.3 jit_solution(4396947335834318472)
XLA Ops:
  4.3 3.0 %collective-permute-start = (bf16[528,768]{1,0:T(8,128)(2,1)S(1)}, bf16[528,768]{1,0:T(8,128)(2,1)S(1)}, u32[]{:S(2)}, u32[]{:S(2)}) collective-permute-start(bf16[528,768]{1,0:T(8,128)(2,1)S(1)} %fusion.6.near.pack), channel_id=1, source_target_pairs={{0,2},{1,3},{2,0},{3,1},{4,6},{5,7},{6,4},{7,5},{8,10},{9,11},{10,... | collective-permute-start | bytes 2433032 | tf_op jit(solution)/shard_map/ppermute | solution.py:524
  7.4 1.6 collective-permute-start.12
  10.3 2.3 %quarter.1 = (bf16[96,896]{1,0:T(8,128)(2,1)}, bf16[96,576]{1,0:T(8,128)(2,1)}) custom-call(bf16[1,96]{1,0:T(2,128)(2,1)} %bitcast.46, bf16[1,96]{1,0:T(2,128)(2,1)} %bitcast.47, bf16[1,96]{1,0:T(2,128)(2,1)} %bitcast.48, bf16[1,96]{1,0:T(2,128)(2,1)} %bitcast.49, bf16[3,96]{1,0:T(4,128)(2,1)} %reshape.319.refs_4_, bf16[1,96]{1,0:T(2,128)(2,1)} %bitcast.50, ...), custom_call_target="tpu_custom_call" | custom-call | tf_op jit(solution)/shard_map/quarter/pallas_call | solution.py:496
  12.5 2.6 %collective-permute-start.9 = (bf16[96,896]{1,0:T(8,128)(2,1)}, bf16[96,896]{1,0:T(8,128)(2,1)S(1)}, u32[]{:S(2)}, u32[]{:S(2)}) collective-permute-start(bf16[96,896]{1,0:T(8,128)(2,1)} %get-tuple-element.35), channel_id=1, source_target_pairs={{0,16},{4,20},{8,24},{12,28},{16,0},{20,4},{24,8},{28,12},{1,17},{... | collective-permute-start | bytes 516104 | tf_op jit(solution)/shard_map/ppermute | solution.py:518
  15.5 1.6 constant_dynamic-update-slice_fusion.5
  18.0 2.3 %fusion.place = bf16[576,2304]{1,0:T(8,128)(2,1)} fusion(s32[2304]{0:T(1024)S(1)} %fusion.13), kind=kLoop, calls=%fused_computation.1 | loop fusion | flops 2654208 | bytes 2663424 | tf_op jit(solution)/shard_map/convert_element_type | solution.py:632
  20.3 1.4 fusion.1.spread
  22.8 6.4 %collective-permute-done.3 = bf16[96,576]{1,0:T(8,128)(2,1)} collective-permute-done((bf16[96,576]{1,0:T(8,128)(2,1)}, bf16[96,576]{1,0:T(8,128)(2,1)}, u32[]{:S(2)}, u32[]{:S(2)}) %collective-permute-start.3) | collective-permute-done | bytes 110624 | tf_op jit(solution)/shard_map/ppermute | solution.py:518
  31.1 7.6 %collective-permute-done.6 = bf16[96,768]{1,0:T(8,128)(2,1)S(1)} collective-permute-done((bf16[96,768]{1,0:T(8,128)(2,1)}, bf16[96,768]{1,0:T(8,128)(2,1)S(1)}, u32[]{:S(2)}, u32[]{:S(2)}) %collective-permute-start.6) | collective-permute-done | bytes 147488 | tf_op jit(solution)/shard_map/ppermute | solution.py:518
  39.6 2.1 collective-permute-start.7
  42.8 11.0 %collective-permute-done.7 = bf16[96,768]{1,0:T(8,128)(2,1)S(1)} collective-permute-done((bf16[96,768]{1,0:T(8,128)(2,1)S(1)}, bf16[96,768]{1,0:T(8,128)(2,1)S(1)}, u32[]{:S(2)}, u32[]{:S(2)}) %collective-permute-start.7) | collective-permute-done | bytes 147488 | tf_op jit(solution)/shard_map/ppermute | solution.py:518
  53.9 3.7 %collective-permute-done.10 = bf16[192,896]{1,0:T(8,128)(2,1)S(1)} collective-permute-done((bf16[192,896]{1,0:T(8,128)(2,1)S(1)}, bf16[192,896]{1,0:T(8,128)(2,1)S(1)}, u32[]{:S(2)}, u32[]{:S(2)}) %collective-permute-start.10) | collective-permute-done | bytes 344096 | tf_op jit(solution)/shard_map/ppermute | solution.py:518
  58.1 7.3 %collective-permute-done.13 = bf16[192,768]{1,0:T(8,128)(2,1)S(1)} collective-permute-done((bf16[192,768]{1,0:T(8,128)(2,1)S(1)}, bf16[192,768]{1,0:T(8,128)(2,1)S(1)}, u32[]{:S(2)}, u32[]{:S(2)}) %collective-permute-start.13) | collective-permute-done | bytes 294944 | tf_op jit(solution)/shard_map/ppermute | solution.py:518
  67.0 1.6 collective-permute-start.5
  69.3 1.4 fusion.3.to_rel
  71.5 6.5 %collective-permute-done.14.down_hi = bf16[384,768]{1,0:T(8,128)(2,1)S(1)} collective-permute-done((bf16[384,768]{1,0:T(8,128)(2,1)S(1)}, bf16[384,768]{1,0:T(8,128)(2,1)S(1)}, u32[]{:S(2)}, u32[]{:S(2)}) %collective-permute-start.14) | collective-permute-done | bytes 589856 | tf_op jit(solution)/shard_map/ppermute | solution.py:518
  77.9 4.8 %collective-permute-done.11.up_hi = bf16[384,896]{1,0:T(8,128)(2,1)S(1)} collective-permute-done((bf16[384,896]{1,0:T(8,128)(2,1)S(1)}, bf16[384,896]{1,0:T(8,128)(2,1)S(1)}, u32[]{:S(2)}, u32[]{:S(2)}) %collective-permute-start.11) | collective-permute-done | bytes 688160 | tf_op jit(solution)/shard_map/ppermute | solution.py:518
  83.6 20.6 %mlp.1 = (bf16[384,1536]{1,0:T(8,128)(2,1)}, bf16[384,1536]{1,0:T(8,128)(2,1)}, f32[4,256,768]{2,1,0:T(8,128)}, f32[4,256,768]{2,1,0:T(8,128)}, bf16[4,256,768]{...) custom-call(bf16[528,768]{1,0:T(8,128)(2,1)} %copy-done.1, bf16[528,768]{1,0:T(8,128)(2,1)} %copy-done.2, ...), custom_call_target="tpu_custom_call" | custom-call | tf_op jit(solution)/shard_map/mlp/pallas_call | solution.py:280
  104.3 25.7 %attention.1 = (bf16[384,896]{1,0:T(8,128)(2,1)}, bf16[384,896]{1,0:T(8,128)(2,1)}, bf16[2,256,1536]{2,1,0:T(8,128)(2,1)}, bf16[2,256,1536]{2,1,0:T(8,128)(2,1)}) custom-call(bf16[528,768]{1,0:T(8,128)(2,1)} %copy-done.1, bf16[528,768]{1,0:T(8,128)(2,1)} %copy-done.2, bf16[528,768]{1,0:T(8,128)(2,1)} %copy-done.3, ...), custom_call_target="tpu_custom_call" | custom-call | tf_op jit(solution)/shard_map/attention/pallas_call | solution.py:331
  130.5 11.2 %collective-permute-done.23 = bf16[384,896]{1,0:T(8,128)(2,1)S(1)} collective-permute-done((bf16[384,896]{1,0:T(8,128)(2,1)}, bf16[384,896]{1,0:T(8,128)(2,1)S(1)}, u32[]{:S(2)}, u32[]{:S(2)}) %collective-permute-start.23) | collective-permute-done | bytes 688160 | tf_op jit(solution)/shard_map/ppermute | solution.py:518
  145.9 6.7 %collective-permute-done.24 = bf16[192,1088]{1,0:T(8,128)(2,1)} collective-permute-done((bf16[192,1088]{1,0:T(8,128)(2,1)}, bf16[192,1088]{1,0:T(8,128)(2,1)}, u32[]{:S(2)}, u32[]{:S(2)}) %collective-permute-start.24) | collective-permute-done | bytes 417824 | tf_op jit(solution)/shard_map/ppermute | solution.py:518
  155.1 2.1 collective-permute-start.25
  157.2 9.3 %collective-permute-done.17 = bf16[384,1536]{1,0:T(8,128)(2,1)} collective-permute-done((bf16[384,1536]{1,0:T(8,128)(2,1)}, bf16[384,1536]{1,0:T(8,128)(2,1)}, u32[]{:S(2)}, u32[]{:S(2)}) %collective-permute-start.17) | collective-permute-done | bytes 1179680 | tf_op jit(solution)/shard_map/ppermute | solution.py:518
  166.6 1.9 add_convert_fusion
  170.4 10.2 %collective-permute-done.18 = bf16[192,1536]{1,0:T(8,128)(2,1)S(1)} collective-permute-done((bf16[192,1536]{1,0:T(8,128)(2,1)S(1)}, bf16[192,1536]{1,0:T(8,128)(2,1)S(1)}, u32[]{:S(2)}, u32[]{:S(2)}) %collective-permute-start.18) | collective-permute-done | bytes 589856 | tf_op jit(solution)/shard_map/ppermute | solution.py:518
  180.8 6.3 %collective-permute-start.19 = (bf16[96,1536]{1,0:T(8,128)(2,1)S(1)}, bf16[96,1536]{1,0:T(8,128)(2,1)S(1)}, u32[]{:S(2)}, u32[]{:S(2)}) collective-permute-start(bf16[96,1536]{1,0:T(8,128)(2,1)S(1)} %slice.129), channel_id=1, source_target_pairs={{0,16},{4,20},{8,24},{12,28},{16,0},{20,4},{24,8},{28,12},{1,17},{... | collective-permute-start | bytes 884744 | tf_op jit(solution)/shard_map/ppermute | solution.py:518
  187.8 6.1 %collective-permute-done.19 = bf16[96,1536]{1,0:T(8,128)(2,1)S(1)} collective-permute-done((bf16[96,1536]{1,0:T(8,128)(2,1)S(1)}, bf16[96,1536]{1,0:T(8,128)(2,1)S(1)}, u32[]{:S(2)}, u32[]{:S(2)}) %collective-permute-start.19) | collective-permute-done | bytes 294944 | tf_op jit(solution)/shard_map/ppermute | solution.py:518
  196.3 6.7 %collective-permute-done.20.refs_1_ = bf16[96,1536]{1,0:T(8,128)(2,1)S(1)} collective-permute-done((bf16[96,1536]{1,0:T(8,128)(2,1)S(1)}, bf16[96,1536]{1,0:T(8,128)(2,1)S(1)}, u32[]{:S(2)}, u32[]{:S(2)}) %collective-permute-start.20) | collective-permute-done | bytes 294944 | tf_op jit(solution)/shard_map/ppermute | solution.py:524
  203.0 1.3 slice_bitcast_fusion.near
  205.2 4.5 %finish.1 = (bf16[256,768]{1,0:T(8,128)(2,1)}, bf16[256,768]{1,0:T(8,128)(2,1)}) custom-call(bf16[528,768]{1,0:T(8,128)(2,1)} %copy-done.1, f32[256,1536]{1,0:T(8,128)} %slice_bitcast_fusion.near, bf16[256,1536]{1,0:T(8,128)(2,1)} %copy-done.10, bf16[768,768]{1,0:T(8,128)(2,1)} %fusion.3.to_rel, f32[1,768]{1,0:T(1,128)} %slice_add_fusion.out_bias, ...), custom_call_target="tpu_custom_call" | custom-call | tf_op jit(solution)/shard_map/finish/pallas_call | solution.py:400
  210.4 4.2 %assemble.1 = (f32[96,2304]{1,0:T(8,128)}, f32[96,768]{1,0:T(8,128)}, f32[96,3072]{1,0:T(8,128)}, f32[384,768]{1,0:T(8,128)}, f32[16,96]{1,0:T(8,128)}) custom-call(bf16[96,1536]{1,0:T(8,128)(2,1)} %copy-done.7, bf16[96,1536]{1,0:T(8,128)(2,1)} %copy-done.16, bf16[96,1536]{1,0:T(8,128)(2,1)} %collective-permute-done.21.refs_2_, ...), custom_call_target="tpu_custom_call" | custom-call | tf_op jit(solution)/shard_map/assemble/pallas_call | solution.py:440
  216.0 1.4 slice_bitcast_fusion.1
  (150 shorter events, 32.7 us)
Async XLA Ops:
  4.3 53.8 %collective-permute-start = (bf16[528,768]{1,0:T(8,128)(2,1)S(1)}, bf16[528,768]{1,0:T(8,128)(2,1)S(1)}, u32[]{:S(2)}, u32[]{:S(2)}) collective-permute-start(bf16[528,768]{1,0:T(8,128)(2,1)S(1)} %fusion.6.near.pack), channel_id=1, source_target_pairs={{0,2},{1,3},{2,0},{3,1},{4,6},{5,7},{6,4},{7,5},{8,10},{9,11},{10,... | collective-permute-start | bytes 2433032 | tf_op jit(solution)/shard_map/ppermute | solution.py:524
  7.4 64.1 %collective-permute-start.1 = (bf16[528,768]{1,0:T(8,128)(2,1)S(1)}, bf16[528,768]{1,0:T(8,128)(2,1)S(1)}, u32[]{:S(2)}, u32[]{:S(2)}) collective-permute-start(bf16[528,768]{1,0:T(8,128)(2,1)S(1)} %fusion.6.near.pack), channel_id=1, source_target_pairs={{0,1},{1,0},{2,3},{3,2},{4,5},{5,4},{6,7},{7,6},{8,9},{9,8},{10,11... | collective-permute-start | bytes 2433032 | tf_op jit(solution)/shard_map/ppermute | solution.py:521
  7.4 32.3 %collective-permute-start.12 = (bf16[96,768]{1,0:T(8,128)(2,1)S(1)}, bf16[96,768]{1,0:T(8,128)(2,1)}, u32[]{:S(2)}, u32[]{:S(2)}) collective-permute-start(bf16[96,768]{1,0:T(8,128)(2,1)S(1)} %dynamic-slice_bitcast_fusion), channel_id=1, source_target_pairs={{0,4},{4,0},{8,12},{12,8},{16,20},{20,16},{24,28},{28,24},{1,5},{5... | collective-permute-start | bytes 442376 | tf_op jit(solution)/shard_map/ppermute | solution.py:518
  12.5 30.1 %collective-permute-start.9 = (bf16[96,896]{1,0:T(8,128)(2,1)}, bf16[96,896]{1,0:T(8,128)(2,1)S(1)}, u32[]{:S(2)}, u32[]{:S(2)}) collective-permute-start(bf16[96,896]{1,0:T(8,128)(2,1)} %get-tuple-element.35), channel_id=1, source_target_pairs={{0,16},{4,20},{8,24},{12,28},{16,0},{20,4},{24,8},{28,12},{1,17},{... | collective-permute-start | bytes 516104 | tf_op jit(solution)/shard_map/ppermute | solution.py:518
  15.1 14.1 %collective-permute-start.3 = (bf16[96,576]{1,0:T(8,128)(2,1)}, bf16[96,576]{1,0:T(8,128)(2,1)}, u32[]{:S(2)}, u32[]{:S(2)}) collective-permute-start(bf16[96,576]{1,0:T(8,128)(2,1)} %get-tuple-element.34), channel_id=1, source_target_pairs={{0,16},{4,20},{8,24},{12,28},{16,0},{20,4},{24,8},{28,12},{1,17},{... | collective-permute-start | bytes 331784 | tf_op jit(solution)/shard_map/ppermute | solution.py:518
  20.3 22.4 %copy-start.12 = (bf16[96,896]{1,0:T(8,128)(2,1)S(1)}, bf16[96,896]{1,0:T(8,128)(2,1)}, u32[]{:S(2)}) copy-start(bf16[96,896]{1,0:T(8,128)(2,1)} %get-tuple-element.35) | copy-start | bytes 516100
  29.2 9.5 %collective-permute-start.6 = (bf16[96,768]{1,0:T(8,128)(2,1)}, bf16[96,768]{1,0:T(8,128)(2,1)S(1)}, u32[]{:S(2)}, u32[]{:S(2)}) collective-permute-start(bf16[96,768]{1,0:T(8,128)(2,1)} %param.30), channel_id=1, source_target_pairs={{0,16},{4,20},{8,24},{12,28},{16,0},{20,4},{24,8},{28,12},{1,17},{... | collective-permute-start | bytes 442376 | tf_op jit(solution)/shard_map/ppermute | solution.py:518
  38.7 28.2 %collective-permute-start.4 = (bf16[192,576]{1,0:T(8,128)(2,1)S(1)}, bf16[192,576]{1,0:T(8,128)(2,1)S(1)}, u32[]{:S(2)}, u32[]{:S(2)}) collective-permute-start(bf16[192,576]{1,0:T(8,128)(2,1)S(1)} %pad_maximum_fusion.4), channel_id=1, source_target_pairs={{0,8},{4,12},{8,0},{12,4},{16,24},{20,28},{24,16},{28,20},{1,9},{5... | collective-permute-start | bytes 663560 | tf_op jit(solution)/shard_map/ppermute | solution.py:518
  39.6 14.2 %collective-permute-start.7 = (bf16[96,768]{1,0:T(8,128)(2,1)S(1)}, bf16[96,768]{1,0:T(8,128)(2,1)S(1)}, u32[]{:S(2)}, u32[]{:S(2)}) collective-permute-start(bf16[96,768]{1,0:T(8,128)(2,1)S(1)} %broadcast_select_fusion), channel_id=1, source_target_pairs={{0,8},{4,12},{8,0},{12,4},{16,24},{20,28},{24,16},{28,20},{1,9},{5... | collective-permute-start | bytes 442376 | tf_op jit(solution)/shard_map/ppermute | solution.py:518
  42.7 14.9 %collective-permute-start.10 = (bf16[192,896]{1,0:T(8,128)(2,1)S(1)}, bf16[192,896]{1,0:T(8,128)(2,1)S(1)}, u32[]{:S(2)}, u32[]{:S(2)}) collective-permute-start(bf16[192,896]{1,0:T(8,128)(2,1)S(1)} %pad_maximum_fusion.1), channel_id=1, source_target_pairs={{0,8},{4,12},{8,0},{12,4},{16,24},{20,28},{24,16},{28,20},{1,9},{5... | collective-permute-start | bytes 1032200 | tf_op jit(solution)/shard_map/ppermute | solution.py:518
  53.8 11.6 %collective-permute-start.13 = (bf16[192,768]{1,0:T(8,128)(2,1)S(1)}, bf16[192,768]{1,0:T(8,128)(2,1)S(1)}, u32[]{:S(2)}, u32[]{:S(2)}) collective-permute-start(bf16[192,768]{1,0:T(8,128)(2,1)S(1)} %pad_maximum_fusion.3), channel_id=1, source_target_pairs={{0,16},{4,20},{8,24},{12,28},{16,0},{20,4},{24,8},{28,12},{1,17},{... | collective-permute-start | bytes 884744 | tf_op jit(solution)/shard_map/ppermute | solution.py:518
  57.6 9.4 %collective-permute-start.8 = (bf16[96,768]{1,0:T(8,128)(2,1)S(1)}, bf16[96,768]{1,0:T(8,128)(2,1)S(1)}, u32[]{:S(2)}, u32[]{:S(2)}) collective-permute-start(bf16[96,768]{1,0:T(8,128)(2,1)S(1)} %broadcast_select_fusion.1), channel_id=1, source_target_pairs={{0,4},{4,0},{8,12},{12,8},{16,20},{20,16},{24,28},{28,24},{1,5},{5... | collective-permute-start | bytes 442376 | tf_op jit(solution)/shard_map/ppermute | solution.py:518
  58.1 25.5 %collective-permute-start.2 = (bf16[528,768]{1,0:T(8,128)(2,1)S(1)}, bf16[528,768]{1,0:T(8,128)(2,1)}, u32[]{:S(2)}, u32[]{:S(2)}) collective-permute-start(bf16[528,768]{1,0:T(8,128)(2,1)S(1)} %collective-permute-done.across), channel_id=1, source_target_pairs={{0,1},{1,0},{2,3},{3,2},{4,5},{5,4},{6,7},{7,6},{8,9},{9,8},{10,11... | collective-permute-start | bytes 2433032 | tf_op jit(solution)/shard_map/ppermute | solution.py:521
  65.4 17.3 %collective-permute-start.11 = (bf16[384,896]{1,0:T(8,128)(2,1)S(1)}, bf16[384,896]{1,0:T(8,128)(2,1)S(1)}, u32[]{:S(2)}, u32[]{:S(2)}) collective-permute-start(bf16[384,896]{1,0:T(8,128)(2,1)S(1)} %constant_dynamic-update-slice_fusion.3.up_lo), channel_id=1, source_target_pairs={{0,4},{4,0},{8,12},{12,8},{16,20},{20,16},{24,28},{28,24},{1,5},{5... | collective-permute-start | bytes 2064392 | tf_op jit(solution)/shard_map/ppermute | solution.py:518
  66.9 11.1 %collective-permute-start.14 = (bf16[384,768]{1,0:T(8,128)(2,1)S(1)}, bf16[384,768]{1,0:T(8,128)(2,1)S(1)}, u32[]{:S(2)}, u32[]{:S(2)}) collective-permute-start(bf16[384,768]{1,0:T(8,128)(2,1)S(1)} %pad_maximum_fusion.down_lo), channel_id=1, source_target_pairs={{0,8},{4,12},{8,0},{12,4},{16,24},{20,28},{24,16},{28,20},{1,9},{5... | collective-permute-start | bytes 1769480 | tf_op jit(solution)/shard_map/ppermute | solution.py:518
  67.0 37.3 %copy-start.11 = (bf16[384,576]{1,0:T(8,128)(2,1)}, bf16[384,576]{1,0:T(8,128)(2,1)S(1)}, u32[]{:S(2)}) copy-start(bf16[384,576]{1,0:T(8,128)(2,1)S(1)} %constant_dynamic-update-slice_fusion.qkv_lo) | copy-start | bytes 1327108
  67.0 37.3 %collective-permute-start.5 = (bf16[384,576]{1,0:T(8,128)(2,1)S(1)}, bf16[384,576]{1,0:T(8,128)(2,1)}, u32[]{:S(2)}, u32[]{:S(2)}) collective-permute-start(bf16[384,576]{1,0:T(8,128)(2,1)S(1)} %constant_dynamic-update-slice_fusion.qkv_lo), channel_id=1, source_target_pairs={{0,4},{4,0},{8,12},{12,8},{16,20},{20,16},{24,28},{28,24},{1,5},{5... | collective-permute-start | bytes 1327112 | tf_op jit(solution)/shard_map/ppermute | solution.py:518
  130.0 11.7 %collective-permute-start.23 = (bf16[384,896]{1,0:T(8,128)(2,1)}, bf16[384,896]{1,0:T(8,128)(2,1)S(1)}, u32[]{:S(2)}, u32[]{:S(2)}) collective-permute-start(bf16[384,896]{1,0:T(8,128)(2,1)} %get-tuple-element.48), channel_id=1, source_target_pairs={{0,4},{4,0},{8,12},{12,8},{16,20},{20,16},{24,28},{28,24},{1,5},{5... | collective-permute-start | bytes 2064392 | tf_op jit(solution)/shard_map/ppermute | solution.py:518
  144.0 8.6 %collective-permute-start.24 = (bf16[192,1088]{1,0:T(8,128)(2,1)}, bf16[192,1088]{1,0:T(8,128)(2,1)}, u32[]{:S(2)}, u32[]{:S(2)}) collective-permute-start(bf16[192,1088]{1,0:T(8,128)(2,1)} %concatenate.52), channel_id=1, source_target_pairs={{0,8},{4,12},{8,0},{12,4},{16,24},{20,28},{24,16},{28,20},{1,9},{5... | collective-permute-start | bytes 1253384 | tf_op jit(solution)/shard_map/ppermute | solution.py:518
  144.0 22.6 %collective-permute-start.17 = (bf16[384,1536]{1,0:T(8,128)(2,1)}, bf16[384,1536]{1,0:T(8,128)(2,1)}, u32[]{:S(2)}, u32[]{:S(2)}) collective-permute-start(bf16[384,1536]{1,0:T(8,128)(2,1)} %get-tuple-element.46), channel_id=1, source_target_pairs={{0,4},{4,0},{8,12},{12,8},{16,20},{20,16},{24,28},{28,24},{1,5},{5... | collective-permute-start | bytes 3538952 | tf_op jit(solution)/shard_map/ppermute | solution.py:518
  145.9 23.7 %collective-permute-start.15 = (bf16[2,256,1536]{2,1,0:T(8,128)(2,1)}, bf16[2,256,1536]{2,1,0:T(8,128)(2,1)S(1)}, u32[]{:S(2)}, u32[]{:S(2)}) collective-permute-start(bf16[2,256,1536]{2,1,0:T(8,128)(2,1)} %get-tuple-element.42), channel_id=1, source_target_pairs={{0,1},{1,0},{2,3},{3,2},{4,5},{5,4},{6,7},{7,6},{8,9},{9,8},{10,11... | collective-permute-start | bytes 4718600 | tf_op jit(solution)/shard_map/ppermute | solution.py:521
  155.1 13.7 %collective-permute-start.25 = (bf16[96,1472]{1,0:T(8,128)(2,1)S(1)}, bf16[96,1472]{1,0:T(8,128)(2,1)S(1)}, u32[]{:S(2)}, u32[]{:S(2)}) collective-permute-start(bf16[96,1472]{1,0:T(8,128)(2,1)S(1)} %concatenate.55), channel_id=1, source_target_pairs={{0,16},{4,20},{8,24},{12,28},{16,0},{20,4},{24,8},{28,12},{1,17},{... | collective-permute-start | bytes 847880 | tf_op jit(solution)/shard_map/ppermute | solution.py:518
  168.5 12.1 %collective-permute-start.18 = (bf16[192,1536]{1,0:T(8,128)(2,1)S(1)}, bf16[192,1536]{1,0:T(8,128)(2,1)S(1)}, u32[]{:S(2)}, u32[]{:S(2)}) collective-permute-start(bf16[192,1536]{1,0:T(8,128)(2,1)S(1)} %slice.127), channel_id=1, source_target_pairs={{0,8},{4,12},{8,0},{12,4},{16,24},{20,28},{24,16},{28,20},{1,9},{5... | collective-permute-start | bytes 1769480 | tf_op jit(solution)/shard_map/ppermute | solution.py:518
  168.8 26.9 %copy-start.6 = (bf16[96,1472]{1,0:T(8,128)(2,1)}, bf16[96,1472]{1,0:T(8,128)(2,1)S(1)}, u32[]{:S(2)}) copy-start(bf16[96,1472]{1,0:T(8,128)(2,1)S(1)} %add_convert_fusion.3.refs_4_) | copy-start | bytes 847876
  168.8 26.9 %collective-permute-start.26 = (bf16[96,1472]{1,0:T(8,128)(2,1)S(1)}, bf16[96,1472]{1,0:T(8,128)(2,1)S(1)}, u32[]{:S(2)}, u32[]{:S(2)}) collective-permute-start(bf16[96,1472]{1,0:T(8,128)(2,1)S(1)} %add_convert_fusion.3.refs_4_), channel_id=1, source_target_pairs={{0,2},{1,3},{2,0},{3,1},{4,6},{5,7},{6,4},{7,5},{8,10},{9,11},{10,... | collective-permute-start | bytes 847880 | tf_op jit(solution)/shard_map/ppermute | solution.py:524
  180.8 13.1 %collective-permute-start.19 = (bf16[96,1536]{1,0:T(8,128)(2,1)S(1)}, bf16[96,1536]{1,0:T(8,128)(2,1)S(1)}, u32[]{:S(2)}, u32[]{:S(2)}) collective-permute-start(bf16[96,1536]{1,0:T(8,128)(2,1)S(1)} %slice.129), channel_id=1, source_target_pairs={{0,16},{4,20},{8,24},{12,28},{16,0},{20,4},{24,8},{28,12},{1,17},{... | collective-permute-start | bytes 884744 | tf_op jit(solution)/shard_map/ppermute | solution.py:518
  187.2 17.2 %collective-permute-start.16 = (bf16[256,1536]{1,0:T(8,128)(2,1)S(1)}, bf16[256,1536]{1,0:T(8,128)(2,1)S(1)}, u32[]{:S(2)}, u32[]{:S(2)}) collective-permute-start(bf16[256,1536]{1,0:T(8,128)(2,1)S(1)} %fusion.7), channel_id=1, source_target_pairs={{0,2},{1,3},{2,0},{3,1},{4,6},{5,7},{6,4},{7,5},{8,10},{9,11},{10,... | collective-permute-start | bytes 2359304 | tf_op jit(solution)/shard_map/ppermute | solution.py:524
  194.0 9.0 %collective-permute-start.20 = (bf16[96,1536]{1,0:T(8,128)(2,1)S(1)}, bf16[96,1536]{1,0:T(8,128)(2,1)S(1)}, u32[]{:S(2)}, u32[]{:S(2)}) collective-permute-start(bf16[96,1536]{1,0:T(8,128)(2,1)S(1)} %add_convert_fusion.5.refs_0_), channel_id=1, source_target_pairs={{0,2},{1,3},{2,0},{3,1},{4,6},{5,7},{6,4},{7,5},{8,10},{9,11},{10,... | collective-permute-start | bytes 884744 | tf_op jit(solution)/shard_map/ppermute | solution.py:524
  195.8 14.0 %collective-permute-start.27 = (bf16[96,1472]{1,0:T(8,128)(2,1)S(1)}, bf16[96,1472]{1,0:T(8,128)(2,1)S(1)}, u32[]{:S(2)}, u32[]{:S(2)}) collective-permute-start(bf16[96,1472]{1,0:T(8,128)(2,1)S(1)} %add_convert_fusion.3.refs_4_), channel_id=1, source_target_pairs={{0,1},{1,0},{2,3},{3,2},{4,5},{5,4},{6,7},{7,6},{8,9},{9,8},{10,11... | collective-permute-start | bytes 847880 | tf_op jit(solution)/shard_map/ppermute | solution.py:521
  195.8 13.9 %collective-permute-start.28 = (bf16[96,1472]{1,0:T(8,128)(2,1)S(1)}, bf16[96,1472]{1,0:T(8,128)(2,1)}, u32[]{:S(2)}, u32[]{:S(2)}) collective-permute-start(bf16[96,1472]{1,0:T(8,128)(2,1)S(1)} %collective-permute-done.26.refs_5_), channel_id=1, source_target_pairs={{0,1},{1,0},{2,3},{3,2},{4,5},{5,4},{6,7},{7,6},{8,9},{9,8},{10,11... | collective-permute-start | bytes 847880 | tf_op jit(solution)/shard_map/ppermute | solution.py:521
  196.3 13.5 %collective-permute-start.21 = (bf16[96,1536]{1,0:T(8,128)(2,1)S(1)}, bf16[96,1536]{1,0:T(8,128)(2,1)}, u32[]{:S(2)}, u32[]{:S(2)}) collective-permute-start(bf16[96,1536]{1,0:T(8,128)(2,1)S(1)} %add_convert_fusion.5.refs_0_), channel_id=1, source_target_pairs={{0,1},{1,0},{2,3},{3,2},{4,5},{5,4},{6,7},{7,6},{8,9},{9,8},{10,11... | collective-permute-start | bytes 884744 | tf_op jit(solution)/shard_map/ppermute | solution.py:521
  203.0 6.7 %collective-permute-start.22 = (bf16[96,1536]{1,0:T(8,128)(2,1)S(1)}, bf16[96,1536]{1,0:T(8,128)(2,1)}, u32[]{:S(2)}, u32[]{:S(2)}) collective-permute-start(bf16[96,1536]{1,0:T(8,128)(2,1)S(1)} %collective-permute-done.20.refs_1_), channel_id=1, source_target_pairs={{0,1},{1,0},{2,3},{3,2},{4,5},{5,4},{6,7},{7,6},{8,9},{9,8},{10,11... | collective-permute-start | bytes 884744 | tf_op jit(solution)/shard_map/ppermute | solution.py:521
  (21 other events, 166.4 us)

commit v2 on v1

--- a/solution.py
+++ b/solution.py
@@ -56,11 +56,15 @@
     return value
 
 
-def mlp_kernel(
+def hot(rows, columns):
+    return jnp.where(rows == columns, 1.0, 0.0).astype(BF16)
+
+
+def mlp_forward_kernel(
     down_place,
-    near, across, beside, far, up_lo, up_hi, down_lo, down_hi, to_rel, rep,
-    keep, send, out_part, grad_norm, values_out, vectors_out, sums,
-    up_rel, down_rel, down_acc, up_acc,
+    near, across, beside, far, up_lo, up_hi, natural, rep,
+    keep, send, slope_out, act_out, unit_out, grad_out_ref, vectors_out, up_rel, to_rel,
+    down_acc,
 ):
     step = pl.program_id(0)
     packs = (near, across, beside, far)
@@ -69,41 +73,65 @@
 
     @pl.when(step == 0)
     def _():
+        to_rel[...] = hot(lax.broadcasted_iota(jnp.int32, (D, D), 0), natural[...])
         up_rel[:half] = dot(up_lo[:, :D], to_rel[...]).astype(BF16)
         up_rel[half:] = dot(up_hi[:, :D], to_rel[...]).astype(BF16)
-        block = D // len(down_place)
-        if down_place == sorted(down_place):
-            down_rel[:half] = down_lo[...]
-            down_rel[half:] = down_hi[...]
-        else:
-            for source, target in enumerate(down_place):
-                piece = down_hi if source * block >= half else down_lo
-                start = source * block % half
-                down_rel[target * block : (target + 1) * block] = piece[start : start + block]
         vectors_out[:, :half] = up_lo[:, D:].astype(F32).T[:16]
         vectors_out[:, half:] = up_hi[:, D:].astype(F32).T[:16]
         down_acc[...] = jnp.zeros_like(down_acc)
-        up_acc[...] = jnp.zeros_like(up_acc)
-        sums[...] = jnp.zeros_like(sums)
 
     inputs = take(step, packs, slice(0, own))
-    grad_out = take(step, packs, slice(own, 2 * own))
-    values = dot(inputs, to_rel[...])
-    values_out[0] = values.astype(BF16)
-    normed, unit = layer_norm(values, vectors_out[2:3], vectors_out[3:4])
+    rest = take(step, packs, slice(own, 2 * own + 16))
+    grad_out_ref[0] = rest
+    grad_out = rest[:own]
+    normed, unit = layer_norm(dot(inputs, to_rel[...]), vectors_out[2:3], vectors_out[3:4])
+    unit_out[0] = unit
     bias = vectors_out[11:12]
     for quarter in range(GROUP - 1):
         bias = jnp.where(rep[0] == quarter, vectors_out[8 + quarter : 9 + quarter], bias)
     pre_act = dot(normed, up_rel[...]) + bias
     phi = 0.5 * (1.0 + lax.erf(pre_act * 0.7071067811865476))
     activ = (pre_act * phi).astype(BF16)
-    slope = phi + pre_act * jnp.exp(-0.5 * pre_act * pre_act) * 0.3989422804014327
+    slope_out[0] = phi + pre_act * jnp.exp(-0.5 * pre_act * pre_act) * 0.3989422804014327
+    act_out[0] = activ
     down_acc[...] += t_dot(activ, grad_out)
-    grad_pre = dot_t(grad_out, down_rel[...]) * slope
+
+    @pl.when(step == pl.num_programs(0) - 1)
+    def _():
+        if down_place == sorted(down_place):
+            keep[...] = down_acc[:half].astype(BF16)
+            send[...] = down_acc[half:].astype(BF16)
+        else:
+            block = D // len(down_place)
+            for target, source in enumerate(down_place):
+                piece = send if target * block >= half else keep
+                start = target * block % half
+                piece[start : start + block] = down_acc[source * block : (source + 1) * block].astype(BF16)
+
+
+def mlp_backward_kernel(
+    cotangents, down_lo, down_hi, up_rel, to_rel, slope, act, unit_ref, vectors,
+    keep, send, out_part, grad_norm, sums,
+    down_rel, up_acc,
+):
+    step = pl.program_id(0)
+    half = D // 2
+
+    @pl.when(step == 0)
+    def _():
+        down_rel[:half] = down_lo[...]
+        down_rel[half:] = down_hi[...]
+        up_acc[...] = jnp.zeros_like(up_acc)
+        sums[...] = jnp.zeros_like(sums)
+
+    unit = unit_ref[0]
+    grad_out = cotangents[0, : unit.shape[0]]
+    normed = (unit * vectors[2:3] + vectors[3:4]).astype(BF16)
+    grad_pre = dot_t(grad_out, down_rel[...]) * slope[0]
     grad_pre_b = grad_pre.astype(BF16)
     up_acc[...] += t_dot(normed, grad_pre_b)
     gn = dot_t(grad_pre_b, up_rel[...])
-    out_part[0] = dot(activ, down_rel[...])
+    out_part[0] = dot(act[0], down_rel[...])
     grad_norm[0] = gn
     sums[0:1] += jnp.sum(gn * unit, axis=0, keepdims=True)
     sums[1:2] += jnp.sum(gn, axis=0, keepdims=True)
@@ -111,27 +139,29 @@
 
     @pl.when(step == pl.num_programs(0) - 1)
     def _():
-        keep[:, :D] = down_acc[:half].astype(BF16)
-        send[:, :D] = down_acc[half:].astype(BF16)
-        keep[:, D:] = dot_t(up_acc[:half].astype(BF16), to_rel[...]).astype(BF16)
-        send[:, D:] = dot_t(up_acc[half:].astype(BF16), to_rel[...]).astype(BF16)
+        keep[...] = dot_t(up_acc[:half].astype(BF16), to_rel[...]).astype(BF16)
+        send[...] = dot_t(up_acc[half:].astype(BF16), to_rel[...]).astype(BF16)
 
 
 def attention_kernel(
     block_rows,
-    near, across, beside, far, qkv_lo, qkv_hi, proj, to_rel, vectors, mlp_sums, place, spread, head_spread,
+    cotangents, qkv_lo, qkv_hi, proj, to_rel, vectors, mlp_sums, found, source, head_natural,
     cosines, sines, mlp_part, mlp_norm, values, rep,
     keep, send, partial_near, partial_far,
-    wide, proj_wide, bias_wide, qkv_rel, qkv_acc, proj_acc, gp_ref, ctx_ref, sums, bias_sums,
+    wide, proj_wide, bias_wide, qkv_rel, qkv_acc, proj_acc, gp_ref, ctx_ref, sums, bias_sums, place, spread, head_spread,
 ):
     step = pl.program_id(0)
-    packs = (near, across, beside, far)
     half = D // 2
-    own = (near.shape[0] - 16) // 2
-    count = 2 * own
+    own = cotangents.shape[1] - 16
 
     @pl.when(step == 0)
     def _():
+        width = 3 * QUART
+        place[...] = hot(lax.broadcasted_iota(jnp.int32, (width, 3 * D), 0), found[...])
+        spread[...] = hot(lax.broadcasted_iota(jnp.int32, (width, 3 * EXT), 0), source[...])
+        padded = lax.broadcasted_iota(jnp.int32, (EXT, QUART), 0)
+        padded = jnp.where(padded % LANES < HDIM, padded // LANES * HDIM + padded % LANES, -1)
+        head_spread[...] = hot(padded, head_natural[...])
         qkv_rel[:half] = qkv_lo[...]
         qkv_rel[half:] = qkv_hi[...]
         wide[:half] = dot(qkv_lo[...], spread[...]).astype(BF16)
@@ -146,9 +176,10 @@
         sums[...] = jnp.zeros_like(sums)
         bias_sums[...] = jnp.zeros_like(bias_sums)
 
-    grad_out = take(step, packs, slice(own, count))
-    segment_row = take(step, packs, slice(count, count + 16)).astype(F32)
-    normed, unit = layer_norm(values[0].astype(F32), vectors[0:1], vectors[1:2])
+    grad_out = cotangents[0, :own]
+    segment_row = cotangents[0, own:].astype(F32)
+    unit = values[0]
+    normed = (unit * vectors[0:1] + vectors[1:2]).astype(BF16)
     projected = dot(normed, wide[...]) + bias_wide[0:1]
     grad_context = dot_t(grad_out, proj_wide[...]).astype(BF16)
     lane = lax.broadcasted_iota(jnp.int32, (LANES, LANES), 1)
@@ -270,38 +301,57 @@
     return pl.BlockSpec(memory_space=pltpu.SMEM)
 
 
-def run_mlp(packs, up_lo, up_hi, down_lo, down_hi, to_rel, rep, down_place):
+def run_mlp_forward(packs, up_lo, up_hi, natural, rep, down_place):
     packed = packs[0].shape[0]
     own = (packed - 16) // 2
     half = D // 2
     wide = D + VEC_LANES
-    grad = jax.ShapeDtypeStruct((half, 2 * D), BF16)
+    grad = jax.ShapeDtypeStruct((half, D), BF16)
+    return pl.pallas_call(
+        functools.partial(mlp_forward_kernel, down_place),
+        grid=(GROUP,),
+        in_specs=[whole(packed, D)] * 4 + [whole(half, wide), whole(half, wide), whole(1, D), smem()],
+        out_specs=[whole(half, D)] * 2
+        + [token_block(own, D)] * 3
+        + [token_block(own + 16, D), whole(16, D), whole(D, D), whole(D, D)],
+        out_shape=[
+            grad,
+            grad,
+            jax.ShapeDtypeStruct((GROUP, own, D), F32),
+            jax.ShapeDtypeStruct((GROUP, own, D), BF16),
+            jax.ShapeDtypeStruct((GROUP, own, D), F32),
+            jax.ShapeDtypeStruct((GROUP, own + 16, D), BF16),
+            jax.ShapeDtypeStruct((16, D), F32),
+            jax.ShapeDtypeStruct((D, D), BF16),
+            jax.ShapeDtypeStruct((D, D), BF16),
+        ],
+        scratch_shapes=[pltpu.VMEM((D, D), F32)],
+        compiler_params=PARAMS,
+        name="mlp_forward",
+    )(*packs, up_lo, up_hi, natural, rep)
+
+
+def run_mlp_backward(cotangents, down_lo, down_hi, up_rel, to_rel, pre, act, values, vectors):
+    own = cotangents.shape[1] - 16
+    half = D // 2
+    grad = jax.ShapeDtypeStruct((half, D), BF16)
     acts = jax.ShapeDtypeStruct((GROUP, own, D), F32)
     return pl.pallas_call(
-        functools.partial(mlp_kernel, down_place),
+        mlp_backward_kernel,
         grid=(GROUP,),
-        in_specs=[whole(packed, D)] * 4
-        + [whole(half, wide), whole(half, wide), whole(half, D), whole(half, D), whole(D, D), smem()],
-        out_specs=[whole(half, 2 * D)] * 2 + [token_block(own, D)] * 3 + [whole(16, D), whole(8, D)],
-        out_shape=[grad] * 2
-        + [acts] * 2
-        + [
-            jax.ShapeDtypeStruct((GROUP, own, D), BF16),
-            jax.ShapeDtypeStruct((16, D), F32), jax.ShapeDtypeStruct((8, D), F32)],
-        scratch_shapes=[
-            pltpu.VMEM((D, D), BF16),
-            pltpu.VMEM((D, D), BF16),
-            pltpu.VMEM((D, D), F32),
-            pltpu.VMEM((D, D), F32),
-        ],
+        in_specs=[token_block(own + 16, D), whole(half, D), whole(half, D), whole(D, D), whole(D, D)]
+        + [token_block(own, D)] * 3
+        + [whole(16, D)],
+        out_specs=[whole(half, D)] * 2 + [token_block(own, D)] * 2 + [whole(8, D)],
+        out_shape=[grad, grad, acts, acts, jax.ShapeDtypeStruct((8, D), F32)],
+        scratch_shapes=[pltpu.VMEM((D, D), BF16), pltpu.VMEM((D, D), F32)],
         compiler_params=PARAMS,
-        name="mlp",
-    )(*packs, up_lo, up_hi, down_lo, down_hi, to_rel, rep)
-
-
-def run_attention(packs, qkv_lo, qkv_hi, proj, to_rel, vectors, mlp_sums, place, head_spread, mlp_part, mlp_norm, values, rep, rows):
-    packed = packs[0].shape[0]
-    own = (packed - 16) // 2
+        name="mlp_backward",
+    )(cotangents, down_lo, down_hi, up_rel, to_rel, pre, act, values, vectors)
+
+
+def run_attention(cotangents, qkv_lo, qkv_hi, proj, to_rel, vectors, mlp_sums, found, head_natural, mlp_part, mlp_norm, values, rep, rows):
+    own = cotangents.shape[1] - 16
     half = D // 2
     width = 3 * QUART
     column = np.arange(3 * EXT)
@@ -311,7 +361,7 @@
     partner = np.where(inner < halfway, inner + halfway, np.where(inner < ROT, inner - halfway, inner))
     source = which * QUART + head * HDIM + np.where(unit < HDIM, inner, partner)
     source = np.where((which == 2) & (unit >= HDIM), -1, source)
-    spread = (jnp.arange(width)[:, None] == jnp.asarray(source, jnp.int32)[None, :]).astype(BF16)
+    source = jnp.asarray(source[None, :], jnp.int32)
     lane = np.arange(LANES) % HDIM
     angle = np.arange(LANES)[:, None] * (10000.0 ** (-(lane % halfway) / halfway))[None, :]
     sign = np.where(lane < halfway, -1.0, 1.0) * np.where(np.arange(LANES) < HDIM, 1.0, -1.0)
@@ -331,17 +381,17 @@
     return pl.pallas_call(
         functools.partial(attention_kernel, rows),
         grid=(GROUP,),
-        in_specs=[whole(packed, D)] * 4
-        + [
+        in_specs=[
+            token_block(own + 16, D),
             whole(half, width),
             whole(half, width),
             whole(QUART, D),
             whole(D, D),
             whole(16, D),
             whole(8, D),
-            whole(width, 3 * D),
-            whole(width, 3 * EXT),
-            whole(EXT, QUART),
+            whole(1, 3 * D),
+            whole(1, 3 * EXT),
+            whole(1, QUART),
             whole(3, LANES, LANES),
             whole(3, LANES, LANES),
             token_block(own, D),
@@ -367,19 +417,24 @@
             pltpu.VMEM((own, EXT), BF16),
             pltpu.VMEM((8, D), F32),
             pltpu.VMEM((8, width), F32),
+            pltpu.VMEM((width, 3 * D), BF16),
+            pltpu.VMEM((width, 3 * EXT), BF16),
+            pltpu.VMEM((EXT, QUART), BF16),
         ],
         compiler_params=PARAMS,
         name="attention",
     )(
-        *packs, qkv_lo, qkv_hi, proj, to_rel, vectors, mlp_sums, place, spread, head_spread, *tables, mlp_part, mlp_norm,
+        cotangents, qkv_lo, qkv_hi, proj, to_rel, vectors, mlp_sums, found, source, head_natural, *tables, mlp_part, mlp_norm,
         values, rep
     )
 
 
-def finish_kernel(pack, near, received, to_rel, out_bias, live, block_out, input_grad):
+def finish_kernel(pack, near, received, to_rel, vectors, live, block_out, input_grad):
+    vectors_nat = dot_t(vectors[...].astype(BF16), to_rel[...])
+    out_bias = vectors_nat[7:8] + vectors_nat[12:13]
     own = near.shape[0]
     partial = near[...].astype(F32) + received[...].astype(F32)
-    block_out[...] = (live[...] * (pack[:own].astype(F32) + partial[:, :D] + out_bias[...])).astype(BF16)
+    block_out[...] = (live[...] * (pack[:own].astype(F32) + partial[:, :D] + out_bias)).astype(BF16)
     values = dot(pack[:own], to_rel[...])
     centered = values - jnp.mean(values, axis=-1, keepdims=True)
     inverse = lax.rsqrt(jnp.mean(centered * centered, axis=-1, keepdims=True) + EPSILON)
@@ -394,79 +449,99 @@
     input_grad[...] = dot_t(grad, to_rel[...]).astype(BF16)
 
 
-def run_finish(pack, near, received, to_rel, out_bias, live):
+def run_finish(pack, near, received, to_rel, vectors, live):
     own = near.shape[0]
     out = jax.ShapeDtypeStruct((own, D), BF16)
     return pl.pallas_call(finish_kernel, out_shape=[out, out], compiler_params=PARAMS, name="finish")(
-        pack, near, received, to_rel, out_bias, live
+        pack, near, received, to_rel, vectors, live
     )
 
 
+def owner(values, rep, natural):
+    first, second, third, fourth = values
+    chosen = jnp.where(rep == natural ^ 1, third, fourth)
+    chosen = jnp.where(rep == natural ^ 2, second, chosen)
+    return jnp.where(rep == natural, first, chosen)
+
+
+def assemble_mlp_kernel(*refs):
+    pairs, rep, up_out, down_out = refs[:4], refs[4][0], refs[5], refs[6]
+    rows = up_out.shape[0]
+    for natural in range(GROUP):
+        down_out[natural * rows : (natural + 1) * rows] = owner([ref[:, :D].astype(F32) for ref in pairs], rep, natural)
+        up = owner([ref[:, D:].astype(F32) for ref in pairs], rep, natural)
+        for shard in range(D // rows):
+            start = (shard * GROUP + natural) * rows
+            up_out[:, start : start + rows] = up[:, shard * rows : (shard + 1) * rows]
+
+
+def run_assemble_mlp(pairs, place, rows):
+    return pl.pallas_call(
+        assemble_mlp_kernel,
+        in_specs=[pl.BlockSpec(memory_space=pltpu.VMEM)] * 4 + [smem()],
+        out_shape=[jax.ShapeDtypeStruct((rows, FF), F32), jax.ShapeDtypeStruct((GROUP * rows, D), F32)],
+        compiler_params=PARAMS,
+        name="assemble_mlp",
+    )(*pairs, place)
+
+
+def assemble_mlp_plain(pairs, place, rows):
+    swapped = jnp.arange(GROUP) ^ place[0]
+    pairs_nat = jnp.stack(pairs).astype(F32)[(swapped % 2) * 2 + swapped // 2]
+    up = pairs_nat[:, :, D:].reshape(GROUP, rows, D // rows, rows).transpose(1, 2, 0, 3)
+    return up.reshape(rows, FF), pairs_nat[:, :, :D].reshape(GROUP * rows, D)
+
+
+VEC_PARTS = (1, 1, 1, 1, 3, 1, GROUP)
+
+
 def assemble_kernel(*refs):
-    pairs, columns = refs[:4], refs[4:8]
-    place = refs[8]
-    qkv_out, proj_out, up_out, down_out, vec_out = refs[9:]
+    columns, place = refs[:4], refs[4]
+    qkv_out, proj_out, vec_outs = refs[5], refs[6], refs[7:]
     rows = proj_out.shape[0]
     width = 3 * QUART
     side = width + VEC_LANES
     rep, top = place[0], place[1]
-
-    def owner(values, natural):
-        first, second, third, fourth = values
-        chosen = jnp.where(rep == natural ^ 1, third, fourth)
-        chosen = jnp.where(rep == natural ^ 2, second, chosen)
-        return jnp.where(rep == natural, first, chosen)
-
     for natural in range(GROUP):
-        down_out[natural * rows : (natural + 1) * rows] = owner([ref[:, :D].astype(F32) for ref in pairs], natural)
-        up = owner([ref[:, D:].astype(F32) for ref in pairs], natural)
-        for shard in range(D // rows):
-            start = (shard * GROUP + natural) * rows
-            up_out[:, start : start + rows] = up[:, shard * rows : (shard + 1) * rows]
-        qkv = owner([ref[:, :width].astype(F32) for ref in columns], natural)
+        qkv = owner([ref[:, :width].astype(F32) for ref in columns], rep, natural)
         for which in range(3):
             start = (which * GROUP + natural) * QUART
             qkv_out[:, start : start + QUART] = qkv[:, which * QUART : (which + 1) * QUART]
-    parts = [ref[:, side:].astype(F32) for ref in columns]
-    chosen = jnp.where((rep ^ top) == 1, parts[2], parts[3])
-    chosen = jnp.where((rep ^ top) == 2, parts[1], chosen)
-    proj_out[...] = jnp.where((rep ^ top) == 0, parts[0], chosen)
+    proj_out[...] = owner([ref[:, side:].astype(F32) for ref in columns], rep, top)
     vec = [ref[:, width:side].astype(F32) for ref in columns]
-    vec_out[...] = ((vec[0] + vec[1]) + (vec[2] + vec[3])).T[:16]
-
-
-def run_assemble(pairs, columns, place, rows):
-    shapes = [(rows, 3 * D), (rows, D), (rows, FF), (GROUP * rows, D), (16, rows)]
+    vec = ((vec[0] + vec[1]) + (vec[2] + vec[3])).T[:16]
+    line = 0
+    for out in vec_outs:
+        for start in range(0, out.shape[1], rows):
+            out[:, start : start + rows] = vec[line : line + 1]
+            line += 1
+
+
+def run_assemble(columns, place, rows):
+    shapes = [(rows, 3 * D), (rows, D)] + [(1, count * rows) for count in VEC_PARTS]
     return pl.pallas_call(
         assemble_kernel,
-        in_specs=[pl.BlockSpec(memory_space=pltpu.VMEM)] * 8 + [smem()],
+        in_specs=[pl.BlockSpec(memory_space=pltpu.VMEM)] * 4 + [smem()],
         out_shape=[jax.ShapeDtypeStruct(shape, F32) for shape in shapes],
         compiler_params=PARAMS,
         name="assemble",
-    )(*pairs, *columns, place)
-
-
-def assemble_plain(pairs, columns, place, rows):
+    )(*columns, place)
+
+
+def assemble_plain(columns, place, rows):
     width = 3 * QUART
     side = width + VEC_LANES
-    rep, top = place[0], place[1]
-    pairs = jnp.stack(pairs).astype(F32)
     columns = jnp.stack(columns).astype(F32)
-    natural = jnp.arange(GROUP)
-    swapped = natural ^ rep
-    order = (swapped % 2) * 2 + swapped // 2
-    pairs_nat, columns_nat = pairs[order], columns[order]
+    swapped = jnp.arange(GROUP) ^ place[0]
+    columns_nat = columns[(swapped % 2) * 2 + swapped // 2]
     qkv = columns_nat[:, :, :width].reshape(GROUP, rows, 3, QUART).transpose(1, 2, 0, 3)
-    up = pairs_nat[:, :, D:].reshape(GROUP, rows, D // rows, rows).transpose(1, 2, 0, 3)
     vec = columns[:, :, width:side]
-    vec = ((vec[0] + vec[1]) + (vec[2] + vec[3])).T[:16]
-    return (
-        qkv.reshape(rows, 3 * D),
-        columns_nat[top][:, side:],
-        up.reshape(rows, FF),
-        pairs_nat[:, :, :D].reshape(GROUP * rows, D),
-        vec,
-    )
+    vec = ((vec[0] + vec[1]) + (vec[2] + vec[3])).T
+    outs, line = [], 0
+    for count in VEC_PARTS:
+        outs.append(vec[line : line + count].reshape(1, count * rows))
+        line += count
+    return (qkv.reshape(rows, 3 * D), columns_nat[place[1]][:, side:], *outs)
 
 
 def quarter_kernel(*refs):
@@ -483,7 +558,9 @@
                 start = (which * GROUP + natural) * QUART
                 qkv_own[:, which * QUART : (which + 1) * QUART] = qkv[:, start : start + QUART]
 
-    lines = [ref[k : k + 1].astype(F32) for ref in vectors for k in range(ref.shape[0])]
+    lines = [
+        ref[:, start : start + rows].astype(F32) for ref in vectors for start in range(0, ref.shape[1], rows)
+    ]
     index = lax.broadcasted_iota(jnp.int32, (VEC_LANES, rows), 0)
     table = jnp.zeros((VEC_LANES, rows), F32)
     for place, line in enumerate(lines):
@@ -536,17 +613,12 @@
     def add(keep, received):
         return keep.astype(F32) + received.astype(F32)
 
-    def reduce_all(keep, send):
-        for mask in lowest_first:
+    def reduce_all(keep, send, order=lowest_first):
+        for mask in order:
             total = add(keep, shard_swap(send, mask)).astype(BF16)
             half = total.shape[0] // 2
             keep, send = total[:half], total[half:]
         return total
-
-    def one_hot(count, width, mine):
-        place = jnp.array([reverse(p, width) for p in range(count)], jnp.int32)
-        natural = ((place ^ mine)[:, None] * rows + jnp.arange(rows)[None, :]).reshape(1, count * rows)
-        return (jnp.arange(count * rows)[:, None] == natural).astype(BF16)
 
     def body(
         block_input,
@@ -576,13 +648,14 @@
 
         rep_ref = rep.reshape(1)
         vectors_own = [
-            value.reshape(-1, rows)
+            value.reshape(1, -1)
             for value in (
                 first_gain, first_shift, second_gain, second_shift, qkv_bias, proj_bias, up_bias, down_bias
             )
         ]
         if rows % 32:
-            vector_own = jnp.pad(jnp.concatenate(vectors_own, axis=0), ((0, VEC_LANES - 13), (0, 0))).T
+            vector_own = jnp.concatenate([value.reshape(-1, rows) for value in vectors_own], axis=0)
+            vector_own = jnp.pad(vector_own, ((0, VEC_LANES - 13), (0, 0))).T
             up_own = lax.dynamic_index_in_dim(
                 up_weight.reshape(rows, shards, GROUP, rows), rep, axis=2, keepdims=False
             ).reshape(rows, D)
@@ -609,7 +682,7 @@
         packs = (token_pack, token_across, token_beside, token_far)
 
         up_lo, up_hi = gather_all(up_own)
-        down_lo, down_hi = gather_all(down_own, down_order)
+        down_lo, down_hi = gather_all(down_own)
         qkv_lo, qkv_hi = gather_all(qkv_own)
 
         proj_part = jnp.where(top_across == across, proj_weight, shard_swap(proj_weight, highest_first[0]))
@@ -617,26 +690,29 @@
         for mask in highest_first[2:]:
             proj_part = jnp.concatenate([proj_part, shard_swap(proj_part, mask)], axis=0)
 
-        to_rel = one_hot(shards, bits, mine)
-        head_to_rel = one_hot(shards // 4, bits - 2, mine % (shards // 4))
-        head_spread = jnp.pad(
-            head_to_rel.reshape(LOCAL_HEADS, HDIM, QUART), ((0, 0), (0, LANES - HDIM), (0, 0))
-        ).reshape(EXT, QUART)
-
         width = 3 * QUART
-        place = jnp.array([reverse(p, bits) for p in range(shards)], jnp.int32)
-        shard_start = (place ^ mine)[None, :, None] * (3 * rows)
-        found = shard_start + jnp.arange(3)[:, None, None] * rows + jnp.arange(rows)[None, None, :]
-        found = found.reshape(1, 3 * D)
-        found = jnp.where(found % D // QUART == rep, found // D * QUART + found % QUART, -1)
-        bias_place = (jnp.arange(width)[:, None] == found).astype(BF16)
-
-        keep, send, mlp_part, mlp_norm, values, vectors, mlp_sums = run_mlp(
-            packs, up_lo, up_hi, down_lo, down_hi, to_rel, rep_ref, down_place
+        block = np.array([reverse(p, bits) for p in range(shards)], np.int32)
+        inner = np.arange(rows, dtype=np.int32)
+        feature_block, feature_inner = np.repeat(block, rows), np.tile(inner, shards)
+        natural = ((feature_block ^ mine) * rows + feature_inner)[None]
+        low_block = np.array([reverse(p, bits - 2) for p in range(shards // 4)], np.int32)
+        low_block, low_inner = np.repeat(low_block, rows), np.tile(inner, shards // 4)
+        head_natural = ((low_block ^ (mine % (shards // 4))) * rows + low_inner)[None]
+        shift = np.repeat(np.arange(3, dtype=np.int32) * rows, D)
+        found = (np.tile(feature_block, 3) ^ mine) * (3 * rows) + (shift + np.tile(feature_inner, 3))
+        found = jnp.where(found % D // QUART == rep, found // D * QUART + found % QUART, -1)[None]
+
+        keep, send, pre, act, values, cotangents, vectors, up_rel, to_rel = run_mlp_forward(
+            packs, up_lo, up_hi, natural, rep_ref, down_place
         )
-        pair = reduce_all(keep, send)
+        down_grad = reduce_all(keep, send, down_order[::-1])
+        keep, send, mlp_part, mlp_norm, mlp_sums = run_mlp_backward(
+            cotangents, down_lo, down_hi, up_rel, to_rel, pre, act, values, vectors
+        )
+        up_grad = reduce_all(keep, send)
+        pair = jnp.concatenate([down_grad, up_grad], axis=1)
         keep, send, partial, partial_far = run_attention(
-            packs, qkv_lo, qkv_hi, proj_part, to_rel, vectors, mlp_sums, bias_place, head_spread,
+            cotangents, qkv_lo, qkv_hi, proj_part, to_rel, vectors, mlp_sums, found, head_natural,
             mlp_part, mlp_norm, values, rep_ref, rows,
         )
 
@@ -666,33 +742,31 @@
 
         summed = add(partial, core_swap(partial_far))
         received = x_swap(summed[1].astype(BF16))
-        vectors_nat = dot_t(vectors.astype(BF16), to_rel)
-        out_bias = (vectors_nat[7] + vectors_nat[12])[None]
-        block_out, input_grad = run_finish(token_pack, summed[0], received, to_rel, out_bias, live)
+        block_out, input_grad = run_finish(token_pack, summed[0], received, to_rel, vectors, live)
 
         pair_across = x_swap(pair)
         pair_all = (pair, pair_across, core_swap(pair), core_swap(pair_across))
         column_across = x_swap(column)
         column_all = (column, column_across, core_swap(column), core_swap(column_across))
-        assemble = assemble_plain if rows % 32 else run_assemble
-        qkv_out, proj_out, up_out, down_out, vec_out = assemble(
-            pair_all, column_all, jnp.stack([rep, top]), rows
-        )
+        where = jnp.stack([rep, top])
+        up_out, down_out = (assemble_mlp_plain if rows % 32 else run_assemble_mlp)(pair_all, where, rows)
+        qkv_out, proj_out, *vec = (assemble_plain if rows % 32 else run_assemble)(column_all, where, rows)
+        vec = [each.reshape(-1) for each in vec]
         return (
             block_out.reshape(micro, slot, D),
             input_grad.reshape(micro, slot, D),
-            vec_out[0],
-            vec_out[1],
-            vec_out[2],
-            vec_out[3],
+            vec[0],
+            vec[1],
+            vec[2],
+            vec[3],
             qkv_out,
-            vec_out[4:7].reshape(3 * rows),
+            vec[4],
             proj_out,
-            vec_out[7],
+            vec[5],
             up_out,
-            vec_out[8:12].reshape(GROUP * rows),
+            vec[6],
             down_out,
-            vec_out[7],
+            vec[5],
         )
 
     return body

time: 220 us -> 200 us (0.909)
  waiting for transfers between devices: 97.4 us -> 72.6 us
  Pallas kernels: 57.3 us -> 63.4 us
  other arithmetic: 21.8 us -> 16.7 us
  starting transfers between devices: 24.6 us -> 28.9 us
    ppermute x18 -> x21, waiting for transfers between devices: 90.7 us -> 68.9 us  [shard_swap(): return lax.ppermute(value, 'fsdp', [(i, i ^ mask) for i in range(shards)])]
    pallas_call x1 -> x3, Pallas kernels: 20.6 us -> 30 us  [the longest x1 14 us: run_mlp_forward(): pl.pallas_call(functools.partial(mlp_forward_kernel, down_place), grid=(G...]
    convert_element_type x3 -> x0, other arithmetic: 5.2 us -> none  [the longest x1 2.33 us: body(): bias_place = (jnp.arange(width)[:, None] == found).astype(BF16)]
    ppermute x18 -> x21, starting transfers between devices: 19 us -> 22.6 us  [shard_swap(): return lax.ppermute(value, 'fsdp', [(i, i ^ mask) for i in range(shards)])]
    ppermute x4, waiting for transfers between devices: 6.69 us -> 3.66 us  [x_swap(): return lax.ppermute(value, 'rep', [(i, i ^ 2) for i in range(GROUP)])]
    pallas_call x0 -> x2, other arithmetic: none -> 2.54 us  [run_assemble(): pl.pallas_call(assemble_kernel, in_specs=[pl.BlockSpec(memory_space=pltpu...]
    pallas_call x1, Pallas kernels: 25.7 us -> 23.3 us  [run_attention(): pl.pallas_call(functools.partial(attention_kernel, rows), grid=(GROUP,),...]
    unnamed x54 -> x68, local copies, waits for them, and re-layouts: 6.95 us -> 7.14 us
  transfers between devices with their start and end apart: 29 -> 32, of which waited for: 13 -> 14; matrix products, arithmetic and copies ran while one was open for 12% -> 12% of each run, Pallas kernels for 12% -> 29%
where the time goes in v2:
time: 200 us; the launch traced here: 199 us
  waiting for transfers between devices  72.6 us (36%)
  Pallas kernels  63.4 us (32%)
  starting transfers between devices  28.9 us (14%)
  local copies, waits for them, and re-layouts  16.7 us (8%)
  other arithmetic  16.7 us (8%)
    ppermute x21, waiting for transfers between devices, shard_swap(): return lax.ppermute(value, 'fsdp', [(i, i ^ mask) for i in range(shards)])  68.9 us
    pallas_call x1, Pallas kernels, run_attention(): pl.pallas_call(functools.partial(attention_kernel, rows), grid=(GROUP,),...  23.3 us
    ppermute x21, starting transfers between devices, shard_swap(): return lax.ppermute(value, 'fsdp', [(i, i ^ mask) for i in range(shards)])  22.6 us
    pallas_call x1, Pallas kernels, run_mlp_forward(): pl.pallas_call(functools.partial(mlp_forward_kernel, down_place), grid=(G...  14 us
    pallas_call x1, Pallas kernels, run_mlp_backward(): pl.pallas_call(mlp_backward_kernel, grid=(GROUP,), in_specs=[token_block(...  13 us
    unnamed x68, local copies, waits for them, and re-layouts  7.14 us
    ppermute x4, starting transfers between devices, x_swap(): return lax.ppermute(value, 'rep', [(i, i ^ 2) for i in range(GROUP)])  5.77 us
    pallas_call x1, Pallas kernels, run_finish(): pl.pallas_call(finish_kernel, out_shape=[out, out], compiler_params=PARAM...  4.66 us
  transfers between devices with their start and end apart: 32, of which 14 were waited for; matrix products, arithmetic and copies ran while one was open for 12% of the time, Pallas kernels for 29%

profile of v2, /device:TPU:0, one launch (start us, length us, event | category | flops | bytes accessed | tf_op | source)
XLA Modules:
  0.0 199.4 jit_solution(2717357541368983083)
XLA Ops:
  4.4 3.0 %collective-permute-start = (bf16[528,768]{1,0:T(8,128)(2,1)S(1)}, bf16[528,768]{1,0:T(8,128)(2,1)}, u32[]{:S(2)}, u32[]{:S(2)}) collective-permute-start(bf16[528,768]{1,0:T(8,128)(2,1)S(1)} %fusion.1.near.pack), channel_id=1, source_target_pairs={{0,2},{1,3},{2,0},{3,1},{4,6},{5,7},{6,4},{7,5},{8,10},{9,11},{10,... | collective-permute-start | bytes 2433032 | tf_op jit(solution)/shard_map/ppermute | solution.py:601
  8.5 2.8 %quarter.1 = (bf16[96,896]{1,0:T(8,128)(2,1)}, bf16[96,576]{1,0:T(8,128)(2,1)}) custom-call(bf16[1,96]{1,0:T(2,128)(2,1)} %bitcast.41, bf16[1,96]{1,0:T(2,128)(2,1)} %bitcast.42, bf16[1,96]{1,0:T(2,128)(2,1)} %bitcast.43, bf16[1,96]{1,0:T(2,128)(2,1)} %bitcast.44, bf16[1,288]{1,0:T(2,128)(2,1)} %reshape.137.refs_4_, bf16[1,96]{1,0:T(2,128)(2,1)} %bitcast.45, ...), custom_call_target="tpu_custom_call" | custom-call | tf_op jit(solution)/shard_map/quarter/pallas_call | solution.py:573
  11.3 2.6 %collective-permute-start.3 = (bf16[96,896]{1,0:T(8,128)(2,1)}, bf16[96,896]{1,0:T(8,128)(2,1)S(1)}, u32[]{:S(2)}, u32[]{:S(2)}) collective-permute-start(bf16[96,896]{1,0:T(8,128)(2,1)} %get-tuple-element.47), channel_id=1, source_target_pairs={{0,16},{4,20},{8,24},{12,28},{16,0},{20,4},{24,8},{28,12},{1,17},{... | collective-permute-start | bytes 516104 | tf_op jit(solution)/shard_map/ppermute | solution.py:595
  14.3 2.6 %collective-permute-start.6 = (bf16[96,576]{1,0:T(8,128)(2,1)}, bf16[96,576]{1,0:T(8,128)(2,1)S(1)}, u32[]{:S(2)}, u32[]{:S(2)}) collective-permute-start(bf16[96,576]{1,0:T(8,128)(2,1)} %get-tuple-element.49), channel_id=1, source_target_pairs={{0,16},{4,20},{8,24},{12,28},{16,0},{20,4},{24,8},{28,12},{1,17},{... | collective-permute-start | bytes 331784 | tf_op jit(solution)/shard_map/ppermute | solution.py:595
  18.5 10.6 %collective-permute-done.3 = bf16[96,896]{1,0:T(8,128)(2,1)S(1)} collective-permute-done((bf16[96,896]{1,0:T(8,128)(2,1)}, bf16[96,896]{1,0:T(8,128)(2,1)S(1)}, u32[]{:S(2)}, u32[]{:S(2)}) %collective-permute-start.3) | collective-permute-done | bytes 172064 | tf_op jit(solution)/shard_map/ppermute | solution.py:595
  30.5 1.8 collective-permute-done.12
  32.7 9.3 %collective-permute-done.4 = bf16[192,896]{1,0:T(8,128)(2,1)S(1)} collective-permute-done((bf16[192,896]{1,0:T(8,128)(2,1)S(1)}, bf16[192,896]{1,0:T(8,128)(2,1)S(1)}, u32[]{:S(2)}, u32[]{:S(2)}) %collective-permute-start.4) | collective-permute-done | bytes 344096 | tf_op jit(solution)/shard_map/ppermute | solution.py:595
  41.9 1.6 collective-permute-start.9
  43.6 1.6 collective-permute-start.5
  45.2 5.3 %collective-permute-done.13 = bf16[192,768]{1,0:T(8,128)(2,1)S(1)} collective-permute-done((bf16[192,768]{1,0:T(8,128)(2,1)S(1)}, bf16[192,768]{1,0:T(8,128)(2,1)S(1)}, u32[]{:S(2)}, u32[]{:S(2)}) %collective-permute-start.13) | collective-permute-done | bytes 294944 | tf_op jit(solution)/shard_map/ppermute | solution.py:595
  54.4 3.9 %collective-permute-done.7 = bf16[192,576]{1,0:T(8,128)(2,1)S(1)} collective-permute-done((bf16[192,576]{1,0:T(8,128)(2,1)S(1)}, bf16[192,576]{1,0:T(8,128)(2,1)S(1)}, u32[]{:S(2)}, u32[]{:S(2)}) %collective-permute-start.7) | collective-permute-done | bytes 221216 | tf_op jit(solution)/shard_map/ppermute | solution.py:595
  58.7 1.6 collective-permute-start.8
  60.3 1.7 collective-permute-done.5.up_hi
  62.8 14.0 %mlp_forward.1 = (bf16[384,768]{1,0:T(8,128)(2,1)}, bf16[384,768]{1,0:T(8,128)(2,1)}, f32[4,256,768]{2,1,0:T(8,128)}, bf16[4,256,768]{2,1,0:T(8,128)(2,1)}, f32[...) custom-call(bf16[528,768]{1,0:T(8,128)(2,1)} %copy-done.2, ...), custom_call_target="tpu_custom_call" | custom-call | tf_op jit(solution)/shard_map/mlp_forward/pallas_call | solution.py:310
  76.8 2.6 %collective-permute-start.23 = (bf16[384,768]{1,0:T(8,128)(2,1)}, bf16[384,768]{1,0:T(8,128)(2,1)S(1)}, u32[]{:S(2)}, u32[]{:S(2)}) collective-permute-start(bf16[384,768]{1,0:T(8,128)(2,1)} %get-tuple-element.74), channel_id=1, source_target_pairs={{0,8},{4,12},{8,0},{12,4},{16,24},{20,28},{24,16},{28,20},{1,9},{5... | collective-permute-start | bytes 1769480 | tf_op jit(solution)/shard_map/ppermute | solution.py:595
  81.0 13.0 %mlp_backward.1 = (bf16[384,768]{1,0:T(8,128)(2,1)}, bf16[384,768]{1,0:T(8,128)(2,1)}, f32[4,256,768]{2,1,0:T(8,128)}, f32[4,256,768]{2,1,0:T(8,128)}, f32[8,768]{1,0:T(8,128)}) custom-call(bf16[4,272,768]{2,1,0:T(8,128)(2,1)} %get-tuple-element.48.cotangents, bf16[384,768]{1,0:T(8,128)(2,1)} %copy-done.3, bf16[384,768]{1,0:T(8,128)(2,1)} %collective-permute-done.14.down_hi, ...), custom_call_target="tpu_custom_call" | custom-call | tf_op jit(solution)/shard_map/mlp_backward/pallas_call | solution.py:339
  96.4 23.3 %attention.1 = (bf16[384,896]{1,0:T(8,128)(2,1)}, bf16[384,896]{1,0:T(8,128)(2,1)}, bf16[2,256,1536]{2,1,0:T(8,128)(2,1)}, bf16[2,256,1536]{2,1,0:T(8,128)(2,1)}) custom-call(bf16[4,272,768]{2,1,0:T(8,128)(2,1)} %get-tuple-element.48.cotangents, bf16[384,576]{1,0:T(8,128)(2,1)} %copy-done.9, bf16[384,576]{1,0:T(8,128)(2,1)} %collective-permute-done.8.qkv_hi, ...), custom_call_target="tpu_custom_call" | custom-call | tf_op jit(solution)/shard_map/attention/pallas_call | solution.py:381
  119.8 1.6 collective-permute-start.17
  123.1 1.8 collective-permute-start.27
  124.9 11.8 %collective-permute-done.17 = bf16[384,896]{1,0:T(8,128)(2,1)S(1)} collective-permute-done((bf16[384,896]{1,0:T(8,128)(2,1)}, bf16[384,896]{1,0:T(8,128)(2,1)S(1)}, u32[]{:S(2)}, u32[]{:S(2)}) %collective-permute-start.17) | collective-permute-done | bytes 688160 | tf_op jit(solution)/shard_map/ppermute | solution.py:595
  137.3 2.0 collective-permute-done.24
  142.6 3.1 %collective-permute-done.25 = bf16[96,768]{1,0:T(8,128)(2,1)S(1)} collective-permute-done((bf16[96,768]{1,0:T(8,128)(2,1)S(1)}, bf16[96,768]{1,0:T(8,128)(2,1)S(1)}, u32[]{:S(2)}, u32[]{:S(2)}) %collective-permute-start.25) | collective-permute-done | bytes 147488 | tf_op jit(solution)/shard_map/ppermute | solution.py:595
  145.7 6.0 %collective-permute-done.18 = bf16[192,1088]{1,0:T(8,128)(2,1)S(1)} collective-permute-done((bf16[192,1088]{1,0:T(8,128)(2,1)S(1)}, bf16[192,1088]{1,0:T(8,128)(2,1)S(1)}, u32[]{:S(2)}, u32[]{:S(2)}) %collective-permute-start.18) | collective-permute-done | bytes 417824 | tf_op jit(solution)/shard_map/ppermute | solution.py:595
  154.7 13.0 %collective-permute-done.19 = bf16[96,1472]{1,0:T(8,128)(2,1)} collective-permute-done((bf16[96,1472]{1,0:T(8,128)(2,1)}, bf16[96,1472]{1,0:T(8,128)(2,1)}, u32[]{:S(2)}, u32[]{:S(2)}) %collective-permute-start.19) | collective-permute-done | bytes 282656 | tf_op jit(solution)/shard_map/ppermute | solution.py:595
  169.3 1.8 convert_add_fusion
  171.2 1.6 copy-done.1
  172.9 1.6 collective-permute-start.16
  176.5 2.3 %collective-permute-done.20.refs_1_ = bf16[96,1472]{1,0:T(8,128)(2,1)S(1)} collective-permute-done((bf16[96,1472]{1,0:T(8,128)(2,1)S(1)}, bf16[96,1472]{1,0:T(8,128)(2,1)S(1)}, u32[]{:S(2)}, u32[]{:S(2)}) %collective-permute-start.20) | collective-permute-done | bytes 282656 | tf_op jit(solution)/shard_map/ppermute | solution.py:601
  178.7 2.8 %slice_bitcast_fusion.near = f32[256,1536]{1,0:T(8,128)} fusion(f32[2,256,1536]{2,1,0:T(8,128)} %copy-done.1), kind=kLoop, calls=%fused_computation.4 | loop fusion | bytes 3145728 | tf_op jit(solution)/shard_map/squeeze | solution.py:745
  182.3 3.1 %assemble_mlp.1 = (f32[96,3072]{1,0:T(8,128)}, f32[384,768]{1,0:T(8,128)}) custom-call(bf16[96,1536]{1,0:T(8,128)(2,1)} %copy-done.6, bf16[96,1536]{1,0:T(8,128)(2,1)} %collective-permute-done.29.refs_1_, bf16[96,1536]{1,0:T(8,128)(2,1)} %copy-done.21, bf16[96,1536]{1,0:T(8,128)(2,1)} %collective-permute-done.31.refs_3_, s32[2]{0:T(128)} %pad_add_fusion.refs_4_), custom_call_target="tpu_custom_call" | custom-call | tf_op jit(solution)/shard_map/assemble_mlp/pallas_call | solution.py:479
  186.8 2.6 %assemble.1 = (f32[96,2304]{1,0:T(8,128)}, f32[96,768]{1,0:T(8,128)}, f32[1,96]{1,0:T(1,128)}, f32[1,96]{1,0:T(1,128)}, f32[1,96]{1,0:T(1,128)}, /*index=5*/f32[...) custom-call(bf16[96,1472]{1,0:T(8,128)(2,1)} %copy-done.5, bf16[96,1472]{1,0:T(8,128)(2,1)} %copy-done.18, ...), custom_call_target="tpu_custom_call" | custom-call | tf_op jit(solution)/shard_map/assemble/pallas_call | solution.py:522
  194.3 4.7 %finish.1 = (bf16[256,768]{1,0:T(8,128)(2,1)}, bf16[256,768]{1,0:T(8,128)(2,1)}) custom-call(bf16[528,768]{1,0:T(8,128)(2,1)} %copy-done.2, f32[256,1536]{1,0:T(8,128)} %slice_bitcast_fusion.near, bf16[256,1536]{1,0:T(8,128)(2,1)} %copy-done.8, bf16[768,768]{1,0:T(8,128)(2,1)} %get-tuple-element.50.to_rel, f32[16,768]{1,0:T(8,128)} %get-tuple-element.51.vectors, ...), custom_call_target="tpu_custom_call" | custom-call | tf_op jit(solution)/shard_map/finish/pallas_call | solution.py:455
  (157 shorter events, 37.5 us)
Async XLA Ops:
  4.4 39.1 %collective-permute-start = (bf16[528,768]{1,0:T(8,128)(2,1)S(1)}, bf16[528,768]{1,0:T(8,128)(2,1)}, u32[]{:S(2)}, u32[]{:S(2)}) collective-permute-start(bf16[528,768]{1,0:T(8,128)(2,1)S(1)} %fusion.1.near.pack), channel_id=1, source_target_pairs={{0,2},{1,3},{2,0},{3,1},{4,6},{5,7},{6,4},{7,5},{8,10},{9,11},{10,... | collective-permute-start | bytes 2433032 | tf_op jit(solution)/shard_map/ppermute | solution.py:601
  7.4 51.3 %collective-permute-start.1 = (bf16[528,768]{1,0:T(8,128)(2,1)S(1)}, bf16[528,768]{1,0:T(8,128)(2,1)}, u32[]{:S(2)}, u32[]{:S(2)}) collective-permute-start(bf16[528,768]{1,0:T(8,128)(2,1)S(1)} %fusion.1.near.pack), channel_id=1, source_target_pairs={{0,1},{1,0},{2,3},{3,2},{4,5},{5,4},{6,7},{7,6},{8,9},{9,8},{10,11... | collective-permute-start | bytes 2433032 | tf_op jit(solution)/shard_map/ppermute | solution.py:598
  11.3 17.8 %collective-permute-start.3 = (bf16[96,896]{1,0:T(8,128)(2,1)}, bf16[96,896]{1,0:T(8,128)(2,1)S(1)}, u32[]{:S(2)}, u32[]{:S(2)}) collective-permute-start(bf16[96,896]{1,0:T(8,128)(2,1)} %get-tuple-element.47), channel_id=1, source_target_pairs={{0,16},{4,20},{8,24},{12,28},{16,0},{20,4},{24,8},{28,12},{1,17},{... | collective-permute-start | bytes 516104 | tf_op jit(solution)/shard_map/ppermute | solution.py:595
  13.9 18.4 %collective-permute-start.12 = (bf16[96,768]{1,0:T(8,128)(2,1)S(1)}, bf16[96,768]{1,0:T(8,128)(2,1)S(1)}, u32[]{:S(2)}, u32[]{:S(2)}) collective-permute-start(bf16[96,768]{1,0:T(8,128)(2,1)S(1)} %dynamic-slice_bitcast_fusion), channel_id=1, source_target_pairs={{0,16},{4,20},{8,24},{12,28},{16,0},{20,4},{24,8},{28,12},{1,17},{... | collective-permute-start | bytes 442376 | tf_op jit(solution)/shard_map/ppermute | solution.py:595
  14.3 29.3 %collective-permute-start.6 = (bf16[96,576]{1,0:T(8,128)(2,1)}, bf16[96,576]{1,0:T(8,128)(2,1)S(1)}, u32[]{:S(2)}, u32[]{:S(2)}) collective-permute-start(bf16[96,576]{1,0:T(8,128)(2,1)} %get-tuple-element.49), channel_id=1, source_target_pairs={{0,16},{4,20},{8,24},{12,28},{16,0},{20,4},{24,8},{28,12},{1,17},{... | collective-permute-start | bytes 331784 | tf_op jit(solution)/shard_map/ppermute | solution.py:595
  30.1 11.9 %collective-permute-start.4 = (bf16[192,896]{1,0:T(8,128)(2,1)S(1)}, bf16[192,896]{1,0:T(8,128)(2,1)S(1)}, u32[]{:S(2)}, u32[]{:S(2)}) collective-permute-start(bf16[192,896]{1,0:T(8,128)(2,1)S(1)} %pad_maximum_fusion.1), channel_id=1, source_target_pairs={{0,8},{4,12},{8,0},{12,4},{16,24},{20,28},{24,16},{28,20},{1,9},{5... | collective-permute-start | bytes 1032200 | tf_op jit(solution)/shard_map/ppermute | solution.py:595
  32.4 18.1 %collective-permute-start.13 = (bf16[192,768]{1,0:T(8,128)(2,1)S(1)}, bf16[192,768]{1,0:T(8,128)(2,1)S(1)}, u32[]{:S(2)}, u32[]{:S(2)}) collective-permute-start(bf16[192,768]{1,0:T(8,128)(2,1)S(1)} %pad_maximum_fusion.3), channel_id=1, source_target_pairs={{0,8},{4,12},{8,0},{12,4},{16,24},{20,28},{24,16},{28,20},{1,9},{5... | collective-permute-start | bytes 884744 | tf_op jit(solution)/shard_map/ppermute | solution.py:595
  41.9 10.0 %collective-permute-start.9 = (bf16[96,768]{1,0:T(8,128)(2,1)}, bf16[96,768]{1,0:T(8,128)(2,1)S(1)}, u32[]{:S(2)}, u32[]{:S(2)}) collective-permute-start(bf16[96,768]{1,0:T(8,128)(2,1)} %param.33), channel_id=1, source_target_pairs={{0,16},{4,20},{8,24},{12,28},{16,0},{20,4},{24,8},{28,12},{1,17},{... | collective-permute-start | bytes 442376 | tf_op jit(solution)/shard_map/ppermute | solution.py:595
  43.5 18.5 %collective-permute-start.2 = (bf16[528,768]{1,0:T(8,128)(2,1)}, bf16[528,768]{1,0:T(8,128)(2,1)}, u32[]{:S(2)}, u32[]{:S(2)}) collective-permute-start(bf16[528,768]{1,0:T(8,128)(2,1)} %collective-permute-done.across), channel_id=1, source_target_pairs={{0,1},{1,0},{2,3},{3,2},{4,5},{5,4},{6,7},{7,6},{8,9},{9,8},{10,11... | collective-permute-start | bytes 2433032 | tf_op jit(solution)/shard_map/ppermute | solution.py:598
  43.6 18.4 %collective-permute-start.5 = (bf16[384,896]{1,0:T(8,128)(2,1)S(1)}, bf16[384,896]{1,0:T(8,128)(2,1)S(1)}, u32[]{:S(2)}, u32[]{:S(2)}) collective-permute-start(bf16[384,896]{1,0:T(8,128)(2,1)S(1)} %constant_dynamic-update-slice_fusion.up_lo), channel_id=1, source_target_pairs={{0,4},{4,0},{8,12},{12,8},{16,20},{20,16},{24,28},{28,24},{1,5},{5... | collective-permute-start | bytes 2064392 | tf_op jit(solution)/shard_map/ppermute | solution.py:595
  50.5 7.9 %collective-permute-start.7 = (bf16[192,576]{1,0:T(8,128)(2,1)S(1)}, bf16[192,576]{1,0:T(8,128)(2,1)S(1)}, u32[]{:S(2)}, u32[]{:S(2)}) collective-permute-start(bf16[192,576]{1,0:T(8,128)(2,1)S(1)} %pad_maximum_fusion.5), channel_id=1, source_target_pairs={{0,8},{4,12},{8,0},{12,4},{16,24},{20,28},{24,16},{28,20},{1,9},{5... | collective-permute-start | bytes 663560 | tf_op jit(solution)/shard_map/ppermute | solution.py:595
  51.9 29.0 %collective-permute-start.14 = (bf16[384,768]{1,0:T(8,128)(2,1)S(1)}, bf16[384,768]{1,0:T(8,128)(2,1)}, u32[]{:S(2)}, u32[]{:S(2)}) collective-permute-start(bf16[384,768]{1,0:T(8,128)(2,1)S(1)} %pad_maximum_fusion.down_lo), channel_id=1, source_target_pairs={{0,4},{4,0},{8,12},{12,8},{16,20},{20,16},{24,28},{28,24},{1,5},{5... | collective-permute-start | bytes 1769480 | tf_op jit(solution)/shard_map/ppermute | solution.py:595
  58.3 21.0 %collective-permute-start.10 = (bf16[96,768]{1,0:T(8,128)(2,1)S(1)}, bf16[96,768]{1,0:T(8,128)(2,1)}, u32[]{:S(2)}, u32[]{:S(2)}) collective-permute-start(bf16[96,768]{1,0:T(8,128)(2,1)S(1)} %broadcast_select_fusion), channel_id=1, source_target_pairs={{0,8},{4,12},{8,0},{12,4},{16,24},{20,28},{24,16},{28,20},{1,9},{5... | collective-permute-start | bytes 442376 | tf_op jit(solution)/shard_map/ppermute | solution.py:595
  58.7 37.7 %collective-permute-start.8 = (bf16[384,576]{1,0:T(8,128)(2,1)S(1)}, bf16[384,576]{1,0:T(8,128)(2,1)}, u32[]{:S(2)}, u32[]{:S(2)}) collective-permute-start(bf16[384,576]{1,0:T(8,128)(2,1)S(1)} %constant_dynamic-update-slice_fusion.3.qkv_lo), channel_id=1, source_target_pairs={{0,4},{4,0},{8,12},{12,8},{16,20},{20,16},{24,28},{28,24},{1,5},{5... | collective-permute-start | bytes 1327112 | tf_op jit(solution)/shard_map/ppermute | solution.py:595
  76.8 44.5 %collective-permute-start.23 = (bf16[384,768]{1,0:T(8,128)(2,1)}, bf16[384,768]{1,0:T(8,128)(2,1)S(1)}, u32[]{:S(2)}, u32[]{:S(2)}) collective-permute-start(bf16[384,768]{1,0:T(8,128)(2,1)} %get-tuple-element.74), channel_id=1, source_target_pairs={{0,8},{4,12},{8,0},{12,4},{16,24},{20,28},{24,16},{28,20},{1,9},{5... | collective-permute-start | bytes 1769480 | tf_op jit(solution)/shard_map/ppermute | solution.py:595
  79.4 16.3 %collective-permute-start.11 = (bf16[96,768]{1,0:T(8,128)(2,1)S(1)}, bf16[96,768]{1,0:T(8,128)(2,1)S(1)}, u32[]{:S(2)}, u32[]{:S(2)}) collective-permute-start(bf16[96,768]{1,0:T(8,128)(2,1)S(1)} %broadcast_select_fusion.1), channel_id=1, source_target_pairs={{0,4},{4,0},{8,12},{12,8},{16,20},{20,16},{24,28},{28,24},{1,5},{5... | collective-permute-start | bytes 442376 | tf_op jit(solution)/shard_map/ppermute | solution.py:595
  93.9 28.3 %collective-permute-start.26 = (bf16[384,768]{1,0:T(8,128)(2,1)}, bf16[384,768]{1,0:T(8,128)(2,1)S(1)}, u32[]{:S(2)}, u32[]{:S(2)}) collective-permute-start(bf16[384,768]{1,0:T(8,128)(2,1)} %get-tuple-element.76), channel_id=1, source_target_pairs={{0,4},{4,0},{8,12},{12,8},{16,20},{20,16},{24,28},{28,24},{1,5},{5... | collective-permute-start | bytes 1769480 | tf_op jit(solution)/shard_map/ppermute | solution.py:595
  119.8 17.0 %collective-permute-start.17 = (bf16[384,896]{1,0:T(8,128)(2,1)}, bf16[384,896]{1,0:T(8,128)(2,1)S(1)}, u32[]{:S(2)}, u32[]{:S(2)}) collective-permute-start(bf16[384,896]{1,0:T(8,128)(2,1)} %get-tuple-element.64), channel_id=1, source_target_pairs={{0,4},{4,0},{8,12},{12,8},{16,20},{20,16},{24,28},{28,24},{1,5},{5... | collective-permute-start | bytes 2064392 | tf_op jit(solution)/shard_map/ppermute | solution.py:595
  121.3 48.0 %collective-permute-start.15 = (bf16[2,256,1536]{2,1,0:T(8,128)(2,1)}, bf16[2,256,1536]{2,1,0:T(8,128)(2,1)}, u32[]{:S(2)}, u32[]{:S(2)}) collective-permute-start(bf16[2,256,1536]{2,1,0:T(8,128)(2,1)} %get-tuple-element.60), channel_id=1, source_target_pairs={{0,1},{1,0},{2,3},{3,2},{4,5},{5,4},{6,7},{7,6},{8,9},{9,8},{10,11... | collective-permute-start | bytes 4718600 | tf_op jit(solution)/shard_map/ppermute | solution.py:598
  122.2 17.0 %collective-permute-start.24 = (bf16[192,768]{1,0:T(8,128)(2,1)}, bf16[192,768]{1,0:T(8,128)(2,1)}, u32[]{:S(2)}, u32[]{:S(2)}) collective-permute-start(bf16[192,768]{1,0:T(8,128)(2,1)} %slice.116), channel_id=1, source_target_pairs={{0,16},{4,20},{8,24},{12,28},{16,0},{20,4},{24,8},{28,12},{1,17},{... | collective-permute-start | bytes 884744 | tf_op jit(solution)/shard_map/ppermute | solution.py:595
  123.1 17.7 %collective-permute-start.27 = (bf16[192,768]{1,0:T(8,128)(2,1)}, bf16[192,768]{1,0:T(8,128)(2,1)}, u32[]{:S(2)}, u32[]{:S(2)}) collective-permute-start(bf16[192,768]{1,0:T(8,128)(2,1)} %slice.120), channel_id=1, source_target_pairs={{0,8},{4,12},{8,0},{12,4},{16,24},{20,28},{24,16},{28,20},{1,9},{5... | collective-permute-start | bytes 884744 | tf_op jit(solution)/shard_map/ppermute | solution.py:595
  137.2 14.5 %collective-permute-start.18 = (bf16[192,1088]{1,0:T(8,128)(2,1)S(1)}, bf16[192,1088]{1,0:T(8,128)(2,1)S(1)}, u32[]{:S(2)}, u32[]{:S(2)}) collective-permute-start(bf16[192,1088]{1,0:T(8,128)(2,1)S(1)} %concatenate.55), channel_id=1, source_target_pairs={{0,8},{4,12},{8,0},{12,4},{16,24},{20,28},{24,16},{28,20},{1,9},{5... | collective-permute-start | bytes 1253384 | tf_op jit(solution)/shard_map/ppermute | solution.py:595
  140.3 5.4 %collective-permute-start.25 = (bf16[96,768]{1,0:T(8,128)(2,1)S(1)}, bf16[96,768]{1,0:T(8,128)(2,1)S(1)}, u32[]{:S(2)}, u32[]{:S(2)}) collective-permute-start(bf16[96,768]{1,0:T(8,128)(2,1)S(1)} %slice.118), channel_id=1, source_target_pairs={{0,4},{4,0},{8,12},{12,8},{16,20},{20,16},{24,28},{28,24},{1,5},{5... | collective-permute-start | bytes 442376 | tf_op jit(solution)/shard_map/ppermute | solution.py:595
  142.5 11.4 %collective-permute-start.28 = (bf16[96,768]{1,0:T(8,128)(2,1)}, bf16[96,768]{1,0:T(8,128)(2,1)S(1)}, u32[]{:S(2)}, u32[]{:S(2)}) collective-permute-start(bf16[96,768]{1,0:T(8,128)(2,1)} %slice.122), channel_id=1, source_target_pairs={{0,16},{4,20},{8,24},{12,28},{16,0},{20,4},{24,8},{28,12},{1,17},{... | collective-permute-start | bytes 442376 | tf_op jit(solution)/shard_map/ppermute | solution.py:595
  152.9 14.8 %collective-permute-start.19 = (bf16[96,1472]{1,0:T(8,128)(2,1)}, bf16[96,1472]{1,0:T(8,128)(2,1)}, u32[]{:S(2)}, u32[]{:S(2)}) collective-permute-start(bf16[96,1472]{1,0:T(8,128)(2,1)} %concatenate.58), channel_id=1, source_target_pairs={{0,16},{4,20},{8,24},{12,28},{16,0},{20,4},{24,8},{28,12},{1,17},{... | collective-permute-start | bytes 847880 | tf_op jit(solution)/shard_map/ppermute | solution.py:595
  154.0 21.9 %collective-permute-start.29 = (bf16[96,1536]{1,0:T(8,128)(2,1)S(1)}, bf16[96,1536]{1,0:T(8,128)(2,1)}, u32[]{:S(2)}, u32[]{:S(2)}) collective-permute-start(bf16[96,1536]{1,0:T(8,128)(2,1)S(1)} %pad_maximum_fusion.4.refs_0_), channel_id=1, source_target_pairs={{0,2},{1,3},{2,0},{3,1},{4,6},{5,7},{6,4},{7,5},{8,10},{9,11},{10,... | collective-permute-start | bytes 884744 | tf_op jit(solution)/shard_map/ppermute | solution.py:601
  168.8 9.9 %collective-permute-start.20 = (bf16[96,1472]{1,0:T(8,128)(2,1)S(1)}, bf16[96,1472]{1,0:T(8,128)(2,1)S(1)}, u32[]{:S(2)}, u32[]{:S(2)}) collective-permute-start(bf16[96,1472]{1,0:T(8,128)(2,1)S(1)} %add_convert_fusion.5.refs_0_), channel_id=1, source_target_pairs={{0,2},{1,3},{2,0},{3,1},{4,6},{5,7},{6,4},{7,5},{8,10},{9,11},{10,... | collective-permute-start | bytes 847880 | tf_op jit(solution)/shard_map/ppermute | solution.py:601
  172.9 20.5 %collective-permute-start.16 = (bf16[256,1536]{1,0:T(8,128)(2,1)S(1)}, bf16[256,1536]{1,0:T(8,128)(2,1)S(1)}, u32[]{:S(2)}, u32[]{:S(2)}) collective-permute-start(bf16[256,1536]{1,0:T(8,128)(2,1)S(1)} %fusion.2), channel_id=1, source_target_pairs={{0,2},{1,3},{2,0},{3,1},{4,6},{5,7},{6,4},{7,5},{8,10},{9,11},{10,... | collective-permute-start | bytes 2359304 | tf_op jit(solution)/shard_map/ppermute | solution.py:601
  175.9 5.7 %collective-permute-start.30 = (bf16[96,1536]{1,0:T(8,128)(2,1)S(1)}, bf16[96,1536]{1,0:T(8,128)(2,1)S(1)}, u32[]{:S(2)}, u32[]{:S(2)}) collective-permute-start(bf16[96,1536]{1,0:T(8,128)(2,1)S(1)} %pad_maximum_fusion.4.refs_0_), channel_id=1, source_target_pairs={{0,1},{1,0},{2,3},{3,2},{4,5},{5,4},{6,7},{7,6},{8,9},{9,8},{10,11... | collective-permute-start | bytes 884744 | tf_op jit(solution)/shard_map/ppermute | solution.py:598
  175.9 6.4 %collective-permute-start.31 = (bf16[96,1536]{1,0:T(8,128)(2,1)}, bf16[96,1536]{1,0:T(8,128)(2,1)}, u32[]{:S(2)}, u32[]{:S(2)}) collective-permute-start(bf16[96,1536]{1,0:T(8,128)(2,1)} %collective-permute-done.29.refs_1_), channel_id=1, source_target_pairs={{0,1},{1,0},{2,3},{3,2},{4,5},{5,4},{6,7},{7,6},{8,9},{9,8},{10,11... | collective-permute-start | bytes 884744 | tf_op jit(solution)/shard_map/ppermute | solution.py:598
  176.4 9.0 %collective-permute-start.21 = (bf16[96,1472]{1,0:T(8,128)(2,1)S(1)}, bf16[96,1472]{1,0:T(8,128)(2,1)S(1)}, u32[]{:S(2)}, u32[]{:S(2)}) collective-permute-start(bf16[96,1472]{1,0:T(8,128)(2,1)S(1)} %add_convert_fusion.5.refs_0_), channel_id=1, source_target_pairs={{0,1},{1,0},{2,3},{3,2},{4,5},{5,4},{6,7},{7,6},{8,9},{9,8},{10,11... | collective-permute-start | bytes 847880 | tf_op jit(solution)/shard_map/ppermute | solution.py:598
  178.7 6.7 %collective-permute-start.22 = (bf16[96,1472]{1,0:T(8,128)(2,1)S(1)}, bf16[96,1472]{1,0:T(8,128)(2,1)S(1)}, u32[]{:S(2)}, u32[]{:S(2)}) collective-permute-start(bf16[96,1472]{1,0:T(8,128)(2,1)S(1)} %collective-permute-done.20.refs_1_), channel_id=1, source_target_pairs={{0,1},{1,0},{2,3},{3,2},{4,5},{5,4},{6,7},{7,6},{8,9},{9,8},{10,11... | collective-permute-start | bytes 847880 | tf_op jit(solution)/shard_map/ppermute | solution.py:598
  (31 other events, 359.0 us)

commit v3 on v2

--- a/solution.py
+++ b/solution.py
@@ -492,7 +492,8 @@
     return up.reshape(rows, FF), pairs_nat[:, :, :D].reshape(GROUP * rows, D)
 
 
-VEC_PARTS = (1, 1, 1, 1, 3, 1, GROUP)
+VEC_PARTS = (1, 1, 1, 1, 3, 1, GROUP, 1)
+VEC_LINES = (0, 1, 2, 3, 4, 7, 8, 7)
 
 
 def assemble_kernel(*refs):
@@ -510,15 +511,13 @@
     proj_out[...] = owner([ref[:, side:].astype(F32) for ref in columns], rep, top)
     vec = [ref[:, width:side].astype(F32) for ref in columns]
     vec = ((vec[0] + vec[1]) + (vec[2] + vec[3])).T[:16]
-    line = 0
-    for out in vec_outs:
-        for start in range(0, out.shape[1], rows):
-            out[:, start : start + rows] = vec[line : line + 1]
-            line += 1
+    for out, line in zip(vec_outs, VEC_LINES):
+        count = out.shape[0] // rows
+        out[...] = jnp.concatenate([vec[line + k : line + k + 1] for k in range(count)], axis=1).reshape(out.shape)
 
 
 def run_assemble(columns, place, rows):
-    shapes = [(rows, 3 * D), (rows, D)] + [(1, count * rows) for count in VEC_PARTS]
+    shapes = [(rows, 3 * D), (rows, D)] + [(count * rows,) for count in VEC_PARTS]
     return pl.pallas_call(
         assemble_kernel,
         in_specs=[pl.BlockSpec(memory_space=pltpu.VMEM)] * 4 + [smem()],
@@ -537,10 +536,7 @@
     qkv = columns_nat[:, :, :width].reshape(GROUP, rows, 3, QUART).transpose(1, 2, 0, 3)
     vec = columns[:, :, width:side]
     vec = ((vec[0] + vec[1]) + (vec[2] + vec[3])).T
-    outs, line = [], 0
-    for count in VEC_PARTS:
-        outs.append(vec[line : line + count].reshape(1, count * rows))
-        line += count
+    outs = [vec[line : line + count].reshape(-1) for line, count in zip(VEC_LINES, VEC_PARTS)]
     return (qkv.reshape(rows, 3 * D), columns_nat[place[1]][:, side:], *outs)
 
 
@@ -559,7 +555,9 @@
                 qkv_own[:, which * QUART : (which + 1) * QUART] = qkv[:, start : start + QUART]
 
     lines = [
-        ref[:, start : start + rows].astype(F32) for ref in vectors for start in range(0, ref.shape[1], rows)
+        ref[...].astype(F32).reshape(1, ref.shape[0])[:, start : start + rows]
+        for ref in vectors
+        for start in range(0, ref.shape[0], rows)
     ]
     index = lax.broadcasted_iota(jnp.int32, (VEC_LANES, rows), 0)
     table = jnp.zeros((VEC_LANES, rows), F32)
@@ -648,7 +646,7 @@
 
         rep_ref = rep.reshape(1)
         vectors_own = [
-            value.reshape(1, -1)
+            value
             for value in (
                 first_gain, first_shift, second_gain, second_shift, qkv_bias, proj_bias, up_bias, down_bias
             )
@@ -751,7 +749,6 @@
         where = jnp.stack([rep, top])
         up_out, down_out = (assemble_mlp_plain if rows % 32 else run_assemble_mlp)(pair_all, where, rows)
         qkv_out, proj_out, *vec = (assemble_plain if rows % 32 else run_assemble)(column_all, where, rows)
-        vec = [each.reshape(-1) for each in vec]
         return (
             block_out.reshape(micro, slot, D),
             input_grad.reshape(micro, slot, D),
@@ -766,7 +763,7 @@
             up_out,
             vec[6],
             down_out,
-            vec[5],
+            vec[7],
         )
 
     return body

time: 200 us -> 198 us (0.990)
  other arithmetic: 16.7 us -> 14.2 us
  waiting for transfers between devices: 72.6 us -> 74.9 us
    pallas_call x2 -> x0, other arithmetic: 2.54 us -> none  [run_assemble(): pl.pallas_call(assemble_kernel, in_specs=[pl.BlockSpec(memory_space=pltpu...]
    ppermute x4, waiting for transfers between devices: 3.66 us -> 6.04 us  [x_swap(): return lax.ppermute(value, 'rep', [(i, i ^ 2) for i in range(GROUP)])]
    unnamed x68 -> x61, local copies, waits for them, and re-layouts: 7.14 us -> 6.63 us
  transfers between devices with their start and end apart: 32 -> 32, of which waited for: 14 -> 14; matrix products, arithmetic and copies ran while one was open for 12% -> 10% of each run, Pallas kernels for 29% -> 30%
where the time goes in v3:
time: 198 us
  waiting for transfers between devices  74.9 us (38%)
  Pallas kernels  63.5 us (32%)
  starting transfers between devices  29 us (15%)
  local copies, waits for them, and re-layouts  15.1 us (8%)
  other arithmetic  14.2 us (7%)
    ppermute x21, waiting for transfers between devices, shard_swap(): return lax.ppermute(value, 'fsdp', [(i, i ^ mask) for i in range(shards)])  68.9 us
    pallas_call x1, Pallas kernels, run_attention(): pl.pallas_call(functools.partial(attention_kernel, rows), grid=(GROUP,),...  23.3 us
    ppermute x21, starting transfers between devices, shard_swap(): return lax.ppermute(value, 'fsdp', [(i, i ^ mask) for i in range(shards)])  22.6 us
    pallas_call x1, Pallas kernels, run_mlp_forward(): pl.pallas_call(functools.partial(mlp_forward_kernel, down_place), grid=(G...  13.9 us
    pallas_call x1, Pallas kernels, run_mlp_backward(): pl.pallas_call(mlp_backward_kernel, grid=(GROUP,), in_specs=[token_block(...  13 us
    unnamed x61, local copies, waits for them, and re-layouts  6.63 us
    ppermute x4, waiting for transfers between devices, x_swap(): return lax.ppermute(value, 'rep', [(i, i ^ 2) for i in range(GROUP)])  6.04 us
    ppermute x4, starting transfers between devices, x_swap(): return lax.ppermute(value, 'rep', [(i, i ^ 2) for i in range(GROUP)])  5.77 us
  transfers between devices with their start and end apart: 32, of which 14 were waited for; matrix products, arithmetic and copies ran while one was open for 10% of the time, Pallas kernels for 30%

profile of v3, /device:TPU:0, one launch (start us, length us, event | category | flops | bytes accessed | tf_op | source)
XLA Modules:
  0.0 197.7 jit_solution(4207971077014776319)
XLA Ops:
  4.4 3.0 %collective-permute-start = (bf16[528,768]{1,0:T(8,128)(2,1)S(1)}, bf16[528,768]{1,0:T(8,128)(2,1)}, u32[]{:S(2)}, u32[]{:S(2)}) collective-permute-start(bf16[528,768]{1,0:T(8,128)(2,1)S(1)} %fusion.1.near.pack), channel_id=1, source_target_pairs={{0,2},{1,3},{2,0},{3,1},{4,6},{5,7},{6,4},{7,5},{8,10},{9,11},{10,... | collective-permute-start | bytes 2433032 | tf_op jit(solution)/shard_map/ppermute | solution.py:599
  7.4 2.8 %quarter.1 = (bf16[96,896]{1,0:T(8,128)(2,1)}, bf16[96,576]{1,0:T(8,128)(2,1)}) custom-call(bf16[96]{0:T(256)(128)(2,1)} %refs_0_.1, bf16[96]{0:T(256)(128)(2,1)} %refs_1_.1, bf16[96]{0:T(256)(128)(2,1)} %refs_2_.1, bf16[96]{0:T(256)(128)(2,1)} %refs_3_.1, bf16[288]{0:T(512)(128)(2,1)} %refs_4_.1, bf16[96]{0:T(256)(128)(2,1)} %refs_5_.1, ...), custom_call_target="tpu_custom_call" | custom-call | tf_op jit(solution)/shard_map/quarter/pallas_call | solution.py:571
  10.1 2.6 %collective-permute-start.3 = (bf16[96,896]{1,0:T(8,128)(2,1)}, bf16[96,896]{1,0:T(8,128)(2,1)S(1)}, u32[]{:S(2)}, u32[]{:S(2)}) collective-permute-start(bf16[96,896]{1,0:T(8,128)(2,1)} %get-tuple-element.48), channel_id=1, source_target_pairs={{0,16},{4,20},{8,24},{12,28},{16,0},{20,4},{24,8},{28,12},{1,17},{... | collective-permute-start | bytes 516104 | tf_op jit(solution)/shard_map/ppermute | solution.py:593
  13.2 2.6 %collective-permute-start.6 = (bf16[96,576]{1,0:T(8,128)(2,1)}, bf16[96,576]{1,0:T(8,128)(2,1)S(1)}, u32[]{:S(2)}, u32[]{:S(2)}) collective-permute-start(bf16[96,576]{1,0:T(8,128)(2,1)} %get-tuple-element.50), channel_id=1, source_target_pairs={{0,16},{4,20},{8,24},{12,28},{16,0},{20,4},{24,8},{28,12},{1,17},{... | collective-permute-start | bytes 331784 | tf_op jit(solution)/shard_map/ppermute | solution.py:593
  17.3 10.6 %collective-permute-done.3 = bf16[96,896]{1,0:T(8,128)(2,1)S(1)} collective-permute-done((bf16[96,896]{1,0:T(8,128)(2,1)}, bf16[96,896]{1,0:T(8,128)(2,1)S(1)}, u32[]{:S(2)}, u32[]{:S(2)}) %collective-permute-start.3) | collective-permute-done | bytes 172064 | tf_op jit(solution)/shard_map/ppermute | solution.py:593
  29.4 1.8 collective-permute-done.12
  31.5 9.3 %collective-permute-done.4 = bf16[192,896]{1,0:T(8,128)(2,1)S(1)} collective-permute-done((bf16[192,896]{1,0:T(8,128)(2,1)S(1)}, bf16[192,896]{1,0:T(8,128)(2,1)S(1)}, u32[]{:S(2)}, u32[]{:S(2)}) %collective-permute-start.4) | collective-permute-done | bytes 344096 | tf_op jit(solution)/shard_map/ppermute | solution.py:593
  42.4 1.6 collective-permute-start.5
  44.1 5.3 %collective-permute-done.13 = bf16[192,768]{1,0:T(8,128)(2,1)S(1)} collective-permute-done((bf16[192,768]{1,0:T(8,128)(2,1)S(1)}, bf16[192,768]{1,0:T(8,128)(2,1)S(1)}, u32[]{:S(2)}, u32[]{:S(2)}) %collective-permute-start.13) | collective-permute-done | bytes 294944 | tf_op jit(solution)/shard_map/ppermute | solution.py:593
  53.2 3.9 %collective-permute-done.7 = bf16[192,576]{1,0:T(8,128)(2,1)S(1)} collective-permute-done((bf16[192,576]{1,0:T(8,128)(2,1)S(1)}, bf16[192,576]{1,0:T(8,128)(2,1)S(1)}, u32[]{:S(2)}, u32[]{:S(2)}) %collective-permute-start.7) | collective-permute-done | bytes 221216 | tf_op jit(solution)/shard_map/ppermute | solution.py:593
  57.6 1.6 collective-permute-start.8
  59.1 1.7 collective-permute-done.5.up_hi
  61.7 13.9 %mlp_forward.1 = (bf16[384,768]{1,0:T(8,128)(2,1)}, bf16[384,768]{1,0:T(8,128)(2,1)}, f32[4,256,768]{2,1,0:T(8,128)}, bf16[4,256,768]{2,1,0:T(8,128)(2,1)}, f32[...) custom-call(bf16[528,768]{1,0:T(8,128)(2,1)} %copy-done.2, ...), custom_call_target="tpu_custom_call" | custom-call | tf_op jit(solution)/shard_map/mlp_forward/pallas_call | solution.py:310
  75.6 2.6 %collective-permute-start.23 = (bf16[384,768]{1,0:T(8,128)(2,1)}, bf16[384,768]{1,0:T(8,128)(2,1)S(1)}, u32[]{:S(2)}, u32[]{:S(2)}) collective-permute-start(bf16[384,768]{1,0:T(8,128)(2,1)} %get-tuple-element.75), channel_id=1, source_target_pairs={{0,8},{4,12},{8,0},{12,4},{16,24},{20,28},{24,16},{28,20},{1,9},{5... | collective-permute-start | bytes 1769480 | tf_op jit(solution)/shard_map/ppermute | solution.py:593
  78.2 1.6 collective-permute-start.11
  79.8 13.0 %mlp_backward.1 = (bf16[384,768]{1,0:T(8,128)(2,1)}, bf16[384,768]{1,0:T(8,128)(2,1)}, f32[4,256,768]{2,1,0:T(8,128)}, f32[4,256,768]{2,1,0:T(8,128)}, f32[8,768]{1,0:T(8,128)}) custom-call(bf16[4,272,768]{2,1,0:T(8,128)(2,1)} %get-tuple-element.49.cotangents, bf16[384,768]{1,0:T(8,128)(2,1)} %copy-done.3, bf16[384,768]{1,0:T(8,128)(2,1)} %collective-permute-done.14.down_hi, ...), custom_call_target="tpu_custom_call" | custom-call | tf_op jit(solution)/shard_map/mlp_backward/pallas_call | solution.py:339
  95.2 23.3 %attention.1 = (bf16[384,896]{1,0:T(8,128)(2,1)}, bf16[384,896]{1,0:T(8,128)(2,1)}, bf16[2,256,1536]{2,1,0:T(8,128)(2,1)}, bf16[2,256,1536]{2,1,0:T(8,128)(2,1)}) custom-call(bf16[4,272,768]{2,1,0:T(8,128)(2,1)} %get-tuple-element.49.cotangents, bf16[384,576]{1,0:T(8,128)(2,1)} %copy-done.9, bf16[384,576]{1,0:T(8,128)(2,1)} %collective-permute-done.8.qkv_hi, ...), custom_call_target="tpu_custom_call" | custom-call | tf_op jit(solution)/shard_map/attention/pallas_call | solution.py:381
  118.6 1.6 collective-permute-start.17
  122.0 1.8 collective-permute-start.27
  123.8 11.8 %collective-permute-done.17 = bf16[384,896]{1,0:T(8,128)(2,1)S(1)} collective-permute-done((bf16[384,896]{1,0:T(8,128)(2,1)}, bf16[384,896]{1,0:T(8,128)(2,1)S(1)}, u32[]{:S(2)}, u32[]{:S(2)}) %collective-permute-start.17) | collective-permute-done | bytes 688160 | tf_op jit(solution)/shard_map/ppermute | solution.py:593
  136.1 2.0 collective-permute-done.24
  141.5 3.1 %collective-permute-done.25 = bf16[96,768]{1,0:T(8,128)(2,1)S(1)} collective-permute-done((bf16[96,768]{1,0:T(8,128)(2,1)S(1)}, bf16[96,768]{1,0:T(8,128)(2,1)S(1)}, u32[]{:S(2)}, u32[]{:S(2)}) %collective-permute-start.25) | collective-permute-done | bytes 147488 | tf_op jit(solution)/shard_map/ppermute | solution.py:593
  144.6 6.0 %collective-permute-done.18 = bf16[192,1088]{1,0:T(8,128)(2,1)S(1)} collective-permute-done((bf16[192,1088]{1,0:T(8,128)(2,1)S(1)}, bf16[192,1088]{1,0:T(8,128)(2,1)S(1)}, u32[]{:S(2)}, u32[]{:S(2)}) %collective-permute-start.18) | collective-permute-done | bytes 417824 | tf_op jit(solution)/shard_map/ppermute | solution.py:593
  153.5 13.0 %collective-permute-done.19 = bf16[96,1472]{1,0:T(8,128)(2,1)} collective-permute-done((bf16[96,1472]{1,0:T(8,128)(2,1)}, bf16[96,1472]{1,0:T(8,128)(2,1)}, u32[]{:S(2)}, u32[]{:S(2)}) %collective-permute-start.19) | collective-permute-done | bytes 282656 | tf_op jit(solution)/shard_map/ppermute | solution.py:593
  168.2 1.8 convert_add_fusion
  170.1 1.6 copy-done.1
  175.3 2.2 %collective-permute-done.20.refs_1_ = bf16[96,1472]{1,0:T(8,128)(2,1)S(1)} collective-permute-done((bf16[96,1472]{1,0:T(8,128)(2,1)S(1)}, bf16[96,1472]{1,0:T(8,128)(2,1)S(1)}, u32[]{:S(2)}, u32[]{:S(2)}) %collective-permute-start.20) | collective-permute-done | bytes 282656 | tf_op jit(solution)/shard_map/ppermute | solution.py:599
  177.5 2.8 %slice_bitcast_fusion.near = f32[256,1536]{1,0:T(8,128)} fusion(f32[2,256,1536]{2,1,0:T(8,128)} %copy-done.1), kind=kLoop, calls=%fused_computation.4 | loop fusion | bytes 3145728 | tf_op jit(solution)/shard_map/squeeze | solution.py:743
  181.1 3.1 %assemble_mlp.1 = (f32[96,3072]{1,0:T(8,128)}, f32[384,768]{1,0:T(8,128)}) custom-call(bf16[96,1536]{1,0:T(8,128)(2,1)} %copy-done.6, bf16[96,1536]{1,0:T(8,128)(2,1)} %collective-permute-done.29.refs_1_, bf16[96,1536]{1,0:T(8,128)(2,1)} %copy-done.21, bf16[96,1536]{1,0:T(8,128)(2,1)} %collective-permute-done.31.refs_3_, s32[2]{0:T(128)} %pad_add_fusion.refs_4_), custom_call_target="tpu_custom_call" | custom-call | tf_op jit(solution)/shard_map/assemble_mlp/pallas_call | solution.py:479
  185.6 2.7 %assemble.1 = (f32[96,2304]{1,0:T(8,128)}, f32[96,768]{1,0:T(8,128)}, f32[96]{0:T(128)}, f32[96]{0:T(128)}, f32[96]{0:T(128)}, /*index=5*/f32[96]{0:T(128)}, f32...) custom-call(bf16[96,1472]{1,0:T(8,128)(2,1)} %copy-done.5, bf16[96,1472]{1,0:T(8,128)(2,1)} %copy-done.18, ...), custom_call_target="tpu_custom_call" | custom-call | tf_op jit(solution)/shard_map/assemble/pallas_call | solution.py:521
  188.4 3.8 %collective-permute-done.16.received = bf16[256,1536]{1,0:T(8,128)(2,1)S(1)} collective-permute-done((bf16[256,1536]{1,0:T(8,128)(2,1)S(1)}, bf16[256,1536]{1,0:T(8,128)(2,1)S(1)}, u32[]{:S(2)}, u32[]{:S(2)}) %collective-permute-start.16) | collective-permute-done | bytes 786464 | tf_op jit(solution)/shard_map/ppermute | solution.py:599
  193.1 4.7 %finish.1 = (bf16[256,768]{1,0:T(8,128)(2,1)}, bf16[256,768]{1,0:T(8,128)(2,1)}) custom-call(bf16[528,768]{1,0:T(8,128)(2,1)} %copy-done.2, f32[256,1536]{1,0:T(8,128)} %slice_bitcast_fusion.near, bf16[256,1536]{1,0:T(8,128)(2,1)} %copy-done.8, bf16[768,768]{1,0:T(8,128)(2,1)} %get-tuple-element.51.to_rel, f32[16,768]{1,0:T(8,128)} %get-tuple-element.52.vectors, ...), custom_call_target="tpu_custom_call" | custom-call | tf_op jit(solution)/shard_map/finish/pallas_call | solution.py:455
  (146 shorter events, 33.6 us)
Async XLA Ops:
  4.4 38.0 %collective-permute-start = (bf16[528,768]{1,0:T(8,128)(2,1)S(1)}, bf16[528,768]{1,0:T(8,128)(2,1)}, u32[]{:S(2)}, u32[]{:S(2)}) collective-permute-start(bf16[528,768]{1,0:T(8,128)(2,1)S(1)} %fusion.1.near.pack), channel_id=1, source_target_pairs={{0,2},{1,3},{2,0},{3,1},{4,6},{5,7},{6,4},{7,5},{8,10},{9,11},{10,... | collective-permute-start | bytes 2433032 | tf_op jit(solution)/shard_map/ppermute | solution.py:599
  7.4 50.2 %collective-permute-start.1 = (bf16[528,768]{1,0:T(8,128)(2,1)S(1)}, bf16[528,768]{1,0:T(8,128)(2,1)}, u32[]{:S(2)}, u32[]{:S(2)}) collective-permute-start(bf16[528,768]{1,0:T(8,128)(2,1)S(1)} %fusion.1.near.pack), channel_id=1, source_target_pairs={{0,1},{1,0},{2,3},{3,2},{4,5},{5,4},{6,7},{7,6},{8,9},{9,8},{10,11... | collective-permute-start | bytes 2433032 | tf_op jit(solution)/shard_map/ppermute | solution.py:596
  10.1 17.8 %collective-permute-start.3 = (bf16[96,896]{1,0:T(8,128)(2,1)}, bf16[96,896]{1,0:T(8,128)(2,1)S(1)}, u32[]{:S(2)}, u32[]{:S(2)}) collective-permute-start(bf16[96,896]{1,0:T(8,128)(2,1)} %get-tuple-element.48), channel_id=1, source_target_pairs={{0,16},{4,20},{8,24},{12,28},{16,0},{20,4},{24,8},{28,12},{1,17},{... | collective-permute-start | bytes 516104 | tf_op jit(solution)/shard_map/ppermute | solution.py:593
  12.8 18.4 %collective-permute-start.12 = (bf16[96,768]{1,0:T(8,128)(2,1)S(1)}, bf16[96,768]{1,0:T(8,128)(2,1)S(1)}, u32[]{:S(2)}, u32[]{:S(2)}) collective-permute-start(bf16[96,768]{1,0:T(8,128)(2,1)S(1)} %dynamic-slice_bitcast_fusion), channel_id=1, source_target_pairs={{0,16},{4,20},{8,24},{12,28},{16,0},{20,4},{24,8},{28,12},{1,17},{... | collective-permute-start | bytes 442376 | tf_op jit(solution)/shard_map/ppermute | solution.py:593
  13.2 29.3 %collective-permute-start.6 = (bf16[96,576]{1,0:T(8,128)(2,1)}, bf16[96,576]{1,0:T(8,128)(2,1)S(1)}, u32[]{:S(2)}, u32[]{:S(2)}) collective-permute-start(bf16[96,576]{1,0:T(8,128)(2,1)} %get-tuple-element.50), channel_id=1, source_target_pairs={{0,16},{4,20},{8,24},{12,28},{16,0},{20,4},{24,8},{28,12},{1,17},{... | collective-permute-start | bytes 331784 | tf_op jit(solution)/shard_map/ppermute | solution.py:593
  28.9 11.9 %collective-permute-start.4 = (bf16[192,896]{1,0:T(8,128)(2,1)S(1)}, bf16[192,896]{1,0:T(8,128)(2,1)S(1)}, u32[]{:S(2)}, u32[]{:S(2)}) collective-permute-start(bf16[192,896]{1,0:T(8,128)(2,1)S(1)} %pad_maximum_fusion.1), channel_id=1, source_target_pairs={{0,8},{4,12},{8,0},{12,4},{16,24},{20,28},{24,16},{28,20},{1,9},{5... | collective-permute-start | bytes 1032200 | tf_op jit(solution)/shard_map/ppermute | solution.py:593
  31.2 18.1 %collective-permute-start.13 = (bf16[192,768]{1,0:T(8,128)(2,1)S(1)}, bf16[192,768]{1,0:T(8,128)(2,1)S(1)}, u32[]{:S(2)}, u32[]{:S(2)}) collective-permute-start(bf16[192,768]{1,0:T(8,128)(2,1)S(1)} %pad_maximum_fusion.3), channel_id=1, source_target_pairs={{0,8},{4,12},{8,0},{12,4},{16,24},{20,28},{24,16},{28,20},{1,9},{5... | collective-permute-start | bytes 884744 | tf_op jit(solution)/shard_map/ppermute | solution.py:593
  40.8 10.0 %collective-permute-start.9 = (bf16[96,768]{1,0:T(8,128)(2,1)}, bf16[96,768]{1,0:T(8,128)(2,1)S(1)}, u32[]{:S(2)}, u32[]{:S(2)}) collective-permute-start(bf16[96,768]{1,0:T(8,128)(2,1)} %param.33), channel_id=1, source_target_pairs={{0,16},{4,20},{8,24},{12,28},{16,0},{20,4},{24,8},{28,12},{1,17},{... | collective-permute-start | bytes 442376 | tf_op jit(solution)/shard_map/ppermute | solution.py:593
  42.4 18.5 %collective-permute-start.2 = (bf16[528,768]{1,0:T(8,128)(2,1)}, bf16[528,768]{1,0:T(8,128)(2,1)}, u32[]{:S(2)}, u32[]{:S(2)}) collective-permute-start(bf16[528,768]{1,0:T(8,128)(2,1)} %collective-permute-done.across), channel_id=1, source_target_pairs={{0,1},{1,0},{2,3},{3,2},{4,5},{5,4},{6,7},{7,6},{8,9},{9,8},{10,11... | collective-permute-start | bytes 2433032 | tf_op jit(solution)/shard_map/ppermute | solution.py:596
  42.4 18.4 %collective-permute-start.5 = (bf16[384,896]{1,0:T(8,128)(2,1)S(1)}, bf16[384,896]{1,0:T(8,128)(2,1)S(1)}, u32[]{:S(2)}, u32[]{:S(2)}) collective-permute-start(bf16[384,896]{1,0:T(8,128)(2,1)S(1)} %constant_dynamic-update-slice_fusion.up_lo), channel_id=1, source_target_pairs={{0,4},{4,0},{8,12},{12,8},{16,20},{20,16},{24,28},{28,24},{1,5},{5... | collective-permute-start | bytes 2064392 | tf_op jit(solution)/shard_map/ppermute | solution.py:593
  49.3 7.9 %collective-permute-start.7 = (bf16[192,576]{1,0:T(8,128)(2,1)S(1)}, bf16[192,576]{1,0:T(8,128)(2,1)S(1)}, u32[]{:S(2)}, u32[]{:S(2)}) collective-permute-start(bf16[192,576]{1,0:T(8,128)(2,1)S(1)} %pad_maximum_fusion.5), channel_id=1, source_target_pairs={{0,8},{4,12},{8,0},{12,4},{16,24},{20,28},{24,16},{28,20},{1,9},{5... | collective-permute-start | bytes 663560 | tf_op jit(solution)/shard_map/ppermute | solution.py:593
  50.8 29.0 %collective-permute-start.14 = (bf16[384,768]{1,0:T(8,128)(2,1)S(1)}, bf16[384,768]{1,0:T(8,128)(2,1)}, u32[]{:S(2)}, u32[]{:S(2)}) collective-permute-start(bf16[384,768]{1,0:T(8,128)(2,1)S(1)} %pad_maximum_fusion.down_lo), channel_id=1, source_target_pairs={{0,4},{4,0},{8,12},{12,8},{16,20},{20,16},{24,28},{28,24},{1,5},{5... | collective-permute-start | bytes 1769480 | tf_op jit(solution)/shard_map/ppermute | solution.py:593
  57.2 21.0 %collective-permute-start.10 = (bf16[96,768]{1,0:T(8,128)(2,1)S(1)}, bf16[96,768]{1,0:T(8,128)(2,1)}, u32[]{:S(2)}, u32[]{:S(2)}) collective-permute-start(bf16[96,768]{1,0:T(8,128)(2,1)S(1)} %broadcast_select_fusion), channel_id=1, source_target_pairs={{0,8},{4,12},{8,0},{12,4},{16,24},{20,28},{24,16},{28,20},{1,9},{5... | collective-permute-start | bytes 442376 | tf_op jit(solution)/shard_map/ppermute | solution.py:593
  57.6 37.7 %collective-permute-start.8 = (bf16[384,576]{1,0:T(8,128)(2,1)S(1)}, bf16[384,576]{1,0:T(8,128)(2,1)}, u32[]{:S(2)}, u32[]{:S(2)}) collective-permute-start(bf16[384,576]{1,0:T(8,128)(2,1)S(1)} %constant_dynamic-update-slice_fusion.3.qkv_lo), channel_id=1, source_target_pairs={{0,4},{4,0},{8,12},{12,8},{16,20},{20,16},{24,28},{28,24},{1,5},{5... | collective-permute-start | bytes 1327112 | tf_op jit(solution)/shard_map/ppermute | solution.py:593
  75.6 44.5 %collective-permute-start.23 = (bf16[384,768]{1,0:T(8,128)(2,1)}, bf16[384,768]{1,0:T(8,128)(2,1)S(1)}, u32[]{:S(2)}, u32[]{:S(2)}) collective-permute-start(bf16[384,768]{1,0:T(8,128)(2,1)} %get-tuple-element.75), channel_id=1, source_target_pairs={{0,8},{4,12},{8,0},{12,4},{16,24},{20,28},{24,16},{28,20},{1,9},{5... | collective-permute-start | bytes 1769480 | tf_op jit(solution)/shard_map/ppermute | solution.py:593
  78.2 16.3 %collective-permute-start.11 = (bf16[96,768]{1,0:T(8,128)(2,1)S(1)}, bf16[96,768]{1,0:T(8,128)(2,1)S(1)}, u32[]{:S(2)}, u32[]{:S(2)}) collective-permute-start(bf16[96,768]{1,0:T(8,128)(2,1)S(1)} %broadcast_select_fusion.1), channel_id=1, source_target_pairs={{0,4},{4,0},{8,12},{12,8},{16,20},{20,16},{24,28},{28,24},{1,5},{5... | collective-permute-start | bytes 442376 | tf_op jit(solution)/shard_map/ppermute | solution.py:593
  92.8 28.3 %collective-permute-start.26 = (bf16[384,768]{1,0:T(8,128)(2,1)}, bf16[384,768]{1,0:T(8,128)(2,1)S(1)}, u32[]{:S(2)}, u32[]{:S(2)}) collective-permute-start(bf16[384,768]{1,0:T(8,128)(2,1)} %get-tuple-element.77), channel_id=1, source_target_pairs={{0,4},{4,0},{8,12},{12,8},{16,20},{20,16},{24,28},{28,24},{1,5},{5... | collective-permute-start | bytes 1769480 | tf_op jit(solution)/shard_map/ppermute | solution.py:593
  118.6 17.0 %collective-permute-start.17 = (bf16[384,896]{1,0:T(8,128)(2,1)}, bf16[384,896]{1,0:T(8,128)(2,1)S(1)}, u32[]{:S(2)}, u32[]{:S(2)}) collective-permute-start(bf16[384,896]{1,0:T(8,128)(2,1)} %get-tuple-element.65), channel_id=1, source_target_pairs={{0,4},{4,0},{8,12},{12,8},{16,20},{20,16},{24,28},{28,24},{1,5},{5... | collective-permute-start | bytes 2064392 | tf_op jit(solution)/shard_map/ppermute | solution.py:593
  120.2 48.1 %collective-permute-start.15 = (bf16[2,256,1536]{2,1,0:T(8,128)(2,1)}, bf16[2,256,1536]{2,1,0:T(8,128)(2,1)}, u32[]{:S(2)}, u32[]{:S(2)}) collective-permute-start(bf16[2,256,1536]{2,1,0:T(8,128)(2,1)} %get-tuple-element.61), channel_id=1, source_target_pairs={{0,1},{1,0},{2,3},{3,2},{4,5},{5,4},{6,7},{7,6},{8,9},{9,8},{10,11... | collective-permute-start | bytes 4718600 | tf_op jit(solution)/shard_map/ppermute | solution.py:596
  121.1 17.0 %collective-permute-start.24 = (bf16[192,768]{1,0:T(8,128)(2,1)}, bf16[192,768]{1,0:T(8,128)(2,1)}, u32[]{:S(2)}, u32[]{:S(2)}) collective-permute-start(bf16[192,768]{1,0:T(8,128)(2,1)} %slice.116), channel_id=1, source_target_pairs={{0,16},{4,20},{8,24},{12,28},{16,0},{20,4},{24,8},{28,12},{1,17},{... | collective-permute-start | bytes 884744 | tf_op jit(solution)/shard_map/ppermute | solution.py:593
  122.0 17.7 %collective-permute-start.27 = (bf16[192,768]{1,0:T(8,128)(2,1)}, bf16[192,768]{1,0:T(8,128)(2,1)}, u32[]{:S(2)}, u32[]{:S(2)}) collective-permute-start(bf16[192,768]{1,0:T(8,128)(2,1)} %slice.120), channel_id=1, source_target_pairs={{0,8},{4,12},{8,0},{12,4},{16,24},{20,28},{24,16},{28,20},{1,9},{5... | collective-permute-start | bytes 884744 | tf_op jit(solution)/shard_map/ppermute | solution.py:593
  136.0 14.5 %collective-permute-start.18 = (bf16[192,1088]{1,0:T(8,128)(2,1)S(1)}, bf16[192,1088]{1,0:T(8,128)(2,1)S(1)}, u32[]{:S(2)}, u32[]{:S(2)}) collective-permute-start(bf16[192,1088]{1,0:T(8,128)(2,1)S(1)} %concatenate.55), channel_id=1, source_target_pairs={{0,8},{4,12},{8,0},{12,4},{16,24},{20,28},{24,16},{28,20},{1,9},{5... | collective-permute-start | bytes 1253384 | tf_op jit(solution)/shard_map/ppermute | solution.py:593
  139.1 5.4 %collective-permute-start.25 = (bf16[96,768]{1,0:T(8,128)(2,1)S(1)}, bf16[96,768]{1,0:T(8,128)(2,1)S(1)}, u32[]{:S(2)}, u32[]{:S(2)}) collective-permute-start(bf16[96,768]{1,0:T(8,128)(2,1)S(1)} %slice.118), channel_id=1, source_target_pairs={{0,4},{4,0},{8,12},{12,8},{16,20},{20,16},{24,28},{28,24},{1,5},{5... | collective-permute-start | bytes 442376 | tf_op jit(solution)/shard_map/ppermute | solution.py:593
  141.4 11.4 %collective-permute-start.28 = (bf16[96,768]{1,0:T(8,128)(2,1)}, bf16[96,768]{1,0:T(8,128)(2,1)S(1)}, u32[]{:S(2)}, u32[]{:S(2)}) collective-permute-start(bf16[96,768]{1,0:T(8,128)(2,1)} %slice.122), channel_id=1, source_target_pairs={{0,16},{4,20},{8,24},{12,28},{16,0},{20,4},{24,8},{28,12},{1,17},{... | collective-permute-start | bytes 442376 | tf_op jit(solution)/shard_map/ppermute | solution.py:593
  151.7 14.8 %collective-permute-start.19 = (bf16[96,1472]{1,0:T(8,128)(2,1)}, bf16[96,1472]{1,0:T(8,128)(2,1)}, u32[]{:S(2)}, u32[]{:S(2)}) collective-permute-start(bf16[96,1472]{1,0:T(8,128)(2,1)} %concatenate.58), channel_id=1, source_target_pairs={{0,16},{4,20},{8,24},{12,28},{16,0},{20,4},{24,8},{28,12},{1,17},{... | collective-permute-start | bytes 847880 | tf_op jit(solution)/shard_map/ppermute | solution.py:593
  152.8 21.9 %collective-permute-start.29 = (bf16[96,1536]{1,0:T(8,128)(2,1)S(1)}, bf16[96,1536]{1,0:T(8,128)(2,1)}, u32[]{:S(2)}, u32[]{:S(2)}) collective-permute-start(bf16[96,1536]{1,0:T(8,128)(2,1)S(1)} %pad_maximum_fusion.4.refs_0_), channel_id=1, source_target_pairs={{0,2},{1,3},{2,0},{3,1},{4,6},{5,7},{6,4},{7,5},{8,10},{9,11},{10,... | collective-permute-start | bytes 884744 | tf_op jit(solution)/shard_map/ppermute | solution.py:599
  167.6 9.9 %collective-permute-start.20 = (bf16[96,1472]{1,0:T(8,128)(2,1)S(1)}, bf16[96,1472]{1,0:T(8,128)(2,1)S(1)}, u32[]{:S(2)}, u32[]{:S(2)}) collective-permute-start(bf16[96,1472]{1,0:T(8,128)(2,1)S(1)} %add_convert_fusion.5.refs_0_), channel_id=1, source_target_pairs={{0,2},{1,3},{2,0},{3,1},{4,6},{5,7},{6,4},{7,5},{8,10},{9,11},{10,... | collective-permute-start | bytes 847880 | tf_op jit(solution)/shard_map/ppermute | solution.py:599
  171.8 20.4 %collective-permute-start.16 = (bf16[256,1536]{1,0:T(8,128)(2,1)S(1)}, bf16[256,1536]{1,0:T(8,128)(2,1)S(1)}, u32[]{:S(2)}, u32[]{:S(2)}) collective-permute-start(bf16[256,1536]{1,0:T(8,128)(2,1)S(1)} %fusion.2), channel_id=1, source_target_pairs={{0,2},{1,3},{2,0},{3,1},{4,6},{5,7},{6,4},{7,5},{8,10},{9,11},{10,... | collective-permute-start | bytes 2359304 | tf_op jit(solution)/shard_map/ppermute | solution.py:599
  174.7 5.6 %collective-permute-start.30 = (bf16[96,1536]{1,0:T(8,128)(2,1)S(1)}, bf16[96,1536]{1,0:T(8,128)(2,1)S(1)}, u32[]{:S(2)}, u32[]{:S(2)}) collective-permute-start(bf16[96,1536]{1,0:T(8,128)(2,1)S(1)} %pad_maximum_fusion.4.refs_0_), channel_id=1, source_target_pairs={{0,1},{1,0},{2,3},{3,2},{4,5},{5,4},{6,7},{7,6},{8,9},{9,8},{10,11... | collective-permute-start | bytes 884744 | tf_op jit(solution)/shard_map/ppermute | solution.py:596
  174.7 6.3 %collective-permute-start.31 = (bf16[96,1536]{1,0:T(8,128)(2,1)}, bf16[96,1536]{1,0:T(8,128)(2,1)}, u32[]{:S(2)}, u32[]{:S(2)}) collective-permute-start(bf16[96,1536]{1,0:T(8,128)(2,1)} %collective-permute-done.29.refs_1_), channel_id=1, source_target_pairs={{0,1},{1,0},{2,3},{3,2},{4,5},{5,4},{6,7},{7,6},{8,9},{9,8},{10,11... | collective-permute-start | bytes 884744 | tf_op jit(solution)/shard_map/ppermute | solution.py:596
  175.2 8.9 %collective-permute-start.21 = (bf16[96,1472]{1,0:T(8,128)(2,1)S(1)}, bf16[96,1472]{1,0:T(8,128)(2,1)S(1)}, u32[]{:S(2)}, u32[]{:S(2)}) collective-permute-start(bf16[96,1472]{1,0:T(8,128)(2,1)S(1)} %add_convert_fusion.5.refs_0_), channel_id=1, source_target_pairs={{0,1},{1,0},{2,3},{3,2},{4,5},{5,4},{6,7},{7,6},{8,9},{9,8},{10,11... | collective-permute-start | bytes 847880 | tf_op jit(solution)/shard_map/ppermute | solution.py:596
  177.5 6.6 %collective-permute-start.22 = (bf16[96,1472]{1,0:T(8,128)(2,1)S(1)}, bf16[96,1472]{1,0:T(8,128)(2,1)S(1)}, u32[]{:S(2)}, u32[]{:S(2)}) collective-permute-start(bf16[96,1472]{1,0:T(8,128)(2,1)S(1)} %collective-permute-done.20.refs_1_), channel_id=1, source_target_pairs={{0,1},{1,0},{2,3},{3,2},{4,5},{5,4},{6,7},{7,6},{8,9},{9,8},{10,11... | collective-permute-start | bytes 847880 | tf_op jit(solution)/shard_map/ppermute | solution.py:596
  (28 other events, 331.2 us)
